TPU v7x, 128 devices: a whole 4x4x4 slice. The times are simulated.
128 devices in a mesh: seq: 32 (over z, x, core), rep: 4 (over y).
Axes of the slice: x: 4, y: 4, z: 4, core: 2. Of those that a mesh axis runs over, the one named last changes fastest.
Arguments:
- tokens: bfloat16 [16384, 2304], P(('rep', 'seq')), parts along dimension 0, may hold values from -6 to 6
- qkv_weight: bfloat16 [2304, 6144], P(None, 'seq'), may hold values from -0.125 to 0.125
- conv_weight: float32 [4, 6144], replicated, may hold values from -3 to 3
- decay_down: bfloat16 [2304, 128], replicated, may hold values from -0.125 to 0.125
- decay_up: bfloat16 [128, 2048], replicated, may hold values from -0.5 to 0.5
- decay_rate: float32 [2048], replicated, may hold values from 0.00024414062 to 0.1
- beta_weight: bfloat16 [2304, 16], replicated, may hold values from -0.125 to 0.125
- beta_scale: float32 [16], replicated, may hold values from 0.03125 to 1
- gate_down: bfloat16 [2304, 128], replicated, may hold values from -0.125 to 0.125
- gate_up: bfloat16 [128, 2048], replicated, may hold values from -0.5 to 0.5
- norm_gain: float32 [128], replicated, may hold values from 0.1 to 1.9
Outputs:
- attended: bfloat16 [16384, 2048], P(('rep', 'seq')), parts along dimension 0
There are 4 independent parts, one for each index of `rep`. A program takes and returns all parts, laid end to end along the dimension named above; an argument that names none is the same for every part. Nothing has to cross between parts.
All inputs are finite; a program needn't handle non-finite values.
Results may differ from a plain program's by a relative error of at most 0.0054.
Values may be sent and summed in bfloat16 or wider, within the bound.
No kernel may reach another device: no remote copies, remote signals or barrier semaphores. Data moves between devices by JAX's collectives and lax.ppermute only.
A program may use at most 192 MiB of HBM per device.

v0:
```python
import jax
import jax.numpy as jnp
from jax import lax
from jax.sharding import PartitionSpec as P

H = 16
DK = 128
CONV = 4
BLOCK = 64


precise = lax.Precision.HIGHEST


def from_behind(block, axis, distance):
    devices = range(lax.axis_size(axis))
    route = [(i - distance, i) for i in devices if i - distance in devices]
    return lax.ppermute(block, axis, route)


def carried_in(x, axis, combine, identity):
    devices, mine = (lax.axis_size(axis), lax.axis_index(axis))
    everything = jax.tree.map(lambda part: lax.all_gather(part, axis), x)
    start = jax.tree.map(
        lambda part, zero: jnp.broadcast_to(jnp.asarray(zero, part.dtype), part.shape), x, identity
    )

    def lap(k, before):
        reached = k < mine
        new = combine(before, jax.tree.map(lambda part: part[k], everything))
        return jax.tree.map(lambda a, b: jnp.where(reached, a, b), new, before)

    return lax.fori_loop(0, devices, lap, start)


def unit_rows(vector):
    return vector * lax.rsqrt(jnp.sum(vector * vector, axis=-1, keepdims=True) + 1e-06)


def features(padded, count, conv_weight):
    combined = conv_weight[0] * padded[0:count].astype(jnp.float32)
    for offset in range(1, CONV):
        combined = combined + conv_weight[offset] * padded[offset : offset + count].astype(
            jnp.float32
        )
    active = jax.nn.silu(combined).reshape(count, 3, H, DK)
    query = unit_rows(active[:, 0]) * DK ** (-0.5)
    keys = unit_rows(active[:, 1])
    values = active[:, 2]
    return (query, keys, values)


def gates(tokens, decay_down, decay_up, decay_rate, beta_weight, beta_scale, gate_down, gate_up):
    beta = beta_scale * jax.nn.sigmoid(
        jnp.dot(tokens, beta_weight, preferred_element_type=jnp.float32)
    )
    decay_low = jnp.dot(tokens, decay_down, preferred_element_type=jnp.float32).astype(jnp.bfloat16)
    logdec = -decay_rate * jax.nn.sigmoid(
        jnp.dot(decay_low, decay_up, preferred_element_type=jnp.float32)
    )
    gate_low = jnp.dot(tokens, gate_down, preferred_element_type=jnp.float32).astype(jnp.bfloat16)
    gate_value = jax.nn.sigmoid(jnp.dot(gate_low, gate_up, preferred_element_type=jnp.float32))
    return (beta, logdec, gate_value)


def to_blocks(array, count):
    return array.reshape(count // BLOCK, BLOCK, H, array.shape[-1]).transpose(0, 2, 1, 3)


def block_terms(query, keys, values, beta, logdec):
    log_sum = jnp.cumsum(logdec, axis=2)
    grow = jnp.exp(log_sum)
    keys_up = keys * grow
    keys_down = keys * jnp.exp(-log_sum)
    query_up = query * grow
    keys_end = keys * jnp.exp(log_sum[:, :, -1:, :] - log_sum)
    length = query.shape[2]
    rows = lax.broadcasted_iota(jnp.int32, (length, length), 0)
    columns = lax.broadcasted_iota(jnp.int32, (length, length), 1)
    scores = jnp.einsum("nhic,nhjc->nhij", keys_up, keys_down, precision=precise) * beta[..., None]
    system = jnp.where(rows > columns, scores, 0.0) + jnp.eye(length, dtype=jnp.float32)
    right_side = jnp.concatenate([values, keys_up], axis=-1) * beta[..., None]
    solved = jax.scipy.linalg.solve_triangular(system, right_side, lower=True, unit_diagonal=True)
    values_w = solved[..., :DK]
    keys_w = solved[..., DK:]
    attend = jnp.where(
        rows >= columns, jnp.einsum("nhic,nhjc->nhij", query_up, keys_down, precision=precise), 0.0
    )
    decay_end = jnp.exp(log_sum[:, :, -1, :])
    return (query_up, keys_end, values_w, keys_w, attend, decay_end)


def advance(state, inputs):
    query_up, keys_end, values_w, keys_w, attend, decay_end = inputs
    update = values_w - jnp.einsum("hcd,hde->hce", keys_w, state, precision=precise)
    output = jnp.einsum("hcd,hde->hce", query_up, state, precision=precise)
    output = output + jnp.einsum("hij,hje->hie", attend, update, precision=precise)
    state = decay_end[..., None] * state + jnp.einsum(
        "hcd,hce->hde", keys_end, update, precision=precise
    )
    return (state, output)


def matmul(left, right):
    return jnp.einsum("...de,...ef->...df", left, right, precision=precise)


def fold_block(carry, inputs):
    matrix, offset = carry
    keys_end, keys_w, values_w, decay_end = inputs
    eye_block = jnp.eye(DK, dtype=jnp.float32)
    block_matrix = decay_end[..., None] * eye_block - jnp.einsum(
        "hcd,hce->hde", keys_end, keys_w, precision=precise
    )
    block_offset = jnp.einsum("hcd,hce->hde", keys_end, values_w, precision=precise)
    return ((matmul(block_matrix, matrix), matmul(block_matrix, offset) + block_offset), None)


def join_pairs(first, second):
    return (matmul(second[0], first[0]), matmul(second[0], first[1]) + second[1])


def finish(core, gate_value, norm_gain, count):
    scaled = core * lax.rsqrt(jnp.mean(core * core, axis=-1, keepdims=True) + 1e-06) * norm_gain
    return (scaled.reshape(count, H * DK) * gate_value).astype(jnp.bfloat16)


def per_device(
    tokens,
    qkv_weight,
    conv_weight,
    decay_down,
    decay_up,
    decay_rate,
    beta_weight,
    beta_scale,
    gate_down,
    gate_up,
    norm_gain,
):
    count = tokens.shape[0]
    mixed = jnp.dot(
        tokens,
        lax.all_gather(qkv_weight, "seq", axis=1, tiled=True),
        preferred_element_type=jnp.float32,
    ).astype(jnp.bfloat16)
    earlier = from_behind(mixed[count - (CONV - 1) :], "seq", 1)
    padded = jnp.concatenate([earlier, mixed], axis=0)
    query, keys, values = features(padded, count, conv_weight)
    beta, logdec, gate_value = gates(
        tokens, decay_down, decay_up, decay_rate, beta_weight, beta_scale, gate_down, gate_up
    )
    beta_blocks = beta.reshape(count // BLOCK, BLOCK, H).transpose(0, 2, 1)
    terms = block_terms(
        to_blocks(query, count),
        to_blocks(keys, count),
        to_blocks(values, count),
        beta_blocks,
        to_blocks(logdec.reshape(count, H, DK), count),
    )
    query_up, keys_end, values_w, keys_w, attend, decay_end = terms
    identity = jnp.broadcast_to(jnp.eye(DK, dtype=jnp.float32), (H, DK, DK))
    zeroed = jnp.zeros((H, DK, DK), jnp.float32)
    (matrix, offset), unused = lax.scan(
        fold_block, (identity, zeroed), (keys_end, keys_w, values_w, decay_end)
    )

    def combine(earlier_pair, later_pair):
        return join_pairs(earlier_pair, later_pair)

    prefix = carried_in((matrix, offset), "seq", combine, (identity, zeroed))
    incoming = prefix[1]
    final_state, outputs = lax.scan(advance, incoming, terms)
    core = outputs.transpose(0, 2, 1, 3).reshape(count, H, DK)
    return finish(core, gate_value, norm_gain, count)


def solution(mesh):
    in_specs = (
        P(("rep", "seq"), None),
        P(None, "seq"),
        P(),
        P(),
        P(),
        P(),
        P(),
        P(),
        P(),
        P(),
        P(),
    )
    out_specs = P(("rep", "seq"), None)
    return jax.shard_map(
        per_device, mesh=mesh, in_specs=in_specs, out_specs=out_specs, check_vma=False
    )
```

profile of v0, /device:TPU:1, one launch (start us, length us, event | category | flops | bytes accessed | tf_op | source)
XLA Modules:
  0.0 684.3 jit_solution(2664302093057689382)
XLA Ops:
  10.9 13.1 %fusion.63 = f32[2,16,64,128]{3,1,2,0:T(8,128)S(1)} fusion(f32[2,64,16,128]{3,2,1,0:T(8,128)S(1)} %bitcast.180), kind=kOutput, calls=%fused_computation.87 | output fusion | flops 16515072 | bytes 2097152 | tf_op jit(solution)/shard_map/jit(cumsum)/reduce_window_sum | solution.py:71
  24.4 89.2 %all-gather.6.cloned.1.call-done = bf16[2304,6144]{0,1:T(8,128)(2,1)} async-done(((bf16[2304,192]{0,1:T(8,128)(2,1)}), bf16[2304,6144]{0,1:T(8,128)(2,1)}) %all-gather.6.cloned.1.call-update) | async-done | bytes 28311568 | tf_op jit(solution)/shard_map/all_gather | solution.py:144
  113.6 14.3 %convolution_convert_fusion = bf16[128,6144]{1,0:T(8,128)(2,1)S(1)} fusion(bf16[128,2304]{1,0:T(8,128)(2,1)S(1)} %copy-done, bf16[2304,6144]{0,1:T(8,128)(2,1)} %all-gather.6.cloned.1.call-done), kind=kOutput, calls=%fused_computation.48 | convolution fusion | flops 3624665088 | bytes 30474240 | tf_op jit(solution)/shard_map/dot_general | solution.py:142
  128.6 3.4 collective-permute-start
  139.4 3.3 fusion.57
  142.7 158.7 %custom-call.4 = f32[2,16,1,64,64]{3,4,2,1,0:T(8,128)} custom-call(f32[2,16,1,64,64]{4,3,2,1,0:T(8,128)} %fusion.57), custom_call_target="InvertDiagBlocksLowerTriangular" | custom-call | tf_op jit(solution)/shard_map/jit(_solve_triangular)/vmap(vmap())/triangular_solve | solution.py:83
  303.0 3.0 fusion.48
  309.2 20.1 %while.40 = (s32[]{:T(128)}, f32[16,128,128]{2,1,0:T(8,128)}, f32[16,128,128]{2,1,0:T(8,128)}, f32[2,16,128]{2,1,0:T(8,128)S(1)}, f32[2,16,64,128]{3,2,1,0:T(8,1...) while((s32[]{:T(128)}, f32[16,128,128]{2,1,0:T(8,128)}, ...), condition=%wide.region_3.4_spmd.clone, body=%wide.region_2.3_spmd.clone.sunk | while | flops 1209040896 | bytes 22177956 | solution.py:164
  309.2 3.1 convolution_subtract_fusion.5
  318.6 3.1 convolution_subtract_fusion.5
  332.7 4.8 convolution_select_fusion
  337.5 107.0 %all-gather.8.cloned.1.call-done = f32[512,128,128]{2,1,0:T(8,128)} async-done(((f32[16,128,128]{2,1,0:T(8,128)}), f32[512,128,128]{2,1,0:T(8,128)}) %all-gather.8.cloned.1.call-update) | async-done | bytes 33554448 | tf_op jit(solution)/shard_map/all_gather | solution.py:23
  444.5 115.5 %all-gather.10.cloned.1.call-done = f32[512,128,128]{2,1,0:T(8,128)} async-done(((f32[16,128,128]{2,1,0:T(8,128)}), f32[512,128,128]{2,1,0:T(8,128)}) %all-gather.10.cloned.1.call-update) | async-done | bytes 33554448 | tf_op jit(solution)/shard_map/all_gather | solution.py:23
  559.9 94.0 %while.41 = (s32[]{:T(128)}, f32[16,128,128]{2,1,0:T(8,128)S(1)}, s32[]{:T(128)}, f32[32,16,128,128]{3,2,1,0:T(8,128)}, f32[32,16,128,128]{3,2,1,0:T(8,128)}, /*index=5*/s32[]{:T(128)}, s32[]{:T(128)}) while((s32[]{:T(128)}, f32[16,128,128]{2,1,0:T(8,128)S(1)}, s32[]{:T(128)}, f32[32,16,128,128]{3,2,1,0:T(8,128)}, ...), condition=%wide.region_5.6_spmd.clone, body=%wide.region_4.5_spmd.clone.sunk | while | flops 403701760 | bytes 7342687 | solution.py:33
  560.0 2.8 fusion.141
  563.0 2.8 fusion.141
  568.8 2.8 fusion.141
  571.8 2.8 fusion.141
  574.7 2.8 fusion.141
  577.6 2.8 fusion.141
  580.6 2.8 fusion.141
  583.5 2.8 fusion.141
  586.5 2.8 fusion.141
  589.4 2.8 fusion.141
  592.3 2.8 fusion.141
  595.3 2.8 fusion.141
  598.2 2.8 fusion.141
  601.1 2.8 fusion.141
  604.1 2.8 fusion.141
  607.0 2.8 fusion.141
  653.9 17.0 %while.39 = (s32[]{:T(128)}, f32[16,128,128]{2,1,0:T(8,128)S(1)}, f32[2,16,64,128]{3,2,1,0:T(8,128)}, f32[2,16,128]{2,1,0:T(8,128)S(1)}, f32[2,16,64,128]{3,2,1,...) while((s32[]{:T(128)}, f32[16,128,128]{2,1,0:T(8,128)S(1)}, ...), condition=%wide.region_8.9_spmd, body=%wide.region_7.8_spmd.sunk | while | flops 705429504 | bytes 22571712 | solution.py:173
  674.9 2.9 fusion.47
  (158 shorter events, 103.0 us)
Async XLA Ops:
  6.5 1.5 copy-start
  6.5 107.1 %all-gather.6.cloned.1.call-start = ((), (), s32[]{:S(2)}) async-start(), calls=%async_computation | async-start | bytes 29196288 | tf_op jit(solution)/shard_map/all_gather | solution.py:144
  7.3 437.2 %all-gather.8.cloned.1.call-start = ((), (), s32[]{:S(2)}) async-start(), calls=%async_computation.1 | async-start | bytes 34603008 | tf_op jit(solution)/shard_map/all_gather | solution.py:23
  9.9 14.0 %copy-start.12 = (bf16[2304,16]{0,1:T(8,128)(2,1)S(1)}, bf16[2304,16]{0,1:T(8,128)(2,1)}, u32[]{:S(2)}) copy-start(bf16[2304,16]{0,1:T(8,128)(2,1)} %param.23) | copy-start | bytes 221188
  9.9 14.0 %copy-start.15 = (f32[16]{0:T(128)S(1)}, f32[16]{0:T(128)}, u32[]{:S(2)}) copy-start(f32[16]{0:T(128)} %param.24) | copy-start | bytes 196
  10.0 14.3 %copy-start.11 = (f32[4,6144]{1,0:T(4,128)S(1)}, f32[4,6144]{1,0:T(4,128)}, u32[]{:S(2)}) copy-start(f32[4,6144]{1,0:T(4,128)} %param.19) | copy-start | bytes 294916
  23.9 104.0 %copy-start.5 = (f32[2,16,64,128]{3,1,2,0:T(8,128)}, f32[2,16,64,128]{3,1,2,0:T(8,128)S(1)}, u32[]{:S(2)}) copy-start(f32[2,16,64,128]{3,1,2,0:T(8,128)S(1)} %fusion.63) | copy-start | bytes 3145732
  128.6 4.7 collective-permute-start
  136.0 1.6 copy-start.6
  137.6 1.8 copy-start.13
  137.6 1.8 copy-start.14
  139.4 163.6 %copy-start.4 = (f32[2,16,64,128]{3,1,2,0:T(8,128)}, f32[2,16,64,128]{3,1,2,0:T(8,128)S(1)}, u32[]{:S(2)}) copy-start(f32[2,16,64,128]{3,1,2,0:T(8,128)S(1)} %get-tuple-element.325) | copy-start | bytes 3145732
  301.4 1.7 copy-start.10
  306.1 1.7 copy-start.7
  309.2 20.9 %copy-start.16 = (f32[128]{0:T(128)S(1)}, f32[128]{0:T(128)}, u32[]{:S(2)}) copy-start(f32[128]{0:T(128)} %param.27) | copy-start | bytes 1540
  312.2 1.2 copy-start.2
  312.3 4.0 copy-start.1
  321.6 2.6 copy-start.2
  321.6 5.4 copy-start.1
  329.3 230.6 %all-gather.10.cloned.1.call-start = ((), (), s32[]{:S(2)}) async-start(), calls=%async_computation.2 | async-start | bytes 34603008 | tf_op jit(solution)/shard_map/all_gather | solution.py:23
  653.9 4.1 copy-start.3
  653.9 4.1 copy-start.8
  659.1 1.0 copy-start.9
  662.4 4.1 copy-start.3
  662.4 4.1 copy-start.8
  667.7 1.0 copy-start.9
  671.0 3.9 copy-start.17
Sparse Core Ops, SparseCore 0:
  9.6 103.9 all-gather.5
  329.4 114.9 all-gather.7
  446.7 113.1 all-gather.9
where the time goes:
time: 686 us; the launch traced here: 684 us
  waiting for transfers between devices  314 us (46%)
  other arithmetic  182 us (27%)
  matrix products  155 us (23%)
  local copies, waits for them, and re-layouts  14.4 us (2%)
  between operations  13.5 us (2%)
    all_gather x2, waiting for transfers between devices, carried_in(): everything = jax.tree.map(lambda part: lax.all_gather(part, axis), x)  222 us
    another operation x2, other arithmetic, block_terms(): jax.scipy.linalg.solve_triangular(system, right_side, lower=True, unit_di...  159 us
    dot_general x36, matrix products, matmul(): return jnp.einsum('...de,...ef->...df', left, right, precision=precise)  98.3 us
    all_gather x1, waiting for transfers between devices, per_device(): lax.all_gather(qkv_weight, 'seq', axis=1, tiled=True)  89.2 us
    dot_general x1, matrix products, per_device(): jnp.dot(tokens, lax.all_gather(qkv_weight, 'seq', axis=1, tiled=True), pr...  14.3 us
  transfers between devices with their start and end apart: 4, of which 4 were waited for; matrix products, arithmetic and copies ran while one was open for 4% of the time, Pallas kernels for 0%

commit v1 on v0

v1 whole, which is shorter than its diff:
```python
import functools

import jax
import jax.numpy as jnp
import numpy as np
from jax import lax
from jax.experimental import pallas as pl
from jax.experimental.pallas import tpu as pltpu
from jax.sharding import Mesh
from jax.sharding import PartitionSpec as P

H = 16
DK = 128
CONV = 4
D = 2304
HV = H * DK
BF = jnp.bfloat16
F32 = jnp.float32

NZ, NX, NC, NY = 4, 4, 2, 4
ROW = NX * NC
SHARD = 128
GROUP = ROW * SHARD
QUART = D // NY
UNIT = 64
PACK = QUART // 2
HALF = PACK // 2
VMEM_LIMIT = 56 * 1024 * 1024


def unit_plan():
    count = NZ * ROW
    units = 3 * HV // UNIT
    dest = {}
    for u in range(units):
        kind, rest = divmod(u, HV // UNIT)
        head, half = divmod(rest, 2)
        dest[u] = (((head % 2) * 2 + half) * ROW + head // 2, kind)
    left = {i: [3 * i, 3 * i + 1, 3 * i + 2] for i in range(count)}
    sends, routes = [], []
    arrival = np.zeros((count, 3), np.int32)
    for r in range(3):
        owner = {}

        def place(i, seen):
            for u in left[i]:
                d = dest[u][0]
                if d in seen:
                    continue
                seen.add(d)
                if d not in owner or place(owner[d][0], seen):
                    owner[d] = (i, u)
                    return True
            return False

        for i in range(count):
            assert place(i, set())
        table = np.zeros(count, np.int32)
        route = []
        for d, (i, u) in owner.items():
            table[i] = u - 3 * i
            arrival[d, dest[u][1]] = r
            route.append((i, d))
            left[i].remove(u)
        sends.append(table)
        routes.append(sorted(route))
    order = arrival.reshape(NZ, ROW, 3).transpose(1, 0, 2).reshape(ROW, NZ * 3)
    return sends, routes, order


SENDS, ROUTES, ORDER = unit_plan()


def ring(distance, size=4):
    return [(i, (i + distance) % size) for i in range(size)]


def ahead(distance, size=4):
    return [(i, i + distance) for i in range(size - distance)]


def split(x):
    high = x.astype(BF)
    return high, (x - high.astype(F32)).astype(BF)


def dot(a, b):
    return lax.dot_general(a, b, (((1,), (0,)), ((), ())), preferred_element_type=F32)


def dot_nt(a, b):
    return lax.dot_general(a, b, (((1,), (1,)), ((), ())), preferred_element_type=F32)


def mm3(a, b):
    ah, al = split(a)
    bh, bl = split(b)
    return dot(jnp.concatenate([ah, al, ah], axis=1), jnp.concatenate([bh, bh, bl], axis=0))


def mm3_nt(a, b):
    ah, al = split(a)
    bh, bl = split(b)
    return dot_nt(jnp.concatenate([ah, al, ah], axis=1), jnp.concatenate([bh, bh, bl], axis=1))


def sigmoid(x):
    return 1.0 / (1.0 + jnp.exp(-x))


def unit_lower_inverse(a, rows, cols):
    eye = jnp.where(rows == cols, 1.0, 0.0)
    inverse = eye - jnp.where((rows // 2) == (cols // 2), a, 0.0)
    size = 2
    while size < SHARD:
        band = ((rows // (2 * size)) == (cols // (2 * size))) & ((rows // size) != (cols // size))
        low = jnp.where(band, a, 0.0).astype(BF)
        near = inverse.astype(BF)
        inverse = inverse - dot(dot(near, low).astype(BF), near)
        size *= 2
    near = inverse.astype(BF)
    ah, al = split(a)
    rest = (
        eye
        - near.astype(F32)
        - dot(jnp.concatenate([ah, al], axis=1), jnp.concatenate([near, near], axis=0))
    )
    return near.astype(F32) + dot(near, rest.astype(BF))


def block_kernel(
    sp,
    own,
    oth,
    halo,
    wsmall,
    decay_up,
    gate_up,
    rate,
    beta_scale,
    conv_q,
    conv_k,
    conv_v,
    *rest,
):
    parts = rest[:8]
    qeff_o, core_o, gate_o, state_o = rest[8:12]
    abuf, bbuf, wbuf, mbuf, tbuf, state, sems = rest[12:]
    step = pl.program_id(0)
    z, c, y, g = sp[0], sp[1], sp[2], sp[3]

    @pl.when(step == 0)
    def _():
        copies = []
        for k in range(4):
            copies.append(
                pltpu.make_async_copy(parts[k], abuf.at[lax.rem(y - k + 4, 4)], sems.at[k])
            )
            copies.append(
                pltpu.make_async_copy(parts[4 + k], bbuf.at[lax.rem(z - k + 4, 4)], sems.at[4 + k])
            )
        for copy in copies:
            copy.start()
        for copy in copies:
            copy.wait()

        def place(row, kind, hp, first, second):
            cols = pl.ds(kind * 256 + hp * 128, 128)
            wbuf[pl.ds(row, HALF), cols] = jnp.concatenate(
                [first[:, :UNIT], second[:, :UNIT]], axis=1
            )
            wbuf[pl.ds(row + PACK, HALF), cols] = jnp.concatenate(
                [first[:, UNIT:], second[:, UNIT:]], axis=1
            )

        for yy in range(4):
            ky = lax.rem(y - yy + 4, 4)
            for kind in range(3):
                for hp in range(2):
                    pa, pb = [], []
                    for half in range(2):
                        zz = 2 * hp + half
                        kz = lax.rem(z - zz + 4, 4)
                        order = sp[4 + 3 * zz + kind]
                        pa.append(abuf[yy, kz, order])
                        pb.append(bbuf[zz, ky, order])
                    place(QUART * yy, kind, hp, *pa)
                    place(QUART * yy + HALF, kind, hp, *pb)
        before = dot(halo[...], wbuf[...]).astype(BF).astype(F32)
        mbuf[0:8] = before[8:16]
        rr = lax.broadcasted_iota(jnp.int32, (DK, 2 * DK), 0)
        cc = lax.broadcasted_iota(jnp.int32, (DK, 2 * DK), 1)
        start = jnp.where(rr == cc, 1.0, 0.0)
        state[0] = start
        state[1] = start

    @pl.when(c == 0)
    def _():
        tbuf[0:SHARD] = own[0]
        tbuf[SHARD:] = oth[0]

    @pl.when(c != 0)
    def _():
        tbuf[0:SHARD] = oth[0]
        tbuf[SHARD:] = own[0]

    tok = tbuf[...]
    small = dot(tok, wsmall[...])
    decay_low = small[:, :128].astype(BF)
    gate_low = small[:, 128:256].astype(BF)
    beta_all = beta_scale[...] * sigmoid(small[:, 256:])
    logdec = -rate[...] * sigmoid(dot(decay_low, decay_up[...]))
    gate_o[...] = sigmoid(dot(gate_low, gate_up[...]))
    mbuf[8:] = dot(tok, wbuf[...]).astype(BF).astype(F32)

    def active(kind, taps):
        cols = slice(256 * kind, 256 * kind + 256)
        total = taps[0:1] * mbuf[5 : 5 + 256, cols]
        for j in range(1, CONV):
            total = total + taps[j : j + 1] * mbuf[5 + j : 5 + j + 256, cols]
        return total * sigmoid(total)

    query = active(0, conv_q)
    keys = active(1, conv_k)
    values = active(2, conv_v)
    mbuf[0:8] = mbuf[256:264]

    rows = lax.broadcasted_iota(jnp.int32, (SHARD, SHARD), 0)
    cols = lax.broadcasted_iota(jnp.int32, (SHARD, SHARD), 1)
    ones_low = jnp.where(rows >= cols, 1.0, 0.0).astype(BF)
    lane = lax.broadcasted_iota(jnp.int32, (SHARD, 128), 1)
    for h in range(2):
        hs = slice(DK * h, DK * h + DK)
        for blk in range(2):
            ts = slice(SHARD * blk, SHARD * blk + SHARD)
            q, k, v = query[ts, hs], keys[ts, hs], values[ts, hs]
            q = q * (lax.rsqrt(jnp.sum(q * q, axis=1, keepdims=True) + 1e-06) * DK**-0.5)
            k = k * lax.rsqrt(jnp.sum(k * k, axis=1, keepdims=True) + 1e-06)
            beta = jnp.sum(
                jnp.where(lane == 2 * g + h, beta_all[ts], 0.0), axis=1, keepdims=True
            )
            lh, ll = split(logdec[ts, hs])
            log_sum = dot(
                jnp.concatenate([ones_low, ones_low], axis=1), jnp.concatenate([lh, ll], axis=0)
            )
            grow = jnp.exp(log_sum)
            end = log_sum[SHARD - 1 : SHARD]
            k_up = k * grow
            k_down = k * jnp.exp(-log_sum)
            q_up = q * grow
            k_end = k * jnp.exp(end - log_sum)
            both = mm3_nt(jnp.concatenate([k_up, q_up], axis=0), k_down)
            system = jnp.where(rows > cols, both[:SHARD], 0.0) * beta
            attend = jnp.where(rows >= cols, both[SHARD:], 0.0)
            inverse = unit_lower_inverse(system, rows, cols)
            solved = mm3(inverse, jnp.concatenate([k_up, v], axis=1) * beta)
            mixed = mm3(jnp.concatenate([attend, k_end.T], axis=0), solved)
            q_full = q_up - mixed[:SHARD, :DK]
            step_matrix = jnp.where(rows == cols, jnp.exp(end), 0.0) - mixed[SHARD:, :DK]
            carry = state[h]
            out = mm3(jnp.concatenate([q_full, step_matrix], axis=0), carry)
            qeff_o[ts, hs] = out[:SHARD, :DK]
            core_o[ts, hs] = out[:SHARD, DK:] + mixed[:SHARD, DK:]
            state[h, :, :DK] = out[SHARD:, :DK]
            state[h, :, DK:] = out[SHARD:, DK:] + mixed[SHARD:, DK:]

    @pl.when(step == pl.num_programs(0) - 1)
    def _():
        state_o[...] = state[...]


def run_blocks(sp, own, oth, halo, wsmall, decay_up, gate_up, rate, beta_scale, conv, parts):
    def fixed(shape):
        return pl.BlockSpec(shape, lambda i, s: (0,) * len(shape))

    def by_group(shape, offset=0):
        return pl.BlockSpec(shape, lambda i, s: (0, s[3] + offset))

    steps = NX
    token_spec = pl.BlockSpec((1, SHARD, D), lambda i, s: (i, 0, 0))
    out_spec = pl.BlockSpec((2 * SHARD, 2 * DK), lambda i, s: (i, 0))
    big = jax.ShapeDtypeStruct((GROUP, 2 * DK), F32)
    return pl.pallas_call(
        block_kernel,
        name="block_terms",
        out_shape=(big, big, big, jax.ShapeDtypeStruct((2, DK, 2 * DK), F32)),
        grid_spec=pltpu.PrefetchScalarGridSpec(
            num_scalar_prefetch=1,
            grid=(steps,),
            in_specs=[
                token_spec,
                token_spec,
                fixed((16, D)),
                fixed((D, 384)),
                by_group((128, 256)),
                by_group((128, 256)),
                by_group((1, 256)),
                fixed((1, 128)),
                by_group((CONV, 256)),
                by_group((CONV, 256), 8),
                by_group((CONV, 256), 16),
            ]
            + [pl.BlockSpec(memory_space=pl.ANY)] * 8,
            out_specs=[out_spec, out_spec, out_spec, fixed((2, DK, 2 * DK))],
            scratch_shapes=[
                pltpu.VMEM((4, 4, 3, HALF, 128), BF),
                pltpu.VMEM((4, 4, 3, HALF, 128), BF),
                pltpu.VMEM((D, 768), BF),
                pltpu.VMEM((8 + 2 * SHARD, 768), F32),
                pltpu.VMEM((2 * SHARD, D), BF),
                pltpu.VMEM((2, DK, 2 * DK), F32),
                pltpu.SemaphoreType.DMA((8,)),
            ],
        ),
        compiler_params=pltpu.CompilerParams(vmem_limit_bytes=VMEM_LIMIT),
    )(
        sp, own, oth, halo, wsmall, decay_up, gate_up, rate, beta_scale, conv, conv, conv, *parts
    )


def finish_kernel(near, middle, far, qeff, core, gate, gain, out, state):
    @pl.when(pl.program_id(0) == 0)
    def _():
        for h in range(2):
            carry = middle[h, :, DK:] + mm3(middle[h, :, :DK], far[h])
            state[h] = near[h, :, DK:] + mm3(near[h, :, :DK], carry)

    for h in range(2):
        hs = slice(DK * h, DK * h + DK)
        full = core[:, hs] + mm3(qeff[:, hs], state[h])
        scale = lax.rsqrt(jnp.mean(full * full, axis=1, keepdims=True) + 1e-06)
        out[:, hs] = (full * scale * gain[...] * gate[:, hs]).astype(BF)


def run_finish(near, middle, far, qeff, core, gate, gain):
    def fixed(shape):
        return pl.BlockSpec(shape, lambda i: (0,) * len(shape))

    tile = pl.BlockSpec((256, 2 * DK), lambda i: (i, 0))
    return pl.pallas_call(
        finish_kernel,
        name="finish",
        out_shape=jax.ShapeDtypeStruct((GROUP, 2 * DK), BF),
        grid=(GROUP // 256,),
        in_specs=[
            fixed((2, DK, 2 * DK)),
            fixed((2, DK, 2 * DK)),
            fixed((2, DK, DK)),
            tile,
            tile,
            tile,
            fixed((1, DK)),
        ],
        out_specs=tile,
        scratch_shapes=[pltpu.VMEM((2, DK, DK), F32)],
        compiler_params=pltpu.CompilerParams(vmem_limit_bytes=VMEM_LIMIT),
    )(near, middle, far, qeff, core, gate, gain)


def gather_weights(weight, z, place, y):
    quarter = lax.dynamic_slice(weight, (QUART * y, 0), (QUART, 3 * UNIT))
    units = jnp.stack(
        [
            jnp.concatenate(
                [
                    quarter[:PACK, UNIT * k : UNIT * k + UNIT],
                    quarter[PACK:, UNIT * k : UNIT * k + UNIT],
                ],
                axis=1,
            )
            for k in range(3)
        ]
    )
    arrived = []
    for table, route in zip(SENDS, ROUTES):
        unit = lax.dynamic_index_in_dim(units, jnp.asarray(table)[place], 0, keepdims=False)
        arrived.append(lax.ppermute(unit, ("z", "x", "c"), route))
    mine = jnp.stack(arrived)

    def spread(block, axis):
        return [block] + [lax.ppermute(block, axis, ring(k)) for k in range(1, 4)]

    upper, lower = mine[:, :HALF], mine[:, HALF:]
    upper_z, lower_y = jnp.stack(spread(upper, "z")), jnp.stack(spread(lower, "y"))
    return spread(upper_z, "y") + spread(lower_y, "z")


def per_device(
    tokens,
    qkv_weight,
    conv_weight,
    decay_down,
    decay_up,
    decay_rate,
    beta_weight,
    beta_scale,
    gate_down,
    gate_up,
    norm_gain,
):
    z, x, c, y = (lax.axis_index(a) for a in ("z", "x", "c", "y"))
    g = x * NC + c
    own = lax.all_gather(tokens, "x", axis=0)
    parts = gather_weights(qkv_weight, z, z * ROW + g, y)
    oth = lax.ppermute(own, "c", [(0, 1), (1, 0)])
    last = jnp.where(c == NC - 1, own[NX - 1, SHARD - 16 :], oth[NX - 1, SHARD - 16 :])
    halo = lax.ppermute(last, "z", ahead(1))
    wsmall = jnp.concatenate(
        [decay_down, gate_down, jnp.pad(beta_weight, ((0, 0), (0, 128 - H)))], axis=1
    )
    sp = jnp.concatenate(
        [jnp.stack([z, c, y, g]).astype(jnp.int32), jnp.asarray(ORDER)[g].astype(jnp.int32)]
    )
    qeff, core, gate, state = run_blocks(
        sp,
        own,
        oth,
        halo,
        wsmall,
        decay_up,
        gate_up,
        decay_rate.reshape(1, HV),
        jnp.pad(beta_scale, (0, 128 - H)).reshape(1, 128),
        conv_weight,
        parts,
    )
    near = lax.ppermute(state, "z", ahead(1))
    middle = lax.ppermute(state, "z", ahead(2))
    far = lax.ppermute(state[:, :, DK:], "z", ahead(3))
    out = run_finish(near, middle, far, qeff, core, gate, norm_gain.reshape(1, DK))
    out = lax.all_to_all(out.reshape(ROW, SHARD, 2 * DK), ("x", "c"), 0, 0)
    return out.transpose(1, 0, 2).reshape(SHARD, HV)


def solution(mesh):
    fine = Mesh(mesh.devices.reshape(NZ, NX, NC, NY), ("z", "x", "c", "y"))
    seq = ("z", "x", "c")
    in_specs = (P(("y",) + seq, None), P(None, seq)) + (P(),) * 9
    return jax.shard_map(
        per_device,
        mesh=fine,
        in_specs=in_specs,
        out_specs=P(("y",) + seq, None),
        check_vma=False,
    )
```

time: 686 us -> 215 us (0.31)
  waiting for transfers between devices: 314 us -> 58 us
  other arithmetic: 182 us -> 5.23 us
  matrix products: 155 us -> 0 us
  Pallas kernels: 0 us -> 58.8 us
  starting transfers between devices: 3.45 us -> 38.5 us
  blocking collectives: 0 us -> 27.6 us
    all_gather x3 -> x1, waiting for transfers between devices: 312 us -> 38 us  [per_device(): own = lax.all_gather(tokens, 'x', axis=0)]
    another operation x3, other arithmetic: 172 us -> 1.2 us  [the longest x1 1.11 us: gather_weights(): jnp.stack(spread(upper, 'z'))]
    dot_general x54 -> x0, matrix products: 152 us -> none  [the longest x36 98.3 us: matmul(): return jnp.einsum('...de,...ef->...df', left, right, precision=precise)]
    pallas_call x0 -> x2, Pallas kernels: none -> 58.8 us  [the longest x1 53.7 us: run_blocks(): pl.pallas_call(block_kernel, name='block_terms', out_shape=(big, big, big...]
    ppermute x1 -> x20, starting transfers between devices: 3.36 us -> 38.5 us  [the longest x12 20.6 us: spread(): return [block] + [lax.ppermute(block, axis, ring(k)) for k in range(1, 4)]]
    all_to_all x0 -> x1, blocking collectives: none -> 27.6 us  [per_device(): out = lax.all_to_all(out.reshape(ROW, SHARD, 2 * DK), ('x', 'c'), 0, 0)]
    ppermute x1 -> x20, waiting for transfers between devices: 1.1 us -> 19.3 us  [the longest x12 14.2 us: spread(): return [block] + [lax.ppermute(block, axis, ring(k)) for k in range(1, 4)]]
    while x55 -> x0, local copies, waits for them, and re-layouts: 7.31 us -> none
  transfers between devices with their start and end apart: 4 -> 21, of which waited for: 4 -> 10; matrix products, arithmetic and copies ran while one was open for 4% -> 6% of each run, Pallas kernels for 0% -> 0%
where the time goes in v1:
time: 215 us; the launch traced here: 212 us
  Pallas kernels  58.8 us (27%)
  waiting for transfers between devices  58 us (27%)
  starting transfers between devices  38.5 us (18%)
  blocking collectives  27.6 us (13%)
  between operations  13.7 us (6%)
  local copies, waits for them, and re-layouts  10.2 us (5%)
  other arithmetic  5.23 us (2%)
    pallas_call x1, Pallas kernels, run_blocks(): pl.pallas_call(block_kernel, name='block_terms', out_shape=(big, big, big...  53.7 us
    all_gather x1, waiting for transfers between devices, per_device(): own = lax.all_gather(tokens, 'x', axis=0)  38 us
    all_to_all x1, blocking collectives, per_device(): out = lax.all_to_all(out.reshape(ROW, SHARD, 2 * DK), ('x', 'c'), 0, 0)  27.6 us
    ppermute x12, starting transfers between devices, spread(): return [block] + [lax.ppermute(block, axis, ring(k)) for k in range(1, 4)]  20.6 us
    ppermute x12, waiting for transfers between devices, spread(): return [block] + [lax.ppermute(block, axis, ring(k)) for k in range(1, 4)]  14.2 us
    ppermute x3, starting transfers between devices, gather_weights(): arrived.append(lax.ppermute(unit, ('z', 'x', 'c'), route))  7.82 us
    pallas_call x1, Pallas kernels, run_finish(): pl.pallas_call(finish_kernel, name='finish', out_shape=jax.ShapeDtypeStru...  5.08 us
    unnamed x39, local copies, waits for them, and re-layouts  4.63 us
  transfers between devices with their start and end apart: 21, of which 10 were waited for; matrix products, arithmetic and copies ran while one was open for 6% of the time, Pallas kernels for 0%

profile of v1, /device:TPU:1, one launch (start us, length us, event | category | flops | bytes accessed | tf_op | source)
XLA Modules:
  0.0 212.0 jit_solution(15341356618005845184)
XLA Ops:
  7.3 38.0 %all-gather.3.cloned.1.call-done = bf16[512,2304]{1,0:T(8,128)(2,1)} async-done(((bf16[128,2304]{1,0:T(8,128)(2,1)}), bf16[512,2304]{1,0:T(8,128)(2,1)}) %all-gather.3.cloned.1.call-update) | async-done | bytes 2359312 | tf_op jit(solution)/shard_map/all_gather | solution.py:403
  45.9 1.2 constant_dynamic-slice_fusion.1
  47.4 3.2 %collective-permute-start.4 = (bf16[288,128]{1,0:T(8,128)(2,1)S(1)}, bf16[288,128]{1,0:T(8,128)(2,1)S(1)}, u32[]{:S(2)}, u32[]{:S(2)}) collective-permute-start(bf16[288,128]{1,0:T(8,128)(2,1)S(1)} %pad_maximum_fusion.5), channel_id=1, source_target_pairs={{0,64},{4,36},{8,8},{12,104},{16,76},{20,48},{24,20},{28,116},{32,... | collective-permute-start | bytes 221192 | tf_op jit(solution)/shard_map/ppermute | solution.py:377
  51.0 4.0 %collective-permute-start.2 = (bf16[288,128]{1,0:T(8,128)(2,1)S(1)}, bf16[288,128]{1,0:T(8,128)(2,1)S(1)}, u32[]{:S(2)}, u32[]{:S(2)}) collective-permute-start(bf16[288,128]{1,0:T(8,128)(2,1)S(1)} %pad_maximum_fusion.3), channel_id=1, source_target_pairs={{0,0},{4,96},{8,68},{12,40},{16,12},{20,108},{24,80},{28,52},{32,2... | collective-permute-start | bytes 221192 | tf_op jit(solution)/shard_map/ppermute | solution.py:377
  56.0 2.0 collective-permute-done.4
  58.0 1.1 collective-permute-done.2
  59.1 0.7 slice_bitcast_fusion
  59.8 5.6 %collective-permute-start.6 = (bf16[3,144,128]{2,1,0:T(8,128)(2,1)S(1)}, bf16[3,144,128]{2,1,0:T(8,128)(2,1)S(1)}, u32[]{:S(2)}, u32[]{:S(2)}) collective-permute-start(bf16[3,144,128]{2,1,0:T(8,128)(2,1)S(1)} %get-tuple-element.22), channel_id=1, source_target_pairs={{0,64},{32,96},{64,0},{96,32},{1,65},{33,97},{65,1},{97,33},{2,66}... | collective-permute-start | bytes 331784 | tf_op jit(solution)/shard_map/ppermute | solution.py:381
  65.7 2.4 %collective-permute-start.7 = (bf16[3,144,128]{2,1,0:T(8,128)(2,1)S(1)}, bf16[3,144,128]{2,1,0:T(8,128)(2,1)S(1)}, u32[]{:S(2)}, u32[]{:S(2)}) collective-permute-start(bf16[3,144,128]{2,1,0:T(8,128)(2,1)S(1)} %get-tuple-element.22), channel_id=1, source_target_pairs={{0,96},{32,0},{64,32},{96,64},{1,97},{33,1},{65,33},{97,65},{2,98}... | collective-permute-start | bytes 331784 | tf_op jit(solution)/shard_map/ppermute | solution.py:381
  68.1 1.2 copy.16
  69.4 1.8 collective-permute-done.5
  71.9 1.1 pad_maximum_fusion.rest_0_
  73.0 2.5 %collective-permute-start.10 = (bf16[4,3,144,128]{3,2,1,0:T(8,128)(2,1)S(1)}, bf16[4,3,144,128]{3,2,1,0:T(8,128)(2,1)}, u32[]{:S(2)}, u32[]{:S(2)}) collective-permute-start(bf16[4,3,144,128]{3,2,1,0:T(8,128)(2,1)S(1)} %pad_maximum_fusion.rest_0_), channel_id=1, source_target_pairs={{0,3},{1,0},{2,1},{3,2},{4,7},{5,4},{6,5},{7,6},{8,11},{9,8},{10,9... | collective-permute-start | bytes 1327112 | tf_op jit(solution)/shard_map/ppermute | solution.py:381
  75.6 2.8 %fusion.1.wsmall = bf16[2304,384]{1,0:T(8,128)(2,1)} fusion(bf16[2304,16]{1,0:T(8,128)(2,1)S(1)} %copy.16, bf16[2304,128]{1,0:T(8,128)(2,1)} %param.23, bf16[2304,128]{1,0:T(8,128)(2,1)} %param.18), kind=kLoop, calls=%fused_computation.2 | loop fusion | flops 7077888 | bytes 3022848 | tf_op jit(solution)/shard_map/concatenate | solution.py:408
  79.5 2.1 collective-permute-start.13
  82.8 0.9 collective-permute-done.12
  84.8 2.4 %collective-permute-start.8 = (bf16[4,3,144,128]{3,2,1,0:T(8,128)(2,1)S(1)}, bf16[4,3,144,128]{3,2,1,0:T(8,128)(2,1)S(1)}, u32[]{:S(2)}, u32[]{:S(2)}) collective-permute-start(bf16[4,3,144,128]{3,2,1,0:T(8,128)(2,1)S(1)} %pad_maximum_fusion.rest_0_), channel_id=1, source_target_pairs={{0,1},{1,2},{2,3},{3,0},{4,5},{5,6},{6,7},{7,4},{8,9},{9,10},{10,1... | collective-permute-start | bytes 1327112 | tf_op jit(solution)/shard_map/ppermute | solution.py:381
  87.3 1.1 collective-permute-start.16
  88.5 2.6 %collective-permute-start.15 = (bf16[4,3,144,128]{3,2,1,0:T(8,128)(2,1)S(1)}, bf16[4,3,144,128]{3,2,1,0:T(8,128)(2,1)S(1)}, u32[]{:S(2)}, u32[]{:S(2)}) collective-permute-start(bf16[4,3,144,128]{3,2,1,0:T(8,128)(2,1)S(1)} %pad_maximum_fusion.1.rest_4_), channel_id=1, source_target_pairs={{0,64},{32,96},{64,0},{96,32},{1,65},{33,97},{65,1},{97,33},{2,66}... | collective-permute-start | bytes 1327112 | tf_op jit(solution)/shard_map/ppermute | solution.py:381
  91.1 1.0 fusion.2
  92.0 1.8 collective-permute-done.9.rest_2_
  93.9 3.0 %collective-permute-start.1 = (bf16[16,2304]{1,0:T(8,128)(2,1)S(1)}, bf16[16,2304]{1,0:T(8,128)(2,1)S(1)}, u32[]{:S(2)}, u32[]{:S(2)}) collective-permute-start(bf16[16,2304]{1,0:T(8,128)(2,1)S(1)} %fusion.2), channel_id=1, source_target_pairs={{0,32},{32,64},{64,96},{1,33},{33,65},{65,97},{2,34},{34,66},{66,9... | collective-permute-start | bytes 221192 | tf_op jit(solution)/shard_map/ppermute | solution.py:407
  97.4 9.0 %collective-permute-done.8.rest_1_ = bf16[4,3,144,128]{3,2,1,0:T(8,128)(2,1)S(1)} collective-permute-done((bf16[4,3,144,128]{3,2,1,0:T(8,128)(2,1)S(1)}, bf16[4,3,144,128]{3,2,1,0:T(8,128)(2,1)S(1)}, u32[]{:S(2)}, u32[]{:S(2)}) %collective-permute-start.8) | collective-permute-done | bytes 442400 | tf_op jit(solution)/shard_map/ppermute | solution.py:381
  107.7 53.7 %block_terms.1 = (f32[1024,256]{1,0:T(8,128)}, f32[1024,256]{1,0:T(8,128)}, f32[1024,256]{1,0:T(8,128)}, f32[2,128,256]{2,1,0:T(8,128)}) custom-call(s32[16]{0:T(128)} %concatenate.15.sp, bf16[4,128,2304]{2,1,0:T(8,128)(2,1)} %bitcast.32, bf16[4,128,2304]{2,1,0:T(8,128)(2,1)} %copy-done, bf16[16,2304]{1,0:T(8,128)(2,1)} %copy-done.14, ...), custom_call_target="tpu_custom_call" | custom-call | tf_op jit(solution)/shard_map/block_terms/pallas_call | solution.py:283
  161.4 3.1 %collective-permute-start.18 = (f32[2,128,256]{2,1,0:T(8,128)}, f32[2,128,256]{2,1,0:T(8,128)S(1)}, u32[]{:S(2)}, u32[]{:S(2)}) collective-permute-start(f32[2,128,256]{2,1,0:T(8,128)} %get-tuple-element.9), channel_id=1, source_target_pairs={{0,64},{32,96},{1,65},{33,97},{2,66},{34,98},{3,67},{35,99},{4,68}... | collective-permute-start | bytes 786440 | tf_op jit(solution)/shard_map/ppermute | solution.py:428
  164.4 2.1 %collective-permute-start.17 = (f32[2,128,256]{2,1,0:T(8,128)}, f32[2,128,256]{2,1,0:T(8,128)S(1)}, u32[]{:S(2)}, u32[]{:S(2)}) collective-permute-start(f32[2,128,256]{2,1,0:T(8,128)} %get-tuple-element.9), channel_id=1, source_target_pairs={{0,32},{32,64},{64,96},{1,33},{33,65},{65,97},{2,34},{34,66},{66,9... | collective-permute-start | bytes 786440 | tf_op jit(solution)/shard_map/ppermute | solution.py:427
  166.6 1.0 slice.43
  167.5 1.3 collective-permute-start.19
  168.8 1.9 collective-permute-done.19.far
  171.6 5.1 %finish.1 = bf16[1024,256]{1,0:T(8,128)(2,1)} custom-call(f32[2,128,256]{2,1,0:T(8,128)} %copy-done.9, f32[2,128,256]{2,1,0:T(8,128)} %copy-done.8, f32[2,128,128]{2,1,0:T(8,128)} %copy-done.10, f32[1024,256]{1,0:T(8,128)} %get-tuple-element.10.qeff, f32[1024,256]{1,0:T(8,128)} %get-tuple-element.11.core, f32[1024,256]{1,0:T(8,128)} %get-tuple-element.12.gate, ...), custom_call_target="tpu_custom_call" | custom-call | tf_op jit(solution)/shard_map/finish/pallas_call | solution.py:340
  176.7 27.6 %all_to_all.5 = bf16[8,128,256]{2,1,0:T(8,128)(2,1)S(1)} all-to-all(bf16[8,128,256]{2,1,0:T(8,128)(2,1)} %bitcast.33), channel_id=1, replica_groups=mesh['z'=4,'x'=4,'c'=2,'y'=4] {'x','c'}, dimensions={0} | all-to-all | bytes 1048576 | tf_op jit(solution)/shard_map/all_to_all | solution.py:431
  204.3 0.8 copy.26
  (68 shorter events, 10.3 us)
Async XLA Ops:
  6.5 38.7 %all-gather.3.cloned.1.call-start = ((), (), s32[]{:S(2)}) async-start(), calls=%async_computation.1 | async-start | bytes 2949120 | tf_op jit(solution)/shard_map/all_gather | solution.py:403
  45.2 45.8 %collective-permute-start = (bf16[4,128,2304]{2,1,0:T(8,128)(2,1)}, bf16[4,128,2304]{2,1,0:T(8,128)(2,1)S(1)}, u32[]{:S(2)}, u32[]{:S(2)}) collective-permute-start(bf16[4,128,2304]{2,1,0:T(8,128)(2,1)} %bitcast.30), channel_id=1, source_target_pairs={{0,4},{4,0},{1,5},{5,1},{2,6},{6,2},{3,7},{7,3},{8,12},{12,8},{9,1... | collective-permute-start | bytes 7077896 | tf_op jit(solution)/shard_map/ppermute | solution.py:405
  47.4 10.5 %collective-permute-start.4 = (bf16[288,128]{1,0:T(8,128)(2,1)S(1)}, bf16[288,128]{1,0:T(8,128)(2,1)S(1)}, u32[]{:S(2)}, u32[]{:S(2)}) collective-permute-start(bf16[288,128]{1,0:T(8,128)(2,1)S(1)} %pad_maximum_fusion.5), channel_id=1, source_target_pairs={{0,64},{4,36},{8,8},{12,104},{16,76},{20,48},{24,20},{28,116},{32,... | collective-permute-start | bytes 221192 | tf_op jit(solution)/shard_map/ppermute | solution.py:377
  51.0 8.1 %collective-permute-start.2 = (bf16[288,128]{1,0:T(8,128)(2,1)S(1)}, bf16[288,128]{1,0:T(8,128)(2,1)S(1)}, u32[]{:S(2)}, u32[]{:S(2)}) collective-permute-start(bf16[288,128]{1,0:T(8,128)(2,1)S(1)} %pad_maximum_fusion.3), channel_id=1, source_target_pairs={{0,0},{4,96},{8,68},{12,40},{16,12},{20,108},{24,80},{28,52},{32,2... | collective-permute-start | bytes 221192 | tf_op jit(solution)/shard_map/ppermute | solution.py:377
  55.3 3.7 %collective-permute-start.3 = (bf16[288,128]{1,0:T(8,128)(2,1)S(1)}, bf16[288,128]{1,0:T(8,128)(2,1)S(1)}, u32[]{:S(2)}, u32[]{:S(2)}) collective-permute-start(bf16[288,128]{1,0:T(8,128)(2,1)S(1)} %pad_maximum_fusion.4), channel_id=1, source_target_pairs={{0,32},{4,4},{8,100},{12,72},{16,44},{20,16},{24,112},{28,84},{32,... | collective-permute-start | bytes 221192 | tf_op jit(solution)/shard_map/ppermute | solution.py:377
  59.8 9.5 %collective-permute-start.6 = (bf16[3,144,128]{2,1,0:T(8,128)(2,1)S(1)}, bf16[3,144,128]{2,1,0:T(8,128)(2,1)S(1)}, u32[]{:S(2)}, u32[]{:S(2)}) collective-permute-start(bf16[3,144,128]{2,1,0:T(8,128)(2,1)S(1)} %get-tuple-element.22), channel_id=1, source_target_pairs={{0,64},{32,96},{64,0},{96,32},{1,65},{33,97},{65,1},{97,33},{2,66}... | collective-permute-start | bytes 331784 | tf_op jit(solution)/shard_map/ppermute | solution.py:381
  65.4 5.8 %collective-permute-start.5 = (bf16[3,144,128]{2,1,0:T(8,128)(2,1)S(1)}, bf16[3,144,128]{2,1,0:T(8,128)(2,1)S(1)}, u32[]{:S(2)}, u32[]{:S(2)}) collective-permute-start(bf16[3,144,128]{2,1,0:T(8,128)(2,1)S(1)} %get-tuple-element.22), channel_id=1, source_target_pairs={{0,32},{32,64},{64,96},{96,0},{1,33},{33,65},{65,97},{97,1},{2,34}... | collective-permute-start | bytes 331784 | tf_op jit(solution)/shard_map/ppermute | solution.py:381
  65.7 5.5 %collective-permute-start.7 = (bf16[3,144,128]{2,1,0:T(8,128)(2,1)S(1)}, bf16[3,144,128]{2,1,0:T(8,128)(2,1)S(1)}, u32[]{:S(2)}, u32[]{:S(2)}) collective-permute-start(bf16[3,144,128]{2,1,0:T(8,128)(2,1)S(1)} %get-tuple-element.22), channel_id=1, source_target_pairs={{0,96},{32,0},{64,32},{96,64},{1,97},{33,1},{65,33},{97,65},{2,98}... | collective-permute-start | bytes 331784 | tf_op jit(solution)/shard_map/ppermute | solution.py:381
  69.4 1.8 copy-start.11
  73.0 33.4 %copy-start.1 = (bf16[4,3,144,128]{3,2,1,0:T(8,128)(2,1)}, bf16[4,3,144,128]{3,2,1,0:T(8,128)(2,1)S(1)}, u32[]{:S(2)}) copy-start(bf16[4,3,144,128]{3,2,1,0:T(8,128)(2,1)S(1)} %pad_maximum_fusion.rest_0_) | copy-start | bytes 1327108
  73.0 23.8 %copy-start.15 = (f32[16]{0:T(128)S(1)}, f32[16]{0:T(128)}, u32[]{:S(2)}) copy-start(f32[16]{0:T(128)} %param.22) | copy-start | bytes 196
  73.0 15.4 %collective-permute-start.10 = (bf16[4,3,144,128]{3,2,1,0:T(8,128)(2,1)S(1)}, bf16[4,3,144,128]{3,2,1,0:T(8,128)(2,1)}, u32[]{:S(2)}, u32[]{:S(2)}) collective-permute-start(bf16[4,3,144,128]{3,2,1,0:T(8,128)(2,1)S(1)} %pad_maximum_fusion.rest_0_), channel_id=1, source_target_pairs={{0,3},{1,0},{2,1},{3,2},{4,7},{5,4},{6,5},{7,6},{8,11},{9,8},{10,9... | collective-permute-start | bytes 1327112 | tf_op jit(solution)/shard_map/ppermute | solution.py:381
  78.3 5.4 %collective-permute-start.12 = (bf16[3,144,128]{2,1,0:T(8,128)(2,1)}, bf16[3,144,128]{2,1,0:T(8,128)(2,1)S(1)}, u32[]{:S(2)}, u32[]{:S(2)}) collective-permute-start(bf16[3,144,128]{2,1,0:T(8,128)(2,1)} %get-tuple-element.21), channel_id=1, source_target_pairs={{0,2},{1,3},{2,0},{3,1},{4,6},{5,7},{6,4},{7,5},{8,10},{9,11},{10,... | collective-permute-start | bytes 331784 | tf_op jit(solution)/shard_map/ppermute | solution.py:381
  78.9 6.0 %collective-permute-start.11 = (bf16[3,144,128]{2,1,0:T(8,128)(2,1)}, bf16[3,144,128]{2,1,0:T(8,128)(2,1)S(1)}, u32[]{:S(2)}, u32[]{:S(2)}) collective-permute-start(bf16[3,144,128]{2,1,0:T(8,128)(2,1)} %get-tuple-element.21), channel_id=1, source_target_pairs={{0,1},{1,2},{2,3},{3,0},{4,5},{5,6},{6,7},{7,4},{8,9},{9,10},{10,1... | collective-permute-start | bytes 331784 | tf_op jit(solution)/shard_map/ppermute | solution.py:381
  79.5 7.8 %collective-permute-start.13 = (bf16[3,144,128]{2,1,0:T(8,128)(2,1)}, bf16[3,144,128]{2,1,0:T(8,128)(2,1)S(1)}, u32[]{:S(2)}, u32[]{:S(2)}) collective-permute-start(bf16[3,144,128]{2,1,0:T(8,128)(2,1)} %get-tuple-element.21), channel_id=1, source_target_pairs={{0,3},{1,0},{2,1},{3,2},{4,7},{5,4},{6,5},{7,6},{8,11},{9,8},{10,9... | collective-permute-start | bytes 331784 | tf_op jit(solution)/shard_map/ppermute | solution.py:381
  83.8 10.1 %collective-permute-start.9 = (bf16[4,3,144,128]{3,2,1,0:T(8,128)(2,1)S(1)}, bf16[4,3,144,128]{3,2,1,0:T(8,128)(2,1)S(1)}, u32[]{:S(2)}, u32[]{:S(2)}) collective-permute-start(bf16[4,3,144,128]{3,2,1,0:T(8,128)(2,1)S(1)} %pad_maximum_fusion.rest_0_), channel_id=1, source_target_pairs={{0,2},{1,3},{2,0},{3,1},{4,6},{5,7},{6,4},{7,5},{8,10},{9,11},{10,... | collective-permute-start | bytes 1327112 | tf_op jit(solution)/shard_map/ppermute | solution.py:381
  84.8 21.5 %collective-permute-start.8 = (bf16[4,3,144,128]{3,2,1,0:T(8,128)(2,1)S(1)}, bf16[4,3,144,128]{3,2,1,0:T(8,128)(2,1)S(1)}, u32[]{:S(2)}, u32[]{:S(2)}) collective-permute-start(bf16[4,3,144,128]{3,2,1,0:T(8,128)(2,1)S(1)} %pad_maximum_fusion.rest_0_), channel_id=1, source_target_pairs={{0,1},{1,2},{2,3},{3,0},{4,5},{5,6},{6,7},{7,4},{8,9},{9,10},{10,1... | collective-permute-start | bytes 1327112 | tf_op jit(solution)/shard_map/ppermute | solution.py:381
  87.3 19.1 %copy-start.2 = (bf16[4,3,144,128]{3,2,1,0:T(8,128)(2,1)}, bf16[4,3,144,128]{3,2,1,0:T(8,128)(2,1)S(1)}, u32[]{:S(2)}) copy-start(bf16[4,3,144,128]{3,2,1,0:T(8,128)(2,1)S(1)} %pad_maximum_fusion.1.rest_4_) | copy-start | bytes 1327108
  87.3 19.0 %collective-permute-start.16 = (bf16[4,3,144,128]{3,2,1,0:T(8,128)(2,1)S(1)}, bf16[4,3,144,128]{3,2,1,0:T(8,128)(2,1)S(1)}, u32[]{:S(2)}, u32[]{:S(2)}) collective-permute-start(bf16[4,3,144,128]{3,2,1,0:T(8,128)(2,1)S(1)} %pad_maximum_fusion.1.rest_4_), channel_id=1, source_target_pairs={{0,96},{32,0},{64,32},{96,64},{1,97},{33,1},{65,33},{97,65},{2,98}... | collective-permute-start | bytes 1327112 | tf_op jit(solution)/shard_map/ppermute | solution.py:381
  88.5 17.9 %collective-permute-start.15 = (bf16[4,3,144,128]{3,2,1,0:T(8,128)(2,1)S(1)}, bf16[4,3,144,128]{3,2,1,0:T(8,128)(2,1)S(1)}, u32[]{:S(2)}, u32[]{:S(2)}) collective-permute-start(bf16[4,3,144,128]{3,2,1,0:T(8,128)(2,1)S(1)} %pad_maximum_fusion.1.rest_4_), channel_id=1, source_target_pairs={{0,64},{32,96},{64,0},{96,32},{1,65},{33,97},{65,1},{97,33},{2,66}... | collective-permute-start | bytes 1327112 | tf_op jit(solution)/shard_map/ppermute | solution.py:381
  91.1 15.3 %copy-start = (bf16[4,128,2304]{2,1,0:T(8,128)(2,1)}, bf16[4,128,2304]{2,1,0:T(8,128)(2,1)S(1)}, u32[]{:S(2)}) copy-start(bf16[4,128,2304]{2,1,0:T(8,128)(2,1)S(1)} %collective-permute-done.oth) | copy-start | bytes 7077892
  91.1 15.3 %collective-permute-start.14 = (bf16[4,3,144,128]{3,2,1,0:T(8,128)(2,1)S(1)}, bf16[4,3,144,128]{3,2,1,0:T(8,128)(2,1)S(1)}, u32[]{:S(2)}, u32[]{:S(2)}) collective-permute-start(bf16[4,3,144,128]{3,2,1,0:T(8,128)(2,1)S(1)} %pad_maximum_fusion.1.rest_4_), channel_id=1, source_target_pairs={{0,32},{32,64},{64,96},{96,0},{1,33},{33,65},{65,97},{97,1},{2,34}... | collective-permute-start | bytes 1327112 | tf_op jit(solution)/shard_map/ppermute | solution.py:381
  93.9 12.6 %copy-start.3 = (bf16[4,3,144,128]{3,2,1,0:T(8,128)(2,1)}, bf16[4,3,144,128]{3,2,1,0:T(8,128)(2,1)S(1)}, u32[]{:S(2)}) copy-start(bf16[4,3,144,128]{3,2,1,0:T(8,128)(2,1)S(1)} %collective-permute-done.9.rest_2_) | copy-start | bytes 1327108
  93.9 12.5 %collective-permute-start.1 = (bf16[16,2304]{1,0:T(8,128)(2,1)S(1)}, bf16[16,2304]{1,0:T(8,128)(2,1)S(1)}, u32[]{:S(2)}, u32[]{:S(2)}) collective-permute-start(bf16[16,2304]{1,0:T(8,128)(2,1)S(1)} %fusion.2), channel_id=1, source_target_pairs={{0,32},{32,64},{64,96},{1,33},{33,65},{65,97},{2,34},{34,66},{66,9... | collective-permute-start | bytes 221192 | tf_op jit(solution)/shard_map/ppermute | solution.py:407
  106.3 0.8 copy-start.4
  106.3 0.9 copy-start.5
  106.3 1.1 copy-start.6
  106.4 1.3 copy-start.7
  106.4 1.3 copy-start.14
  161.4 9.4 %collective-permute-start.18 = (f32[2,128,256]{2,1,0:T(8,128)}, f32[2,128,256]{2,1,0:T(8,128)S(1)}, u32[]{:S(2)}, u32[]{:S(2)}) collective-permute-start(f32[2,128,256]{2,1,0:T(8,128)} %get-tuple-element.9), channel_id=1, source_target_pairs={{0,64},{32,96},{1,65},{33,97},{2,66},{34,98},{3,67},{35,99},{4,68}... | collective-permute-start | bytes 786440 | tf_op jit(solution)/shard_map/ppermute | solution.py:428
  164.4 6.4 %collective-permute-start.17 = (f32[2,128,256]{2,1,0:T(8,128)}, f32[2,128,256]{2,1,0:T(8,128)S(1)}, u32[]{:S(2)}, u32[]{:S(2)}) collective-permute-start(f32[2,128,256]{2,1,0:T(8,128)} %get-tuple-element.9), channel_id=1, source_target_pairs={{0,32},{32,64},{64,96},{1,33},{33,65},{65,97},{2,34},{34,66},{66,9... | collective-permute-start | bytes 786440 | tf_op jit(solution)/shard_map/ppermute | solution.py:427
  167.5 3.2 %collective-permute-start.19 = (f32[2,128,128]{2,1,0:T(8,128)S(1)}, f32[2,128,128]{2,1,0:T(8,128)S(1)}, u32[]{:S(2)}, u32[]{:S(2)}) collective-permute-start(f32[2,128,128]{2,1,0:T(8,128)S(1)} %slice.43), channel_id=1, source_target_pairs={{0,96},{1,97},{2,98},{3,99},{4,100},{5,101},{6,102},{7,103},{8,104... | collective-permute-start | bytes 393224 | tf_op jit(solution)/shard_map/ppermute | solution.py:429
  (5 other events, 3.4 us)
Sparse Core Ops, SparseCore 0:
  9.0 36.1 all-gather.2

commit v2 on v1

v2 whole, which is shorter than its diff:
```python
import functools

import jax
import jax.numpy as jnp
import numpy as np
from jax import lax
from jax.experimental import pallas as pl
from jax.experimental.pallas import tpu as pltpu
from jax.sharding import Mesh
from jax.sharding import PartitionSpec as P

H = 16
DK = 128
CONV = 4
D = 2304
HV = H * DK
BF = jnp.bfloat16
F32 = jnp.float32

NZ, NX, NC, NY = 4, 4, 2, 4
ROW = NX * NC
SHARD = 128
GROUP = ROW * SHARD
UNIT = 64
PACK = D // 2
HALF = PACK // 2
STEP = 2 * SHARD
VMEM_LIMIT = 56 * 1024 * 1024


def unit_plan():
    count = NZ * ROW
    units = 3 * HV // UNIT
    dest = {}
    for u in range(units):
        kind, rest = divmod(u, HV // UNIT)
        head, half = divmod(rest, 2)
        dest[u] = (((head % 2) * 2 + half) * ROW + head // 2, kind)
    left = {i: [3 * i, 3 * i + 1, 3 * i + 2] for i in range(count)}
    sends, routes = [], []
    arrival = np.zeros((count, 3), np.int32)
    for r in range(3):
        owner = {}

        def place(i, seen):
            for u in left[i]:
                d = dest[u][0]
                if d in seen:
                    continue
                seen.add(d)
                if d not in owner or place(owner[d][0], seen):
                    owner[d] = (i, u)
                    return True
            return False

        for i in range(count):
            assert place(i, set())
        table = np.zeros(count, np.int32)
        route = []
        for d, (i, u) in owner.items():
            table[i] = u - 3 * i
            arrival[d, dest[u][1]] = r
            route.append((i, d))
            left[i].remove(u)
        sends.append(table)
        routes.append(sorted(route))
    order = arrival.reshape(NZ, ROW, 3).transpose(1, 0, 2).reshape(ROW, NZ * 3)
    return sends, routes, order


SENDS, ROUTES, ORDER = unit_plan()


def ring(distance, size=4):
    return [(i, (i + distance) % size) for i in range(size)]


def ahead(distance, size=4):
    return [(i, i + distance) for i in range(size - distance)]


def split(x):
    high = x.astype(BF)
    return high, (x - high.astype(F32)).astype(BF)


def dot(a, b):
    return lax.dot_general(a, b, (((1,), (0,)), ((), ())), preferred_element_type=F32)


def dot_nt(a, b):
    return lax.dot_general(a, b, (((1,), (1,)), ((), ())), preferred_element_type=F32)


def mm3(a, b):
    ah, al = split(a)
    bh, bl = split(b)
    return dot(jnp.concatenate([ah, al, ah], axis=1), jnp.concatenate([bh, bh, bl], axis=0))


def mm3_nt(a, b):
    ah, al = split(a)
    bh, bl = split(b)
    return dot_nt(jnp.concatenate([ah, al, ah], axis=1), jnp.concatenate([bh, bh, bl], axis=1))


def sigmoid(x):
    return 1.0 / (1.0 + jnp.exp(-x))


def unit_lower_inverses(systems, rows, cols):
    eye = jnp.where(rows == cols, 1.0, 0.0)
    pair = (rows // 2) == (cols // 2)
    found = [eye - jnp.where(pair, a, 0.0) for a in systems]
    size = 2
    while size < SHARD:
        band = ((rows // (2 * size)) == (cols // (2 * size))) & ((rows // size) != (cols // size))
        low = [jnp.where(band, a, 0.0).astype(BF) for a in systems]
        near = [t.astype(BF) for t in found]
        half = [dot(t, a).astype(BF) for t, a in zip(near, low)]
        step = [dot(p, t) for p, t in zip(half, near)]
        found = [t - s for t, s in zip(found, step)]
        size *= 2
    near = [t.astype(BF) for t in found]
    parts = [jnp.concatenate(split(a), axis=1) for a in systems]
    rest = [
        eye - t.astype(F32) - dot(a, jnp.concatenate([t, t], axis=0)) for a, t in zip(parts, near)
    ]
    return [t.astype(F32) + dot(t, r.astype(BF)) for t, r in zip(near, rest)]


def fixed(shape):
    return pl.BlockSpec(shape, lambda i, s: (0,) * len(shape))


def by_group(shape, offset=0):
    return pl.BlockSpec(shape, lambda i, s: (0, s[2] + offset))


def by_step(columns):
    return pl.BlockSpec((STEP, columns), lambda i, s: (i, 0))


def params():
    return pltpu.CompilerParams(vmem_limit_bytes=VMEM_LIMIT)


def cost(flops, size):
    return pl.CostEstimate(flops=int(flops), bytes_accessed=int(size), transcendentals=0)


def gate_kernel(sp, tokens, wsmall, decay_up, gate_up, rate, scale, log_o, beta_o, gate_o):
    g = sp[2]
    small = dot(tokens[...], wsmall[...])
    decay_low = small[:, :128].astype(BF)
    gate_low = small[:, 128:256].astype(BF)
    beta_all = scale[...] * sigmoid(small[:, 256:])
    logdec = -rate[...] * sigmoid(dot(decay_low, decay_up[...]))
    gate_o[...] = sigmoid(dot(gate_low, gate_up[...]))
    rows = lax.broadcasted_iota(jnp.int32, (SHARD, SHARD), 0)
    cols = lax.broadcasted_iota(jnp.int32, (SHARD, SHARD), 1)
    ones_low = jnp.where(rows >= cols, 1.0, 0.0).astype(BF)
    ones_twice = jnp.concatenate([ones_low, ones_low], axis=1)
    high, low = split(logdec)
    for blk in range(STEP // SHARD):
        ts = slice(SHARD * blk, SHARD * blk + SHARD)
        log_o[ts] = dot(ones_twice, jnp.concatenate([high[ts], low[ts]], axis=0))
    lane = lax.broadcasted_iota(jnp.int32, (STEP, 128), 1)
    for h in range(2):
        mine = jnp.sum(jnp.where(lane == 2 * g + h, beta_all, 0.0), axis=1, keepdims=True)
        beta_o[:, DK * h : DK * h + DK] = jnp.broadcast_to(mine, (STEP, DK))


def run_gates(sp, tokens, wsmall, decay_up, gate_up, rate, scale):
    wide = jax.ShapeDtypeStruct((GROUP, 2 * DK), F32)
    return pl.pallas_call(
        gate_kernel,
        name="block_gates",
        out_shape=(wide, wide, wide),
        grid_spec=pltpu.PrefetchScalarGridSpec(
            num_scalar_prefetch=1,
            grid=(GROUP // STEP,),
            in_specs=[
                by_step(D),
                fixed((D, 384)),
                by_group((128, 256)),
                by_group((128, 256)),
                by_group((1, 256)),
                fixed((1, 128)),
            ],
            out_specs=[by_step(2 * DK)] * 3,
        ),
        compiler_params=params(),
        cost_estimate=cost(2e9, 1e7),
    )(sp, tokens, wsmall, decay_up, gate_up, rate, scale)


def active(mixed, cols, taps):
    total = taps[0:1] * mixed[5 : 5 + STEP, cols]
    for j in range(1, CONV):
        total = total + taps[j : j + 1] * mixed[5 + j : 5 + j + STEP, cols]
    return total * sigmoid(total)


def state_kernel(sp, tokens, halo, log_sums, betas, conv_k, conv_v, *rest):
    parts = rest[:8]
    down_o, solved_o, carry_o, wq_o, state_o = rest[8:13]
    abuf, bbuf, wbuf, mixed, state, sems = rest[13:]
    step = pl.program_id(0)
    z, y = sp[0], sp[1]

    @pl.when(step == 0)
    def _():
        copies = []
        for k in range(4):
            copies.append(
                pltpu.make_async_copy(parts[k], abuf.at[lax.rem(y - k + 4, 4)], sems.at[k])
            )
            copies.append(
                pltpu.make_async_copy(parts[4 + k], bbuf.at[lax.rem(z - k + 4, 4)], sems.at[4 + k])
            )
        for copy in copies:
            copy.start()
        for copy in copies:
            copy.wait()

        def place(row, kind, hp, first, second):
            target = wq_o if kind == 0 else wbuf
            cols = pl.ds((kind - 1 if kind else 0) * 256 + hp * 128, 128)
            target[pl.ds(row, HALF), cols] = jnp.concatenate(
                [first[:, :UNIT], second[:, :UNIT]], axis=1
            )
            target[pl.ds(row + PACK, HALF), cols] = jnp.concatenate(
                [first[:, UNIT:], second[:, UNIT:]], axis=1
            )

        for kind in range(3):
            for hp in range(2):
                pa, pb = [], []
                for half in range(2):
                    zz = 2 * hp + half
                    kz = lax.rem(z - zz + 4, 4)
                    plane = sp[3 + 3 * zz + kind]
                    pa.append(abuf[plane, kz])
                    pb.append(bbuf[zz, plane])
                place(0, kind, hp, *pa)
                place(HALF, kind, hp, *pb)
        before = dot(halo[...], wbuf[...]).astype(BF).astype(F32)
        mixed[0:8] = before[8:16]
        rr = lax.broadcasted_iota(jnp.int32, (DK, 2 * DK), 0)
        cc = lax.broadcasted_iota(jnp.int32, (DK, 2 * DK), 1)
        start = jnp.where(rr == cc, 1.0, 0.0)
        state[0] = start
        state[1] = start

    mixed[8:] = dot(tokens[...], wbuf[...]).astype(BF).astype(F32)
    keys = active(mixed, slice(0, 256), conv_k)
    values = active(mixed, slice(256, 512), conv_v)
    mixed[0:8] = mixed[STEP : STEP + 8]

    rows = lax.broadcasted_iota(jnp.int32, (SHARD, SHARD), 0)
    cols = lax.broadcasted_iota(jnp.int32, (SHARD, SHARD), 1)
    places = [
        (h, blk, slice(SHARD * blk, SHARD * blk + SHARD), slice(DK * h, DK * h + DK))
        for blk in range(STEP // SHARD)
        for h in range(2)
    ]
    systems, sides, ends, tails = [], [], [], []
    for h, blk, ts, hs in places:
        k, beta, log_sum = keys[ts, hs], betas[ts, hs], log_sums[ts, hs]
        k = k * lax.rsqrt(jnp.sum(k * k, axis=1, keepdims=True) + 1e-06)
        end = log_sum[SHARD - 1 : SHARD]
        k_up = k * jnp.exp(log_sum)
        k_down = k * jnp.exp(-log_sum)
        down_o[ts, hs] = k_down
        systems.append(jnp.where(rows > cols, mm3_nt(k_up, k_down), 0.0) * beta)
        sides.append(jnp.concatenate([k_up * beta, values[ts, hs] * beta], axis=1))
        ends.append((k * jnp.exp(end - log_sum)).T)
        tails.append(jnp.where(rows == cols, jnp.exp(end), 0.0))
    inverses = unit_lower_inverses(systems, rows, cols)
    solved = [mm3(t, r) for t, r in zip(inverses, sides)]
    moves = [mm3(e, s) for e, s in zip(ends, solved)]
    for (h, blk, ts, hs), tail, sol, move in zip(places, tails, solved, moves):
        solved_o[ts, 2 * DK * h : 2 * DK * h + 2 * DK] = sol
        carry = state[h]
        carry_o[ts, 2 * DK * h : 2 * DK * h + 2 * DK] = carry
        new = mm3(tail - move[:, :DK], carry)
        state[h, :, :DK] = new[:, :DK]
        state[h, :, DK:] = new[:, DK:] + move[:, DK:]

    @pl.when(step == pl.num_programs(0) - 1)
    def _():
        state_o[...] = state[...]


def run_state(sp, tokens, halo, log_sums, betas, conv, parts):
    return pl.pallas_call(
        state_kernel,
        name="block_state",
        out_shape=(
            jax.ShapeDtypeStruct((GROUP, 2 * DK), F32),
            jax.ShapeDtypeStruct((GROUP, 4 * DK), F32),
            jax.ShapeDtypeStruct((GROUP, 4 * DK), F32),
            jax.ShapeDtypeStruct((D, 2 * DK), BF),
            jax.ShapeDtypeStruct((2, DK, 2 * DK), F32),
        ),
        grid_spec=pltpu.PrefetchScalarGridSpec(
            num_scalar_prefetch=1,
            grid=(GROUP // STEP,),
            in_specs=[
                by_step(D),
                fixed((16, D)),
                by_step(2 * DK),
                by_step(2 * DK),
                by_group((CONV, 256), 8),
                by_group((CONV, 256), 16),
            ]
            + [pl.BlockSpec(memory_space=pl.ANY)] * 8,
            out_specs=[
                by_step(2 * DK),
                by_step(4 * DK),
                by_step(4 * DK),
                fixed((D, 2 * DK)),
                fixed((2, DK, 2 * DK)),
            ],
            scratch_shapes=[
                pltpu.VMEM((NY, NZ, HALF, 128), BF),
                pltpu.VMEM((NZ, 3, HALF, 128), BF),
                pltpu.VMEM((D, 512), BF),
                pltpu.VMEM((8 + STEP, 512), F32),
                pltpu.VMEM((2, DK, 2 * DK), F32),
                pltpu.SemaphoreType.DMA((8,)),
            ],
        ),
        compiler_params=params(),
        cost_estimate=cost(1e10, 2e7),
    )(sp, tokens, halo, log_sums, betas, conv, conv, *parts)


def query_kernel(
    sp, tokens, halo, wq, conv_q, log_sums, k_downs, solved, carries, qeff_o, core_o, mixed
):
    @pl.when(pl.program_id(0) == 0)
    def _():
        before = dot(halo[...], wq[...]).astype(BF).astype(F32)
        mixed[0:8] = before[8:16]

    mixed[8:] = dot(tokens[...], wq[...]).astype(BF).astype(F32)
    query = active(mixed, slice(0, 256), conv_q)
    mixed[0:8] = mixed[STEP : STEP + 8]
    rows = lax.broadcasted_iota(jnp.int32, (SHARD, SHARD), 0)
    cols = lax.broadcasted_iota(jnp.int32, (SHARD, SHARD), 1)
    for blk in range(STEP // SHARD):
        for h in range(2):
            ts = slice(SHARD * blk, SHARD * blk + SHARD)
            hs = slice(DK * h, DK * h + DK)
            both = slice(2 * DK * h, 2 * DK * h + 2 * DK)
            q = query[ts, hs]
            q = q * (lax.rsqrt(jnp.sum(q * q, axis=1, keepdims=True) + 1e-06) * DK**-0.5)
            q_up = q * jnp.exp(log_sums[ts, hs])
            attend = jnp.where(rows >= cols, mm3_nt(q_up, k_downs[ts, hs]), 0.0)
            within = mm3(attend, solved[ts, both])
            out = mm3(q_up - within[:, :DK], carries[ts, both])
            qeff_o[ts, hs] = out[:, :DK]
            core_o[ts, hs] = out[:, DK:] + within[:, DK:]


def run_queries(sp, tokens, halo, wq, conv, log_sums, k_downs, solved, carries):
    wide = jax.ShapeDtypeStruct((GROUP, 2 * DK), F32)
    return pl.pallas_call(
        query_kernel,
        name="block_query",
        out_shape=(wide, wide),
        grid_spec=pltpu.PrefetchScalarGridSpec(
            num_scalar_prefetch=1,
            grid=(GROUP // STEP,),
            in_specs=[
                by_step(D),
                fixed((16, D)),
                fixed((D, 2 * DK)),
                by_group((CONV, 256)),
                by_step(2 * DK),
                by_step(2 * DK),
                by_step(4 * DK),
                by_step(4 * DK),
            ],
            out_specs=[by_step(2 * DK)] * 2,
            scratch_shapes=[pltpu.VMEM((8 + STEP, 256), F32)],
        ),
        compiler_params=params(),
        cost_estimate=cost(5e9, 2e7),
    )(sp, tokens, halo, wq, conv, log_sums, k_downs, solved, carries)


def finish_kernel(near, middle, far, qeff, core, gate, gain, out, state):
    @pl.when(pl.program_id(0) == 0)
    def _():
        for h in range(2):
            carry = middle[h, :, DK:] + mm3(middle[h, :, :DK], far[h])
            state[h] = near[h, :, DK:] + mm3(near[h, :, :DK], carry)

    for h in range(2):
        hs = slice(DK * h, DK * h + DK)
        full = core[:, hs] + mm3(qeff[:, hs], state[h])
        scale = lax.rsqrt(jnp.mean(full * full, axis=1, keepdims=True) + 1e-06)
        out[:, hs] = (full * scale * gain[...] * gate[:, hs]).astype(BF)


def run_finish(near, middle, far, qeff, core, gate, gain):
    def whole(shape):
        return pl.BlockSpec(shape, lambda i: (0,) * len(shape))

    tile = pl.BlockSpec((256, 2 * DK), lambda i: (i, 0))
    return pl.pallas_call(
        finish_kernel,
        name="finish",
        out_shape=jax.ShapeDtypeStruct((GROUP, 2 * DK), BF),
        grid=(GROUP // 256,),
        in_specs=[
            whole((2, DK, 2 * DK)),
            whole((2, DK, 2 * DK)),
            whole((2, DK, DK)),
            tile,
            tile,
            tile,
            whole((1, DK)),
        ],
        out_specs=tile,
        scratch_shapes=[pltpu.VMEM((2, DK, DK), F32)],
        compiler_params=pltpu.CompilerParams(vmem_limit_bytes=VMEM_LIMIT),
    )(near, middle, far, qeff, core, gate, gain)


def gather_weights(weight, spot, y):
    sent = jnp.asarray(np.stack(SENDS))[jnp.minimum(y, 2), spot]
    units = [weight[:, UNIT * k : UNIT * k + UNIT] for k in range(3)]
    unit = jnp.where(sent == 0, units[0], jnp.where(sent == 1, units[1], units[2]))
    packed = jnp.concatenate([unit[:PACK], unit[PACK:]], axis=1)
    route = [(i * NY + r, d * NY + r) for r in range(3) for i, d in ROUTES[r]]
    mine = lax.ppermute(packed, ("z", "x", "c", "y"), route)
    from_planes = [[(i, (i + k) % NY) for i in range(3)] for k in range(4)]
    upper, lower = mine[:HALF], mine[HALF:]
    upper_z = jnp.stack([upper] + [lax.ppermute(upper, "z", ring(k)) for k in range(1, 4)])
    lower_y = jnp.stack([lower] + [lax.ppermute(lower, "y", from_planes[k]) for k in range(1, 4)])
    lower_y = jnp.stack(
        [
            lax.dynamic_index_in_dim(lower_y, lax.rem(y - plane + NY, NY), 0, keepdims=False)
            for plane in range(3)
        ]
    )
    upper_z, lower_y = lax.optimization_barrier((upper_z, lower_y))
    return (
        [upper_z]
        + [lax.ppermute(upper_z, "y", from_planes[k]) for k in range(1, 4)]
        + [lower_y]
        + [lax.ppermute(lower_y, "z", ring(k)) for k in range(1, 4)]
    )


def per_device(
    tokens,
    qkv_weight,
    conv_weight,
    decay_down,
    decay_up,
    decay_rate,
    beta_weight,
    beta_scale,
    gate_down,
    gate_up,
    norm_gain,
):
    z, x, c, y = (lax.axis_index(a) for a in ("z", "x", "c", "y"))
    g = x * NC + c
    row = lax.all_gather(tokens, ("x", "c"), axis=0, tiled=True)
    parts = gather_weights(qkv_weight, z * ROW + g, y)
    halo = lax.ppermute(row[GROUP - 16 :], "z", ahead(1))
    wsmall = jnp.concatenate(
        [decay_down, gate_down, jnp.pad(beta_weight, ((0, 0), (0, 128 - H)))], axis=1
    )
    sp = jnp.concatenate(
        [jnp.stack([z, y, g]).astype(jnp.int32), jnp.asarray(ORDER)[g].astype(jnp.int32)]
    )
    log_sums, betas, gate = run_gates(
        sp,
        row,
        wsmall,
        decay_up,
        gate_up,
        decay_rate.reshape(1, HV),
        jnp.pad(beta_scale, (0, 128 - H)).reshape(1, 128),
    )
    k_downs, solved, carries, wq, state = run_state(
        sp, row, halo, log_sums, betas, conv_weight, parts
    )
    near = lax.ppermute(state, "z", ahead(1))
    middle = lax.ppermute(state, "z", ahead(2))
    far = lax.ppermute(state[:, :, DK:], "z", ahead(3))
    qeff, core = run_queries(sp, row, halo, wq, conv_weight, log_sums, k_downs, solved, carries)
    out = run_finish(near, middle, far, qeff, core, gate, norm_gain.reshape(1, DK))
    out = lax.all_to_all(out.reshape(ROW, SHARD, 2 * DK), ("x", "c"), 0, 0)
    return out.transpose(1, 0, 2).reshape(SHARD, HV)


def solution(mesh):
    fine = Mesh(mesh.devices.reshape(NZ, NX, NC, NY), ("z", "x", "c", "y"))
    seq = ("z", "x", "c")
    in_specs = (P(("y",) + seq, None), P(None, seq)) + (P(),) * 9
    return jax.shard_map(
        per_device,
        mesh=fine,
        in_specs=in_specs,
        out_specs=P(("y",) + seq, None),
        check_vma=False,
    )
```

time: 215 us -> 164 us (0.76)
  waiting for transfers between devices: 58 us -> 20.9 us
  blocking collectives: 27.6 us -> 14.7 us
  starting transfers between devices: 38.5 us -> 49 us
  Pallas kernels: 58.8 us -> 51.4 us
  other arithmetic: 5.23 us -> 2.58 us
    all_gather x1, waiting for transfers between devices: 38 us -> 0.01 us  [per_device(): row = lax.all_gather(tokens, ('x', 'c'), axis=0, tiled=True)]
    all_to_all x1, blocking collectives: 27.6 us -> 14.7 us  [per_device(): out = lax.all_to_all(out.reshape(ROW, SHARD, 2 * DK), ('x', 'c'), 0, 0)]
    ppermute x17 -> x14, starting transfers between devices: 32 us -> 41.2 us  [the longest x3 17.8 us: gather_weights(): lax.ppermute(lower, 'y', from_planes[k])]
    pallas_call x1 -> x3, Pallas kernels: 53.7 us -> 46.4 us  [the longest x1 23.6 us: run_state(): pl.pallas_call(state_kernel, name='block_state', out_shape=(jax.ShapeDtyp...]
    ppermute x17 -> x14, waiting for transfers between devices: 17.2 us -> 20.2 us  [the longest x3 7.77 us: gather_weights(): lax.ppermute(lower_y, 'z', ring(k))]
    unnamed x39 -> x26, local copies, waits for them, and re-layouts: 4.63 us -> 2.77 us
  transfers between devices with their start and end apart: 21 -> 18, of which waited for: 10 -> 8; matrix products, arithmetic and copies ran while one was open for 6% -> 5% of each run, Pallas kernels for 0% -> 14%
where the time goes in v2:
time: 164 us; the launch traced here: 163 us
  Pallas kernels  51.4 us (31%)
  starting transfers between devices  49 us (30%)
  waiting for transfers between devices  20.9 us (13%)
  between operations  15 us (9%)
  blocking collectives  14.7 us (9%)
  local copies, waits for them, and re-layouts  9.34 us (6%)
  other arithmetic  2.58 us (2%)
    pallas_call x1, Pallas kernels, run_state(): pl.pallas_call(state_kernel, name='block_state', out_shape=(jax.ShapeDtyp...  23.6 us
    ppermute x3, starting transfers between devices, gather_weights(): lax.ppermute(lower, 'y', from_planes[k])  17.8 us
    all_to_all x1, blocking collectives, per_device(): out = lax.all_to_all(out.reshape(ROW, SHARD, 2 * DK), ('x', 'c'), 0, 0)  14.7 us
    pallas_call x1, Pallas kernels, run_queries(): pl.pallas_call(query_kernel, name='block_query', out_shape=(wide, wide),...  14.5 us
    ppermute x3, starting transfers between devices, gather_weights(): lax.ppermute(upper_z, 'y', from_planes[k])  9.49 us
    pallas_call x1, Pallas kernels, run_gates(): pl.pallas_call(gate_kernel, name='block_gates', out_shape=(wide, wide, wi...  8.24 us
    ppermute x3, waiting for transfers between devices, gather_weights(): lax.ppermute(lower_y, 'z', ring(k))  7.77 us
    ppermute x1, starting transfers between devices, gather_weights(): mine = lax.ppermute(packed, ('z', 'x', 'c', 'y'), route)  7.06 us
  transfers between devices with their start and end apart: 18, of which 8 were waited for; matrix products, arithmetic and copies ran while one was open for 5% of the time, Pallas kernels for 14%

profile of v2, /device:TPU:1, one launch (start us, length us, event | category | flops | bytes accessed | tf_op | source)
XLA Modules:
  0.0 163.1 jit_solution(8733392717484025117)
XLA Ops:
  7.3 1.3 dynamic_slice.17
  9.8 1.2 fusion.3
  12.3 7.1 %collective-permute-start.1 = (bf16[1152,128]{1,0:T(8,128)(2,1)S(1)}, bf16[1152,128]{1,0:T(8,128)(2,1)S(1)}, u32[]{:S(2)}, u32[]{:S(2)}) collective-permute-start(bf16[1152,128]{1,0:T(8,128)(2,1)S(1)} %pad_maximum_fusion.3), channel_id=1, source_target_pairs={{0,0},{4,96},{8,68},{12,40},{16,12},{20,108},{24,80},{28,52},{32,2... | collective-permute-start | bytes 884744 | tf_op jit(solution)/shard_map/ppermute | solution.py:440
  19.4 6.0 %collective-permute-done.1 = bf16[1152,128]{1,0:T(8,128)(2,1)S(1)} collective-permute-done((bf16[1152,128]{1,0:T(8,128)(2,1)S(1)}, bf16[1152,128]{1,0:T(8,128)(2,1)S(1)}, u32[]{:S(2)}, u32[]{:S(2)}) %collective-permute-start.1) | collective-permute-done | bytes 294944 | tf_op jit(solution)/shard_map/ppermute | solution.py:440
  25.5 14.6 %collective-permute-start.6 = (bf16[576,128]{1,0:T(8,128)(2,1)S(1)}, bf16[576,128]{1,0:T(8,128)(2,1)S(1)}, u32[]{:S(2)}, u32[]{:S(2)}) collective-permute-start(bf16[576,128]{1,0:T(8,128)(2,1)S(1)} %get-tuple-element.39), channel_id=1, source_target_pairs={{0,2},{1,3},{2,0},{4,6},{5,7},{6,4},{8,10},{9,11},{10,8},{12,14},{... | collective-permute-start | bytes 442376 | tf_op jit(solution)/shard_map/ppermute | solution.py:444
  40.2 1.3 collective-permute-start.5
  41.5 1.9 %collective-permute-start.7 = (bf16[576,128]{1,0:T(8,128)(2,1)S(1)}, bf16[576,128]{1,0:T(8,128)(2,1)S(1)}, u32[]{:S(2)}, u32[]{:S(2)}) collective-permute-start(bf16[576,128]{1,0:T(8,128)(2,1)S(1)} %get-tuple-element.39), channel_id=1, source_target_pairs={{0,3},{1,0},{2,1},{4,7},{5,4},{6,5},{8,11},{9,8},{10,9},{12,15},{1... | collective-permute-start | bytes 442376 | tf_op jit(solution)/shard_map/ppermute | solution.py:444
  43.5 1.0 collective-permute-start.2
  44.5 1.8 %collective-permute-start.4 = (bf16[576,128]{1,0:T(8,128)(2,1)S(1)}, bf16[576,128]{1,0:T(8,128)(2,1)S(1)}, u32[]{:S(2)}, u32[]{:S(2)}) collective-permute-start(bf16[576,128]{1,0:T(8,128)(2,1)S(1)} %get-tuple-element.40), channel_id=1, source_target_pairs={{0,96},{32,0},{64,32},{96,64},{1,97},{33,1},{65,33},{97,65},{2,98}... | collective-permute-start | bytes 442376 | tf_op jit(solution)/shard_map/ppermute | solution.py:443
  46.3 1.1 collective-permute-done.7
  47.6 1.5 collective-permute-done.3
  49.1 1.3 collective-permute-done.2
  50.4 1.0 collective-permute-done.4
  51.5 2.6 %collective-permute-start.13 = (bf16[3,576,128]{2,1,0:T(8,128)(2,1)S(1)}, bf16[3,576,128]{2,1,0:T(8,128)(2,1)}, u32[]{:S(2)}, u32[]{:S(2)}) collective-permute-start(bf16[3,576,128]{2,1,0:T(8,128)(2,1)S(1)} %pad_maximum_fusion.2.rest_4_), channel_id=1, source_target_pairs={{0,96},{32,0},{64,32},{96,64},{1,97},{33,1},{65,33},{97,65},{2,98}... | collective-permute-start | bytes 1327112 | tf_op jit(solution)/shard_map/ppermute | solution.py:456
  55.4 1.9 %collective-permute-start.10 = (bf16[4,576,128]{2,1,0:T(8,128)(2,1)S(1)}, bf16[4,576,128]{2,1,0:T(8,128)(2,1)S(1)}, u32[]{:S(2)}, u32[]{:S(2)}) collective-permute-start(bf16[4,576,128]{2,1,0:T(8,128)(2,1)S(1)} %pad_maximum_fusion.rest_0_), channel_id=1, source_target_pairs={{0,3},{1,0},{2,1},{4,7},{5,4},{6,5},{8,11},{9,8},{10,9},{12,15},{1... | collective-permute-start | bytes 1769480 | tf_op jit(solution)/shard_map/ppermute | solution.py:454
  57.4 5.5 %collective-permute-start.9 = (bf16[4,576,128]{2,1,0:T(8,128)(2,1)S(1)}, bf16[4,576,128]{2,1,0:T(8,128)(2,1)}, u32[]{:S(2)}, u32[]{:S(2)}) collective-permute-start(bf16[4,576,128]{2,1,0:T(8,128)(2,1)S(1)} %pad_maximum_fusion.rest_0_), channel_id=1, source_target_pairs={{0,2},{1,3},{2,0},{4,6},{5,7},{6,4},{8,10},{9,11},{10,8},{12,14},{... | collective-permute-start | bytes 1769480 | tf_op jit(solution)/shard_map/ppermute | solution.py:454
  62.8 2.1 %collective-permute-start.8 = (bf16[4,576,128]{2,1,0:T(8,128)(2,1)S(1)}, bf16[4,576,128]{2,1,0:T(8,128)(2,1)}, u32[]{:S(2)}, u32[]{:S(2)}) collective-permute-start(bf16[4,576,128]{2,1,0:T(8,128)(2,1)S(1)} %pad_maximum_fusion.rest_0_), channel_id=1, source_target_pairs={{0,1},{1,2},{2,3},{4,5},{5,6},{6,7},{8,9},{9,10},{10,11},{12,13},{... | collective-permute-start | bytes 1769480 | tf_op jit(solution)/shard_map/ppermute | solution.py:454
  65.9 6.8 %collective-permute-done.13.rest_7_ = bf16[3,576,128]{2,1,0:T(8,128)(2,1)} collective-permute-done((bf16[3,576,128]{2,1,0:T(8,128)(2,1)S(1)}, bf16[3,576,128]{2,1,0:T(8,128)(2,1)}, u32[]{:S(2)}, u32[]{:S(2)}) %collective-permute-start.13) | collective-permute-done | bytes 442400 | tf_op jit(solution)/shard_map/ppermute | solution.py:456
  72.6 1.5 fusion.1.wsmall
  74.2 0.9 slice.36
  75.1 1.3 collective-permute-start
  76.4 8.2 %block_gates.1 = (f32[1024,256]{1,0:T(8,128)}, f32[1024,256]{1,0:T(8,128)}, f32[1024,256]{1,0:T(8,128)}) custom-call(s32[15]{0:T(128)} %pad_add_fusion.sp, bf16[1024,2304]{1,0:T(8,128)(2,1)} %all-gather.2.cloned.1.call-done.tokens, bf16[2304,384]{1,0:T(8,128)(2,1)} %fusion.1.wsmall, bf16[128,2048]{1,0:T(8,128)(2,1)} %decay_up.1, bf16[128,2048]{1,0:T(8,128)(2,1)} %gate_up.1, ...), custom_call_target="tpu_custom_call" | custom-call | flops 2000000000 | bytes 10000000 | tf_op jit(solution)/shard_map/block_gates/pallas_call | solution.py:176
  84.7 1.0 collective-permute-done.11.rest_5_
  85.7 1.5 collective-permute-done.8.rest_1_
  87.8 23.6 %block_state.1 = (f32[1024,256]{1,0:T(8,128)}, f32[1024,512]{1,0:T(8,128)}, f32[1024,512]{1,0:T(8,128)}, bf16[2304,256]{1,0:T(8,128)(2,1)}, f32[2,128,256]{2,1,0:T(8,128)}) custom-call(s32[15]{0:T(128)} %pad_add_fusion.sp, bf16[1024,2304]{1,0:T(8,128)(2,1)} %all-gather.2.cloned.1.call-done.tokens, bf16[16,2304]{1,0:T(8,128)(2,1)} %copy-done.9, ...), custom_call_target="tpu_custom_call" | custom-call | flops 10000000000 | bytes 20000000 | tf_op jit(solution)/shard_map/block_state/pallas_call | solution.py:297
  111.4 0.9 slice.35
  112.3 5.1 %collective-permute-start.15 = (f32[2,128,256]{2,1,0:T(8,128)}, f32[2,128,256]{2,1,0:T(8,128)S(1)}, u32[]{:S(2)}, u32[]{:S(2)}) collective-permute-start(f32[2,128,256]{2,1,0:T(8,128)} %get-tuple-element.21), channel_id=1, source_target_pairs={{0,64},{32,96},{1,65},{33,97},{2,66},{34,98},{3,67},{35,99},{4,68}... | collective-permute-start | bytes 786440 | tf_op jit(solution)/shard_map/ppermute | solution.py:497
  117.4 1.3 collective-permute-start.14
  118.7 1.5 collective-permute-start.16
  120.2 14.5 %block_query.1 = (f32[1024,256]{1,0:T(8,128)}, f32[1024,256]{1,0:T(8,128)}) custom-call(s32[15]{0:T(128)} %pad_add_fusion.sp, bf16[1024,2304]{1,0:T(8,128)(2,1)} %all-gather.2.cloned.1.call-done.tokens, bf16[16,2304]{1,0:T(8,128)(2,1)} %copy-done.9, bf16[2304,256]{1,0:T(8,128)(2,1)} %get-tuple-element.22.wq, f32[4,6144]{1,0:T(4,128)} %conv_q.1, ...), custom_call_target="tpu_custom_call" | custom-call | flops 5000000000 | bytes 20000000 | tf_op jit(solution)/shard_map/block_query/pallas_call | solution.py:370
  135.6 5.1 %finish.1 = bf16[1024,256]{1,0:T(8,128)(2,1)} custom-call(f32[2,128,256]{2,1,0:T(8,128)} %copy-done.5, f32[2,128,256]{2,1,0:T(8,128)} %copy-done.4, f32[2,128,128]{2,1,0:T(8,128)} %copy-done.6, f32[1024,256]{1,0:T(8,128)} %get-tuple-element.26.qeff, f32[1024,256]{1,0:T(8,128)} %get-tuple-element.27.core, f32[1024,256]{1,0:T(8,128)} %get-tuple-element.28.gate, ...), custom_call_target="tpu_custom_call" | custom-call | tf_op jit(solution)/shard_map/finish/pallas_call | solution.py:414
  140.7 14.7 %all_to_all.5 = bf16[8,128,256]{2,1,0:T(8,128)(2,1)S(1)} all-to-all(bf16[8,128,256]{2,1,0:T(8,128)(2,1)} %bitcast.25), channel_id=1, replica_groups=mesh['z'=4,'x'=4,'c'=2,'y'=4] {'x','c'}, dimensions={0} | all-to-all | bytes 1048576 | tf_op jit(solution)/shard_map/all_to_all | solution.py:501
  (53 shorter events, 6.9 us)
Async XLA Ops:
  6.5 67.6 %all-gather.2.cloned.1.call-start = ((), (), s32[]{:S(2)}) async-start(), calls=%async_computation.1 | async-start | bytes 5308416 | tf_op jit(solution)/shard_map/all_gather | solution.py:475
  12.3 13.1 %collective-permute-start.1 = (bf16[1152,128]{1,0:T(8,128)(2,1)S(1)}, bf16[1152,128]{1,0:T(8,128)(2,1)S(1)}, u32[]{:S(2)}, u32[]{:S(2)}) collective-permute-start(bf16[1152,128]{1,0:T(8,128)(2,1)S(1)} %pad_maximum_fusion.3), channel_id=1, source_target_pairs={{0,0},{4,96},{8,68},{12,40},{16,12},{20,108},{24,80},{28,52},{32,2... | collective-permute-start | bytes 884744 | tf_op jit(solution)/shard_map/ppermute | solution.py:440
  25.5 19.0 %collective-permute-start.6 = (bf16[576,128]{1,0:T(8,128)(2,1)S(1)}, bf16[576,128]{1,0:T(8,128)(2,1)S(1)}, u32[]{:S(2)}, u32[]{:S(2)}) collective-permute-start(bf16[576,128]{1,0:T(8,128)(2,1)S(1)} %get-tuple-element.39), channel_id=1, source_target_pairs={{0,2},{1,3},{2,0},{4,6},{5,7},{6,4},{8,10},{9,11},{10,8},{12,14},{... | collective-permute-start | bytes 442376 | tf_op jit(solution)/shard_map/ppermute | solution.py:444
  40.2 6.1 %collective-permute-start.5 = (bf16[576,128]{1,0:T(8,128)(2,1)S(1)}, bf16[576,128]{1,0:T(8,128)(2,1)S(1)}, u32[]{:S(2)}, u32[]{:S(2)}) collective-permute-start(bf16[576,128]{1,0:T(8,128)(2,1)S(1)} %get-tuple-element.39), channel_id=1, source_target_pairs={{0,1},{1,2},{2,3},{4,5},{5,6},{6,7},{8,9},{9,10},{10,11},{12,13},{... | collective-permute-start | bytes 442376 | tf_op jit(solution)/shard_map/ppermute | solution.py:444
  41.5 5.9 %collective-permute-start.7 = (bf16[576,128]{1,0:T(8,128)(2,1)S(1)}, bf16[576,128]{1,0:T(8,128)(2,1)S(1)}, u32[]{:S(2)}, u32[]{:S(2)}) collective-permute-start(bf16[576,128]{1,0:T(8,128)(2,1)S(1)} %get-tuple-element.39), channel_id=1, source_target_pairs={{0,3},{1,0},{2,1},{4,7},{5,4},{6,5},{8,11},{9,8},{10,9},{12,15},{1... | collective-permute-start | bytes 442376 | tf_op jit(solution)/shard_map/ppermute | solution.py:444
  43.4 10.7 %copy-start.10 = (f32[16]{0:T(128)S(1)}, f32[16]{0:T(128)}, u32[]{:S(2)}) copy-start(f32[16]{0:T(128)} %param.20) | copy-start | bytes 196
  43.4 22.1 %copy-start.7 = (bf16[2304,16]{0,1:T(8,128)(2,1)S(1)}, bf16[2304,16]{0,1:T(8,128)(2,1)}, u32[]{:S(2)}) copy-start(bf16[2304,16]{0,1:T(8,128)(2,1)} %param.19) | copy-start | bytes 221188
  43.4 5.7 %collective-permute-start.3 = (bf16[576,128]{1,0:T(8,128)(2,1)S(1)}, bf16[576,128]{1,0:T(8,128)(2,1)S(1)}, u32[]{:S(2)}, u32[]{:S(2)}) collective-permute-start(bf16[576,128]{1,0:T(8,128)(2,1)S(1)} %get-tuple-element.40), channel_id=1, source_target_pairs={{0,64},{32,96},{64,0},{96,32},{1,65},{33,97},{65,1},{97,33},{2,66}... | collective-permute-start | bytes 442376 | tf_op jit(solution)/shard_map/ppermute | solution.py:443
  43.5 6.9 %collective-permute-start.2 = (bf16[576,128]{1,0:T(8,128)(2,1)S(1)}, bf16[576,128]{1,0:T(8,128)(2,1)S(1)}, u32[]{:S(2)}, u32[]{:S(2)}) collective-permute-start(bf16[576,128]{1,0:T(8,128)(2,1)S(1)} %get-tuple-element.40), channel_id=1, source_target_pairs={{0,32},{32,64},{64,96},{96,0},{1,33},{33,65},{65,97},{97,1},{2,34}... | collective-permute-start | bytes 442376 | tf_op jit(solution)/shard_map/ppermute | solution.py:443
  44.5 6.9 %collective-permute-start.4 = (bf16[576,128]{1,0:T(8,128)(2,1)S(1)}, bf16[576,128]{1,0:T(8,128)(2,1)S(1)}, u32[]{:S(2)}, u32[]{:S(2)}) collective-permute-start(bf16[576,128]{1,0:T(8,128)(2,1)S(1)} %get-tuple-element.40), channel_id=1, source_target_pairs={{0,96},{32,0},{64,32},{96,64},{1,97},{33,1},{65,33},{97,65},{2,98}... | collective-permute-start | bytes 442376 | tf_op jit(solution)/shard_map/ppermute | solution.py:443
  47.4 25.2 %copy-start = (bf16[2304,128]{1,0:T(8,128)(2,1)S(1)}, bf16[2304,128]{1,0:T(8,128)(2,1)}, u32[]{:S(2)}) copy-start(bf16[2304,128]{1,0:T(8,128)(2,1)} %param.21) | copy-start | bytes 1769476
  47.5 25.2 %copy-start.1 = (bf16[2304,128]{1,0:T(8,128)(2,1)S(1)}, bf16[2304,128]{1,0:T(8,128)(2,1)}, u32[]{:S(2)}) copy-start(bf16[2304,128]{1,0:T(8,128)(2,1)} %param.16) | copy-start | bytes 1769476
  47.6 26.6 %copy-start.3 = (bf16[3,576,128]{2,1,0:T(8,128)(2,1)}, bf16[3,576,128]{2,1,0:T(8,128)(2,1)S(1)}, u32[]{:S(2)}) copy-start(bf16[3,576,128]{2,1,0:T(8,128)(2,1)S(1)} %pad_maximum_fusion.2.rest_4_) | copy-start | bytes 1327108
  51.5 22.7 %copy-start.2 = (bf16[4,576,128]{2,1,0:T(8,128)(2,1)}, bf16[4,576,128]{2,1,0:T(8,128)(2,1)S(1)}, u32[]{:S(2)}) copy-start(bf16[4,576,128]{2,1,0:T(8,128)(2,1)S(1)} %pad_maximum_fusion.rest_0_) | copy-start | bytes 1769476
  51.5 21.1 %collective-permute-start.13 = (bf16[3,576,128]{2,1,0:T(8,128)(2,1)S(1)}, bf16[3,576,128]{2,1,0:T(8,128)(2,1)}, u32[]{:S(2)}, u32[]{:S(2)}) collective-permute-start(bf16[3,576,128]{2,1,0:T(8,128)(2,1)S(1)} %pad_maximum_fusion.2.rest_4_), channel_id=1, source_target_pairs={{0,96},{32,0},{64,32},{96,64},{1,97},{33,1},{65,33},{97,65},{2,98}... | collective-permute-start | bytes 1327112 | tf_op jit(solution)/shard_map/ppermute | solution.py:456
  55.4 19.6 %collective-permute-start.12 = (bf16[3,576,128]{2,1,0:T(8,128)(2,1)S(1)}, bf16[3,576,128]{2,1,0:T(8,128)(2,1)}, u32[]{:S(2)}, u32[]{:S(2)}) collective-permute-start(bf16[3,576,128]{2,1,0:T(8,128)(2,1)S(1)} %pad_maximum_fusion.2.rest_4_), channel_id=1, source_target_pairs={{0,64},{32,96},{64,0},{96,32},{1,65},{33,97},{65,1},{97,33},{2,66}... | collective-permute-start | bytes 1327112 | tf_op jit(solution)/shard_map/ppermute | solution.py:456
  55.4 30.2 %collective-permute-start.10 = (bf16[4,576,128]{2,1,0:T(8,128)(2,1)S(1)}, bf16[4,576,128]{2,1,0:T(8,128)(2,1)S(1)}, u32[]{:S(2)}, u32[]{:S(2)}) collective-permute-start(bf16[4,576,128]{2,1,0:T(8,128)(2,1)S(1)} %pad_maximum_fusion.rest_0_), channel_id=1, source_target_pairs={{0,3},{1,0},{2,1},{4,7},{5,4},{6,5},{8,11},{9,8},{10,9},{12,15},{1... | collective-permute-start | bytes 1769480 | tf_op jit(solution)/shard_map/ppermute | solution.py:454
  57.4 28.3 %collective-permute-start.9 = (bf16[4,576,128]{2,1,0:T(8,128)(2,1)S(1)}, bf16[4,576,128]{2,1,0:T(8,128)(2,1)}, u32[]{:S(2)}, u32[]{:S(2)}) collective-permute-start(bf16[4,576,128]{2,1,0:T(8,128)(2,1)S(1)} %pad_maximum_fusion.rest_0_), channel_id=1, source_target_pairs={{0,2},{1,3},{2,0},{4,6},{5,7},{6,4},{8,10},{9,11},{10,8},{12,14},{... | collective-permute-start | bytes 1769480 | tf_op jit(solution)/shard_map/ppermute | solution.py:454
  62.8 24.3 %collective-permute-start.8 = (bf16[4,576,128]{2,1,0:T(8,128)(2,1)S(1)}, bf16[4,576,128]{2,1,0:T(8,128)(2,1)}, u32[]{:S(2)}, u32[]{:S(2)}) collective-permute-start(bf16[4,576,128]{2,1,0:T(8,128)(2,1)S(1)} %pad_maximum_fusion.rest_0_), channel_id=1, source_target_pairs={{0,1},{1,2},{2,3},{4,5},{5,6},{6,7},{8,9},{9,10},{10,11},{12,13},{... | collective-permute-start | bytes 1769480 | tf_op jit(solution)/shard_map/ppermute | solution.py:454
  72.6 13.0 %collective-permute-start.11 = (bf16[3,576,128]{2,1,0:T(8,128)(2,1)S(1)}, bf16[3,576,128]{2,1,0:T(8,128)(2,1)}, u32[]{:S(2)}, u32[]{:S(2)}) collective-permute-start(bf16[3,576,128]{2,1,0:T(8,128)(2,1)S(1)} %pad_maximum_fusion.2.rest_4_), channel_id=1, source_target_pairs={{0,32},{32,64},{64,96},{96,0},{1,33},{33,65},{65,97},{97,1},{2,34}... | collective-permute-start | bytes 1327112 | tf_op jit(solution)/shard_map/ppermute | solution.py:456
  75.1 12.1 %collective-permute-start = (bf16[16,2304]{1,0:T(8,128)(2,1)S(1)}, bf16[16,2304]{1,0:T(8,128)(2,1)S(1)}, u32[]{:S(2)}, u32[]{:S(2)}) collective-permute-start(bf16[16,2304]{1,0:T(8,128)(2,1)S(1)} %slice.36), channel_id=1, source_target_pairs={{0,32},{32,64},{64,96},{1,33},{33,65},{65,97},{2,34},{34,66},{66,9... | collective-permute-start | bytes 221192 | tf_op jit(solution)/shard_map/ppermute | solution.py:477
  85.7 1.5 copy-start.8
  87.2 0.6 copy-start.9
  112.3 22.4 %collective-permute-start.15 = (f32[2,128,256]{2,1,0:T(8,128)}, f32[2,128,256]{2,1,0:T(8,128)S(1)}, u32[]{:S(2)}, u32[]{:S(2)}) collective-permute-start(f32[2,128,256]{2,1,0:T(8,128)} %get-tuple-element.21), channel_id=1, source_target_pairs={{0,64},{32,96},{1,65},{33,97},{2,66},{34,98},{3,67},{35,99},{4,68}... | collective-permute-start | bytes 786440 | tf_op jit(solution)/shard_map/ppermute | solution.py:497
  117.4 17.4 %collective-permute-start.14 = (f32[2,128,256]{2,1,0:T(8,128)}, f32[2,128,256]{2,1,0:T(8,128)S(1)}, u32[]{:S(2)}, u32[]{:S(2)}) collective-permute-start(f32[2,128,256]{2,1,0:T(8,128)} %get-tuple-element.21), channel_id=1, source_target_pairs={{0,32},{32,64},{64,96},{1,33},{33,65},{65,97},{2,34},{34,66},{66,9... | collective-permute-start | bytes 786440 | tf_op jit(solution)/shard_map/ppermute | solution.py:496
  118.7 16.0 %collective-permute-start.16 = (f32[2,128,128]{2,1,0:T(8,128)S(1)}, f32[2,128,128]{2,1,0:T(8,128)S(1)}, u32[]{:S(2)}, u32[]{:S(2)}) collective-permute-start(f32[2,128,128]{2,1,0:T(8,128)S(1)} %slice.35), channel_id=1, source_target_pairs={{0,96},{1,97},{2,98},{3,99},{4,100},{5,101},{6,102},{7,103},{8,104... | collective-permute-start | bytes 393224 | tf_op jit(solution)/shard_map/ppermute | solution.py:498
  134.7 0.7 copy-start.6
  134.8 0.7 copy-start.4
  134.8 0.8 copy-start.5
Sparse Core Ops, SparseCore 0:
  9.0 37.8 all-gather.1

commit v3 on v2

--- a/solution.py
+++ b/solution.py
@@ -1,4 +1,4 @@
-import functools
+import itertools
 
 import jax
 import jax.numpy as jnp
@@ -22,53 +22,40 @@
 SHARD = 128
 GROUP = ROW * SHARD
 UNIT = 64
-PACK = D // 2
-HALF = PACK // 2
+ROWS = D // 2
+PACK = ROWS // 2
 STEP = 2 * SHARD
 VMEM_LIMIT = 56 * 1024 * 1024
 
 
-def unit_plan():
-    count = NZ * ROW
-    units = 3 * HV // UNIT
-    dest = {}
-    for u in range(units):
-        kind, rest = divmod(u, HV // UNIT)
-        head, half = divmod(rest, 2)
-        dest[u] = (((head % 2) * 2 + half) * ROW + head // 2, kind)
-    left = {i: [3 * i, 3 * i + 1, 3 * i + 2] for i in range(count)}
-    sends, routes = [], []
-    arrival = np.zeros((count, 3), np.int32)
-    for r in range(3):
-        owner = {}
-
-        def place(i, seen):
-            for u in left[i]:
-                d = dest[u][0]
-                if d in seen:
-                    continue
-                seen.add(d)
-                if d not in owner or place(owner[d][0], seen):
-                    owner[d] = (i, u)
-                    return True
-            return False
-
-        for i in range(count):
-            assert place(i, set())
-        table = np.zeros(count, np.int32)
-        route = []
-        for d, (i, u) in owner.items():
-            table[i] = u - 3 * i
-            arrival[d, dest[u][1]] = r
-            route.append((i, d))
-            left[i].remove(u)
-        sends.append(table)
-        routes.append(sorted(route))
-    order = arrival.reshape(NZ, ROW, 3).transpose(1, 0, 2).reshape(ROW, NZ * 3)
-    return sends, routes, order
-
-
-SENDS, ROUTES, ORDER = unit_plan()
+def nearest(sources):
+    def way(order):
+        return sum(min((order[i] - sources[i] // ROW) % 4, (sources[i] // ROW - order[i]) % 4) for i in range(4))
+
+    return min(itertools.permutations(range(4)), key=way)
+
+
+def block_plan():
+    whole_route, half_route, tables = [], [], []
+    for group in range(ROW):
+        blocks = [(kind, hp, 16 * kind + 2 * group + hp) for kind in range(3) for hp in range(2)]
+        whole = [b for b in blocks if b[2] % 3 != 1]
+        halves = [b for b in blocks if b[2] % 3 == 1]
+        sources = [2 * (m // 3) + (m % 3) // 2 for _, _, m in whole]
+        order = nearest(sources)
+        at_z = [0] * 4
+        for place, source, (kind, hp, _) in zip(order, sources, whole):
+            whole_route.append((source, place * ROW + group))
+            at_z[place] = 2 * kind + hp
+        sources = [2 * (m // 3) + side for _, _, m in halves for side in range(2)]
+        order = nearest(sources)
+        for place, source in zip(order, sources):
+            half_route.append((source, place * ROW + group))
+        tables.append(at_z + [2 * kind + hp for kind, hp, _ in halves] + list(order))
+    return sorted(whole_route), sorted(half_route), np.asarray(tables, np.int32)
+
+
+WHOLE_ROUTE, HALF_ROUTE, TABLES = block_plan()
 
 
 def ring(distance, size=4):
@@ -141,6 +128,38 @@
     return pl.BlockSpec((STEP, columns), lambda i, s: (i, 0))
 
 
+def block_columns(block):
+    return pl.ds(pl.multiple_of(block * DK, DK), DK)
+
+
+def fetch_weights(sp, parts, halves, weights, sems):
+    z, mine = sp[0], lax.rem(sp[1], 2)
+    copies = []
+    for side in range(2):
+        rows = mine if side == 0 else 1 - mine
+        for k in range(NZ):
+            part = parts[NZ * side + k]
+            place = lax.rem(z - k + NZ, NZ)
+            top = pl.multiple_of(rows * ROWS, 128)
+            copies.append((part.at[pl.ds(0, ROWS)], weights.at[pl.ds(top, ROWS), block_columns(sp[3 + place])]))
+            copies.append((part.at[pl.ds(ROWS, PACK)], halves.at[rows, place]))
+    copies = [pltpu.make_async_copy(s, d, sems.at[i]) for i, (s, d) in enumerate(copies)]
+    for copy in copies:
+        copy.start()
+    for copy in copies:
+        copy.wait()
+    for rows in range(2):
+        for b in range(2):
+            pair = [halves[rows, sp[9 + 2 * b + side]] for side in range(2)]
+            cols = block_columns(sp[7 + b])
+            weights[pl.ds(ROWS * rows, PACK), cols] = jnp.concatenate(
+                [u[:, :UNIT] for u in pair], axis=1
+            )
+            weights[pl.ds(ROWS * rows + PACK, PACK), cols] = jnp.concatenate(
+                [u[:, UNIT:] for u in pair], axis=1
+            )
+
+
 def params():
     return pltpu.CompilerParams(vmem_limit_bytes=VMEM_LIMIT)
 
@@ -149,7 +168,9 @@
     return pl.CostEstimate(flops=int(flops), bytes_accessed=int(size), transcendentals=0)
 
 
-def gate_kernel(sp, tokens, wsmall, decay_up, gate_up, rate, scale, log_o, beta_o, gate_o):
+def gate_kernel(
+    sp, tokens, wsmall, decay_up, gate_up, rate, scale, log_o, beta_o, gate_o
+):
     g = sp[2]
     small = dot(tokens[...], wsmall[...])
     decay_low = small[:, :128].astype(BF)
@@ -205,47 +226,14 @@
 def state_kernel(sp, tokens, halo, log_sums, betas, conv_k, conv_v, *rest):
     parts = rest[:8]
     down_o, solved_o, carry_o, wq_o, state_o = rest[8:13]
-    abuf, bbuf, wbuf, mixed, state, sems = rest[13:]
+    halves, wbuf, mixed, state, sems = rest[13:]
     step = pl.program_id(0)
-    z, y = sp[0], sp[1]
 
     @pl.when(step == 0)
     def _():
-        copies = []
-        for k in range(4):
-            copies.append(
-                pltpu.make_async_copy(parts[k], abuf.at[lax.rem(y - k + 4, 4)], sems.at[k])
-            )
-            copies.append(
-                pltpu.make_async_copy(parts[4 + k], bbuf.at[lax.rem(z - k + 4, 4)], sems.at[4 + k])
-            )
-        for copy in copies:
-            copy.start()
-        for copy in copies:
-            copy.wait()
-
-        def place(row, kind, hp, first, second):
-            target = wq_o if kind == 0 else wbuf
-            cols = pl.ds((kind - 1 if kind else 0) * 256 + hp * 128, 128)
-            target[pl.ds(row, HALF), cols] = jnp.concatenate(
-                [first[:, :UNIT], second[:, :UNIT]], axis=1
-            )
-            target[pl.ds(row + PACK, HALF), cols] = jnp.concatenate(
-                [first[:, UNIT:], second[:, UNIT:]], axis=1
-            )
-
-        for kind in range(3):
-            for hp in range(2):
-                pa, pb = [], []
-                for half in range(2):
-                    zz = 2 * hp + half
-                    kz = lax.rem(z - zz + 4, 4)
-                    plane = sp[3 + 3 * zz + kind]
-                    pa.append(abuf[plane, kz])
-                    pb.append(bbuf[zz, plane])
-                place(0, kind, hp, *pa)
-                place(HALF, kind, hp, *pb)
-        before = dot(halo[...], wbuf[...]).astype(BF).astype(F32)
+        fetch_weights(sp, parts, halves, wbuf, sems)
+        wq_o[...] = wbuf[:, : 2 * DK]
+        before = dot(halo[...], wbuf[:, 2 * DK :]).astype(BF).astype(F32)
         mixed[0:8] = before[8:16]
         rr = lax.broadcasted_iota(jnp.int32, (DK, 2 * DK), 0)
         cc = lax.broadcasted_iota(jnp.int32, (DK, 2 * DK), 1)
@@ -253,7 +241,7 @@
         state[0] = start
         state[1] = start
 
-    mixed[8:] = dot(tokens[...], wbuf[...]).astype(BF).astype(F32)
+    mixed[8:] = dot(tokens[...], wbuf[:, 2 * DK :]).astype(BF).astype(F32)
     keys = active(mixed, slice(0, 256), conv_k)
     values = active(mixed, slice(256, 512), conv_v)
     mixed[0:8] = mixed[STEP : STEP + 8]
@@ -324,12 +312,11 @@
                 fixed((2, DK, 2 * DK)),
             ],
             scratch_shapes=[
-                pltpu.VMEM((NY, NZ, HALF, 128), BF),
-                pltpu.VMEM((NZ, 3, HALF, 128), BF),
-                pltpu.VMEM((D, 512), BF),
+                pltpu.VMEM((2, NZ, PACK, 128), BF),
+                pltpu.VMEM((D, 6 * DK), BF),
                 pltpu.VMEM((8 + STEP, 512), F32),
                 pltpu.VMEM((2, DK, 2 * DK), F32),
-                pltpu.SemaphoreType.DMA((8,)),
+                pltpu.SemaphoreType.DMA((16,)),
             ],
         ),
         compiler_params=params(),
@@ -431,30 +418,17 @@
     )(near, middle, far, qeff, core, gate, gain)
 
 
-def gather_weights(weight, spot, y):
-    sent = jnp.asarray(np.stack(SENDS))[jnp.minimum(y, 2), spot]
-    units = [weight[:, UNIT * k : UNIT * k + UNIT] for k in range(3)]
-    unit = jnp.where(sent == 0, units[0], jnp.where(sent == 1, units[1], units[2]))
-    packed = jnp.concatenate([unit[:PACK], unit[PACK:]], axis=1)
-    route = [(i * NY + r, d * NY + r) for r in range(3) for i, d in ROUTES[r]]
-    mine = lax.ppermute(packed, ("z", "x", "c", "y"), route)
-    from_planes = [[(i, (i + k) % NY) for i in range(3)] for k in range(4)]
-    upper, lower = mine[:HALF], mine[HALF:]
-    upper_z = jnp.stack([upper] + [lax.ppermute(upper, "z", ring(k)) for k in range(1, 4)])
-    lower_y = jnp.stack([lower] + [lax.ppermute(lower, "y", from_planes[k]) for k in range(1, 4)])
-    lower_y = jnp.stack(
-        [
-            lax.dynamic_index_in_dim(lower_y, lax.rem(y - plane + NY, NY), 0, keepdims=False)
-            for plane in range(3)
-        ]
+def gather_weights(weight, c, y):
+    rows = lax.dynamic_slice(weight, (ROWS * lax.rem(y, 2), 0), (ROWS, 3 * UNIT))
+    whole = jnp.where(c == 0, rows[:, : 2 * UNIT], rows[:, UNIT:])
+    half = jnp.where(c == 0, rows[:, 2 * UNIT :], rows[:, :UNIT])
+    half = jnp.concatenate([half[:PACK], half[PACK:]], axis=1)
+    seq = ("z", "x", "c")
+    mine = jnp.concatenate(
+        [lax.ppermute(whole, seq, WHOLE_ROUTE), lax.ppermute(half, seq, HALF_ROUTE)], axis=0
     )
-    upper_z, lower_y = lax.optimization_barrier((upper_z, lower_y))
-    return (
-        [upper_z]
-        + [lax.ppermute(upper_z, "y", from_planes[k]) for k in range(1, 4)]
-        + [lower_y]
-        + [lax.ppermute(lower_y, "z", ring(k)) for k in range(1, 4)]
-    )
+    near = [mine] + [lax.ppermute(mine, "z", ring(k)) for k in range(1, NZ)]
+    return near, [lax.ppermute(p, "y", ring(d)) for p, d in zip(near, (1, 3, 3, 1))]
 
 
 def per_device(
@@ -472,15 +446,14 @@
 ):
     z, x, c, y = (lax.axis_index(a) for a in ("z", "x", "c", "y"))
     g = x * NC + c
-    row = lax.all_gather(tokens, ("x", "c"), axis=0, tiled=True)
-    parts = gather_weights(qkv_weight, z * ROW + g, y)
-    halo = lax.ppermute(row[GROUP - 16 :], "z", ahead(1))
     wsmall = jnp.concatenate(
         [decay_down, gate_down, jnp.pad(beta_weight, ((0, 0), (0, 128 - H)))], axis=1
     )
-    sp = jnp.concatenate(
-        [jnp.stack([z, y, g]).astype(jnp.int32), jnp.asarray(ORDER)[g].astype(jnp.int32)]
-    )
+    sp = jnp.concatenate([jnp.stack([z, y, g]).astype(jnp.int32), jnp.asarray(TABLES)[g]])
+    scale = jnp.pad(beta_scale, (0, 128 - H)).reshape(1, 128)
+    row = lax.all_gather(tokens, ("x", "c"), axis=0, tiled=True)
+    near, far = gather_weights(qkv_weight, c, y)
+    halo = lax.ppermute(row[GROUP - 16 :], "z", ahead(1))
     log_sums, betas, gate = run_gates(
         sp,
         row,
@@ -488,16 +461,16 @@
         decay_up,
         gate_up,
         decay_rate.reshape(1, HV),
-        jnp.pad(beta_scale, (0, 128 - H)).reshape(1, 128),
+        scale,
     )
     k_downs, solved, carries, wq, state = run_state(
-        sp, row, halo, log_sums, betas, conv_weight, parts
+        sp, row, halo, log_sums, betas, conv_weight, near + far
     )
-    near = lax.ppermute(state, "z", ahead(1))
-    middle = lax.ppermute(state, "z", ahead(2))
-    far = lax.ppermute(state[:, :, DK:], "z", ahead(3))
+    first = lax.ppermute(state, "z", ahead(1))
+    second = lax.ppermute(state, "z", ahead(2))
+    third = lax.ppermute(state[:, :, DK:], "z", ahead(3))
     qeff, core = run_queries(sp, row, halo, wq, conv_weight, log_sums, k_downs, solved, carries)
-    out = run_finish(near, middle, far, qeff, core, gate, norm_gain.reshape(1, DK))
+    out = run_finish(first, second, third, qeff, core, gate, norm_gain.reshape(1, DK))
     out = lax.all_to_all(out.reshape(ROW, SHARD, 2 * DK), ("x", "c"), 0, 0)
     return out.transpose(1, 0, 2).reshape(SHARD, HV)
 

time: 164 us -> 150 us (0.915)
  starting transfers between devices: 49 us -> 43.1 us
  waiting for transfers between devices: 20.9 us -> 16.1 us
    ppermute x16 -> x12, starting transfers between devices: 47.7 us -> 40.3 us  [the longest x3 13.4 us: gather_weights(): near = [mine] + [lax.ppermute(mine, 'z', ring(k)) for k in range(1, NZ)]]
    ppermute x16 -> x12, waiting for transfers between devices: 20.2 us -> 15.4 us  [the longest x3 12.8 us: gather_weights(): near = [mine] + [lax.ppermute(mine, 'z', ring(k)) for k in range(1, NZ)]]
  transfers between devices with their start and end apart: 18 -> 14, of which waited for: 8 -> 4; matrix products, arithmetic and copies ran while one was open for 5% -> 5% of each run, Pallas kernels for 14% -> 15%
where the time goes in v3:
time: 150 us
  Pallas kernels  51 us (34%)
  starting transfers between devices  43.1 us (29%)
  waiting for transfers between devices  16.1 us (11%)
  blocking collectives  14.9 us (10%)
  between operations  13.7 us (9%)
  local copies, waits for them, and re-layouts  8.74 us (6%)
  other arithmetic  2.36 us (2%)
    pallas_call x1, Pallas kernels, run_state(): pl.pallas_call(state_kernel, name='block_state', out_shape=(jax.ShapeDtyp...  23.1 us
    all_to_all x1, blocking collectives, per_device(): out = lax.all_to_all(out.reshape(ROW, SHARD, 2 * DK), ('x', 'c'), 0, 0)  14.9 us
    pallas_call x1, Pallas kernels, run_queries(): pl.pallas_call(query_kernel, name='block_query', out_shape=(wide, wide),...  14.5 us
    ppermute x3, starting transfers between devices, gather_weights(): near = [mine] + [lax.ppermute(mine, 'z', ring(k)) for k in range(1, NZ)]  13.4 us
    ppermute x3, waiting for transfers between devices, gather_weights(): near = [mine] + [lax.ppermute(mine, 'z', ring(k)) for k in range(1, NZ)]  12.8 us
    ppermute x1, starting transfers between devices, gather_weights(): lax.ppermute(half, seq, HALF_ROUTE)  9.78 us
    pallas_call x1, Pallas kernels, run_gates(): pl.pallas_call(gate_kernel, name='block_gates', out_shape=(wide, wide, wi...  8.25 us
    ppermute x4, starting transfers between devices, gather_weights(): lax.ppermute(p, 'y', ring(d))  7.47 us
  transfers between devices with their start and end apart: 14, of which 4 were waited for; matrix products, arithmetic and copies ran while one was open for 5% of the time, Pallas kernels for 15%

profile of v3, /device:TPU:1, one launch (start us, length us, event | category | flops | bytes accessed | tf_op | source)
XLA Modules:
  0.0 149.8 jit_solution(1845080222192743721)
XLA Ops:
  6.5 0.7 all-gather.2.cloned.1.call-update
  7.3 1.1 fusion.3
  8.9 0.7 collective-permute-start.1
  9.6 1.0 constant_dynamic-slice_fusion.1
  11.3 9.8 %collective-permute-start.2 = (bf16[576,128]{1,0:T(8,128)(2,1)S(1)}, bf16[576,128]{1,0:T(8,128)(2,1)S(1)}, u32[]{:S(2)}, u32[]{:S(2)}) collective-permute-start(bf16[576,128]{1,0:T(8,128)(2,1)S(1)} %pad_maximum_fusion), channel_id=1, source_target_pairs={{0,0},{4,96},{8,8},{12,40},{16,12},{20,108},{24,20},{28,52},{32,24... | collective-permute-start | bytes 442376 | tf_op jit(solution)/shard_map/ppermute | solution.py:428
  21.1 2.0 %collective-permute-done.2 = bf16[576,128]{1,0:T(8,128)(2,1)S(1)} collective-permute-done((bf16[576,128]{1,0:T(8,128)(2,1)S(1)}, bf16[576,128]{1,0:T(8,128)(2,1)S(1)}, u32[]{:S(2)}, u32[]{:S(2)}) %collective-permute-start.2) | collective-permute-done | bytes 147488 | tf_op jit(solution)/shard_map/ppermute | solution.py:428
  23.2 8.4 %collective-permute-start.5 = (bf16[1728,128]{1,0:T(8,128)(2,1)S(1)}, bf16[1728,128]{1,0:T(8,128)(2,1)S(1)}, u32[]{:S(2)}, u32[]{:S(2)}) collective-permute-start(bf16[1728,128]{1,0:T(8,128)(2,1)S(1)} %constant_dynamic-update-slice_fusion.rest_0_), channel_id=1, source_target_pairs={{0,96},{32,0},{64,32},{96,64},{1,97},{33,1},{65,33},{97,65},{2,98}... | collective-permute-start | bytes 1327112 | tf_op jit(solution)/shard_map/ppermute | solution.py:430
  31.6 4.2 %collective-permute-start.4 = (bf16[1728,128]{1,0:T(8,128)(2,1)S(1)}, bf16[1728,128]{1,0:T(8,128)(2,1)S(1)}, u32[]{:S(2)}, u32[]{:S(2)}) collective-permute-start(bf16[1728,128]{1,0:T(8,128)(2,1)S(1)} %constant_dynamic-update-slice_fusion.rest_0_), channel_id=1, source_target_pairs={{0,64},{32,96},{64,0},{96,32},{1,65},{33,97},{65,1},{97,33},{2,66}... | collective-permute-start | bytes 1327112 | tf_op jit(solution)/shard_map/ppermute | solution.py:430
  35.8 0.8 collective-permute-start.3
  37.5 0.7 fusion.2
  38.2 0.6 pad_add_fusion.sp
  38.8 1.4 collective-permute-start.6
  40.2 10.8 %collective-permute-done.5.rest_3_ = bf16[1728,128]{1,0:T(8,128)(2,1)S(1)} collective-permute-done((bf16[1728,128]{1,0:T(8,128)(2,1)S(1)}, bf16[1728,128]{1,0:T(8,128)(2,1)S(1)}, u32[]{:S(2)}, u32[]{:S(2)}) %collective-permute-start.5) | collective-permute-done | bytes 442400 | tf_op jit(solution)/shard_map/ppermute | solution.py:430
  51.0 1.4 collective-permute-start.9
  52.4 1.7 %collective-permute-start.8 = (bf16[1728,128]{1,0:T(8,128)(2,1)S(1)}, bf16[1728,128]{1,0:T(8,128)(2,1)}, u32[]{:S(2)}, u32[]{:S(2)}) collective-permute-start(bf16[1728,128]{1,0:T(8,128)(2,1)S(1)} %collective-permute-done.4.rest_2_), channel_id=1, source_target_pairs={{0,3},{1,0},{2,1},{3,2},{4,7},{5,4},{6,5},{7,6},{8,11},{9,8},{10,9... | collective-permute-start | bytes 1327112 | tf_op jit(solution)/shard_map/ppermute | solution.py:431
  54.1 2.0 %collective-permute-done.3.rest_1_ = bf16[1728,128]{1,0:T(8,128)(2,1)} collective-permute-done((bf16[1728,128]{1,0:T(8,128)(2,1)S(1)}, bf16[1728,128]{1,0:T(8,128)(2,1)}, u32[]{:S(2)}, u32[]{:S(2)}) %collective-permute-start.3) | collective-permute-done | bytes 442400 | tf_op jit(solution)/shard_map/ppermute | solution.py:430
  56.0 3.0 %collective-permute-start.7 = (bf16[1728,128]{1,0:T(8,128)(2,1)}, bf16[1728,128]{1,0:T(8,128)(2,1)}, u32[]{:S(2)}, u32[]{:S(2)}) collective-permute-start(bf16[1728,128]{1,0:T(8,128)(2,1)} %collective-permute-done.3.rest_1_), channel_id=1, source_target_pairs={{0,3},{1,0},{2,1},{3,2},{4,7},{5,4},{6,5},{7,6},{8,11},{9,8},{10,9... | collective-permute-start | bytes 1327112 | tf_op jit(solution)/shard_map/ppermute | solution.py:431
  59.1 1.6 %fusion.1.wsmall = bf16[2304,384]{1,0:T(8,128)(2,1)} fusion(bf16[2304,16]{1,0:T(8,128)(2,1)S(1)} %copy.13, bf16[2304,128]{1,0:T(8,128)(2,1)S(1)} %copy-done, bf16[2304,128]{1,0:T(8,128)(2,1)S(1)} %copy-done.1), kind=kLoop, calls=%fused_computation.2 | loop fusion | flops 7077888 | bytes 3022848 | tf_op jit(solution)/shard_map/concatenate | solution.py:449
  60.6 0.9 slice.32
  61.5 2.8 %collective-permute-start = (bf16[16,2304]{1,0:T(8,128)(2,1)S(1)}, bf16[16,2304]{1,0:T(8,128)(2,1)S(1)}, u32[]{:S(2)}, u32[]{:S(2)}) collective-permute-start(bf16[16,2304]{1,0:T(8,128)(2,1)S(1)} %slice.32), channel_id=1, source_target_pairs={{0,32},{32,64},{64,96},{1,33},{33,65},{65,97},{2,34},{34,66},{66,9... | collective-permute-start | bytes 221192 | tf_op jit(solution)/shard_map/ppermute | solution.py:456
  64.4 8.2 %block_gates.1 = (f32[1024,256]{1,0:T(8,128)}, f32[1024,256]{1,0:T(8,128)}, f32[1024,256]{1,0:T(8,128)}) custom-call(s32[13]{0:T(128)} %pad_add_fusion.sp, bf16[1024,2304]{1,0:T(8,128)(2,1)} %all-gather.2.cloned.1.call-done.tokens, bf16[2304,384]{1,0:T(8,128)(2,1)} %fusion.1.wsmall, bf16[128,2048]{1,0:T(8,128)(2,1)} %decay_up.1, bf16[128,2048]{1,0:T(8,128)(2,1)} %gate_up.1, ...), custom_call_target="tpu_custom_call" | custom-call | flops 2000000000 | bytes 10000000 | tf_op jit(solution)/shard_map/block_gates/pallas_call | solution.py:197
  73.2 0.6 copy-done.9
  73.8 23.1 %block_state.1 = (f32[1024,256]{1,0:T(8,128)}, f32[1024,512]{1,0:T(8,128)}, f32[1024,512]{1,0:T(8,128)}, bf16[2304,256]{1,0:T(8,128)(2,1)}, f32[2,128,256]{2,1,0:T(8,128)}) custom-call(s32[13]{0:T(128)} %pad_add_fusion.sp, bf16[1024,2304]{1,0:T(8,128)(2,1)} %all-gather.2.cloned.1.call-done.tokens, bf16[16,2304]{1,0:T(8,128)(2,1)} %copy-done.9, ...), custom_call_target="tpu_custom_call" | custom-call | flops 10000000000 | bytes 20000000 | tf_op jit(solution)/shard_map/block_state/pallas_call | solution.py:285
  96.9 0.9 slice.31
  97.8 5.0 %collective-permute-start.11 = (f32[2,128,256]{2,1,0:T(8,128)}, f32[2,128,256]{2,1,0:T(8,128)S(1)}, u32[]{:S(2)}, u32[]{:S(2)}) collective-permute-start(f32[2,128,256]{2,1,0:T(8,128)} %get-tuple-element.17), channel_id=1, source_target_pairs={{0,64},{32,96},{1,65},{33,97},{2,66},{34,98},{3,67},{35,99},{4,68}... | collective-permute-start | bytes 786440 | tf_op jit(solution)/shard_map/ppermute | solution.py:470
  102.9 2.4 %collective-permute-start.10 = (f32[2,128,256]{2,1,0:T(8,128)}, f32[2,128,256]{2,1,0:T(8,128)S(1)}, u32[]{:S(2)}, u32[]{:S(2)}) collective-permute-start(f32[2,128,256]{2,1,0:T(8,128)} %get-tuple-element.17), channel_id=1, source_target_pairs={{0,32},{32,64},{64,96},{1,33},{33,65},{65,97},{2,34},{34,66},{66,9... | collective-permute-start | bytes 786440 | tf_op jit(solution)/shard_map/ppermute | solution.py:469
  105.3 1.5 collective-permute-start.12
  106.8 14.5 %block_query.1 = (f32[1024,256]{1,0:T(8,128)}, f32[1024,256]{1,0:T(8,128)}) custom-call(s32[13]{0:T(128)} %pad_add_fusion.sp, bf16[1024,2304]{1,0:T(8,128)(2,1)} %all-gather.2.cloned.1.call-done.tokens, bf16[16,2304]{1,0:T(8,128)(2,1)} %copy-done.9, bf16[2304,256]{1,0:T(8,128)(2,1)} %get-tuple-element.18.wq, f32[4,6144]{1,0:T(4,128)} %conv_q.1, ...), custom_call_target="tpu_custom_call" | custom-call | flops 5000000000 | bytes 20000000 | tf_op jit(solution)/shard_map/block_query/pallas_call | solution.py:357
  121.4 0.6 copy-done.5
  122.2 5.1 %finish.1 = bf16[1024,256]{1,0:T(8,128)(2,1)} custom-call(f32[2,128,256]{2,1,0:T(8,128)} %copy-done.3, f32[2,128,256]{2,1,0:T(8,128)} %copy-done.2, f32[2,128,128]{2,1,0:T(8,128)} %copy-done.5, f32[1024,256]{1,0:T(8,128)} %get-tuple-element.22.qeff, f32[1024,256]{1,0:T(8,128)} %get-tuple-element.23.core, f32[1024,256]{1,0:T(8,128)} %get-tuple-element.24.gate, ...), custom_call_target="tpu_custom_call" | custom-call | tf_op jit(solution)/shard_map/finish/pallas_call | solution.py:401
  127.2 14.9 %all_to_all.5 = bf16[8,128,256]{2,1,0:T(8,128)(2,1)S(1)} all-to-all(bf16[8,128,256]{2,1,0:T(8,128)(2,1)} %bitcast.13), channel_id=1, replica_groups=mesh['z'=4,'x'=4,'c'=2,'y'=4] {'x','c'}, dimensions={0} | all-to-all | bytes 1048576 | tf_op jit(solution)/shard_map/all_to_all | solution.py:474
  142.1 0.8 copy.21
  (44 shorter events, 2.8 us)
Async XLA Ops:
  6.5 54.1 %all-gather.2.cloned.1.call-start = ((), (), s32[]{:S(2)}) async-start(), calls=%async_computation.1 | async-start | bytes 5308416 | tf_op jit(solution)/shard_map/all_gather | solution.py:454
  8.9 12.2 %collective-permute-start.1 = (bf16[1152,128]{1,0:T(8,128)(2,1)S(1)}, bf16[1152,128]{1,0:T(8,128)(2,1)S(1)}, u32[]{:S(2)}, u32[]{:S(2)}) collective-permute-start(bf16[1152,128]{1,0:T(8,128)(2,1)S(1)} %broadcast_select_fusion.1), channel_id=1, source_target_pairs={{0,0},{4,4},{8,100},{12,8},{16,12},{20,16},{24,48},{28,20},{32,56}... | collective-permute-start | bytes 884744 | tf_op jit(solution)/shard_map/ppermute | solution.py:428
  9.5 27.1 %copy-start.6 = (bf16[2304,16]{0,1:T(8,128)(2,1)S(1)}, bf16[2304,16]{0,1:T(8,128)(2,1)}, u32[]{:S(2)}) copy-start(bf16[2304,16]{0,1:T(8,128)(2,1)} %param.18) | copy-start | bytes 221188
  10.6 26.3 %copy-start.10 = (f32[16]{0:T(128)S(1)}, f32[16]{0:T(128)}, u32[]{:S(2)}) copy-start(f32[16]{0:T(128)} %param.19) | copy-start | bytes 196
  10.6 48.4 %copy-start = (bf16[2304,128]{1,0:T(8,128)(2,1)S(1)}, bf16[2304,128]{1,0:T(8,128)(2,1)}, u32[]{:S(2)}) copy-start(bf16[2304,128]{1,0:T(8,128)(2,1)} %param.20) | copy-start | bytes 1769476
  10.6 48.4 %copy-start.1 = (bf16[2304,128]{1,0:T(8,128)(2,1)S(1)}, bf16[2304,128]{1,0:T(8,128)(2,1)}, u32[]{:S(2)}) copy-start(bf16[2304,128]{1,0:T(8,128)(2,1)} %param.15) | copy-start | bytes 1769476
  11.3 11.9 %collective-permute-start.2 = (bf16[576,128]{1,0:T(8,128)(2,1)S(1)}, bf16[576,128]{1,0:T(8,128)(2,1)S(1)}, u32[]{:S(2)}, u32[]{:S(2)}) collective-permute-start(bf16[576,128]{1,0:T(8,128)(2,1)S(1)} %pad_maximum_fusion), channel_id=1, source_target_pairs={{0,0},{4,96},{8,8},{12,40},{16,12},{20,108},{24,20},{28,52},{32,24... | collective-permute-start | bytes 442376 | tf_op jit(solution)/shard_map/ppermute | solution.py:428
  23.2 37.5 %copy-start.4 = (bf16[1728,128]{1,0:T(8,128)(2,1)}, bf16[1728,128]{1,0:T(8,128)(2,1)S(1)}, u32[]{:S(2)}) copy-start(bf16[1728,128]{1,0:T(8,128)(2,1)S(1)} %constant_dynamic-update-slice_fusion.rest_0_) | copy-start | bytes 1327108
  23.2 27.8 %collective-permute-start.5 = (bf16[1728,128]{1,0:T(8,128)(2,1)S(1)}, bf16[1728,128]{1,0:T(8,128)(2,1)S(1)}, u32[]{:S(2)}, u32[]{:S(2)}) collective-permute-start(bf16[1728,128]{1,0:T(8,128)(2,1)S(1)} %constant_dynamic-update-slice_fusion.rest_0_), channel_id=1, source_target_pairs={{0,96},{32,0},{64,32},{96,64},{1,97},{33,1},{65,33},{97,65},{2,98}... | collective-permute-start | bytes 1327112 | tf_op jit(solution)/shard_map/ppermute | solution.py:430
  31.6 20.8 %collective-permute-start.4 = (bf16[1728,128]{1,0:T(8,128)(2,1)S(1)}, bf16[1728,128]{1,0:T(8,128)(2,1)S(1)}, u32[]{:S(2)}, u32[]{:S(2)}) collective-permute-start(bf16[1728,128]{1,0:T(8,128)(2,1)S(1)} %constant_dynamic-update-slice_fusion.rest_0_), channel_id=1, source_target_pairs={{0,64},{32,96},{64,0},{96,32},{1,65},{33,97},{65,1},{97,33},{2,66}... | collective-permute-start | bytes 1327112 | tf_op jit(solution)/shard_map/ppermute | solution.py:430
  35.8 20.2 %collective-permute-start.3 = (bf16[1728,128]{1,0:T(8,128)(2,1)S(1)}, bf16[1728,128]{1,0:T(8,128)(2,1)}, u32[]{:S(2)}, u32[]{:S(2)}) collective-permute-start(bf16[1728,128]{1,0:T(8,128)(2,1)S(1)} %constant_dynamic-update-slice_fusion.rest_0_), channel_id=1, source_target_pairs={{0,32},{32,64},{64,96},{96,0},{1,33},{33,65},{65,97},{97,1},{2,34}... | collective-permute-start | bytes 1327112 | tf_op jit(solution)/shard_map/ppermute | solution.py:430
  38.8 33.8 %collective-permute-start.6 = (bf16[1728,128]{1,0:T(8,128)(2,1)S(1)}, bf16[1728,128]{1,0:T(8,128)(2,1)}, u32[]{:S(2)}, u32[]{:S(2)}) collective-permute-start(bf16[1728,128]{1,0:T(8,128)(2,1)S(1)} %constant_dynamic-update-slice_fusion.rest_0_), channel_id=1, source_target_pairs={{0,1},{1,2},{2,3},{3,0},{4,5},{5,6},{6,7},{7,4},{8,9},{9,10},{10,1... | collective-permute-start | bytes 1327112 | tf_op jit(solution)/shard_map/ppermute | solution.py:431
  51.0 21.6 %copy-start.7 = (bf16[1728,128]{1,0:T(8,128)(2,1)}, bf16[1728,128]{1,0:T(8,128)(2,1)S(1)}, u32[]{:S(2)}) copy-start(bf16[1728,128]{1,0:T(8,128)(2,1)S(1)} %collective-permute-done.5.rest_3_) | copy-start | bytes 1327108
  51.0 21.6 %collective-permute-start.9 = (bf16[1728,128]{1,0:T(8,128)(2,1)S(1)}, bf16[1728,128]{1,0:T(8,128)(2,1)}, u32[]{:S(2)}, u32[]{:S(2)}) collective-permute-start(bf16[1728,128]{1,0:T(8,128)(2,1)S(1)} %collective-permute-done.5.rest_3_), channel_id=1, source_target_pairs={{0,1},{1,2},{2,3},{3,0},{4,5},{5,6},{6,7},{7,4},{8,9},{9,10},{10,1... | collective-permute-start | bytes 1327112 | tf_op jit(solution)/shard_map/ppermute | solution.py:431
  52.4 20.2 %copy-start.8 = (bf16[1728,128]{1,0:T(8,128)(2,1)}, bf16[1728,128]{1,0:T(8,128)(2,1)S(1)}, u32[]{:S(2)}) copy-start(bf16[1728,128]{1,0:T(8,128)(2,1)S(1)} %collective-permute-done.4.rest_2_) | copy-start | bytes 1327108
  52.4 20.3 %collective-permute-start.8 = (bf16[1728,128]{1,0:T(8,128)(2,1)S(1)}, bf16[1728,128]{1,0:T(8,128)(2,1)}, u32[]{:S(2)}, u32[]{:S(2)}) collective-permute-start(bf16[1728,128]{1,0:T(8,128)(2,1)S(1)} %collective-permute-done.4.rest_2_), channel_id=1, source_target_pairs={{0,3},{1,0},{2,1},{3,2},{4,7},{5,4},{6,5},{7,6},{8,11},{9,8},{10,9... | collective-permute-start | bytes 1327112 | tf_op jit(solution)/shard_map/ppermute | solution.py:431
  56.0 17.1 %collective-permute-start.7 = (bf16[1728,128]{1,0:T(8,128)(2,1)}, bf16[1728,128]{1,0:T(8,128)(2,1)}, u32[]{:S(2)}, u32[]{:S(2)}) collective-permute-start(bf16[1728,128]{1,0:T(8,128)(2,1)} %collective-permute-done.3.rest_1_), channel_id=1, source_target_pairs={{0,3},{1,0},{2,1},{3,2},{4,7},{5,4},{6,5},{7,6},{8,11},{9,8},{10,9... | collective-permute-start | bytes 1327112 | tf_op jit(solution)/shard_map/ppermute | solution.py:431
  61.5 11.7 %collective-permute-start = (bf16[16,2304]{1,0:T(8,128)(2,1)S(1)}, bf16[16,2304]{1,0:T(8,128)(2,1)S(1)}, u32[]{:S(2)}, u32[]{:S(2)}) collective-permute-start(bf16[16,2304]{1,0:T(8,128)(2,1)S(1)} %slice.32), channel_id=1, source_target_pairs={{0,32},{32,64},{64,96},{1,33},{33,65},{65,97},{2,34},{34,66},{66,9... | collective-permute-start | bytes 221192 | tf_op jit(solution)/shard_map/ppermute | solution.py:456
  73.2 0.6 copy-start.9
  97.8 23.5 %collective-permute-start.11 = (f32[2,128,256]{2,1,0:T(8,128)}, f32[2,128,256]{2,1,0:T(8,128)S(1)}, u32[]{:S(2)}, u32[]{:S(2)}) collective-permute-start(f32[2,128,256]{2,1,0:T(8,128)} %get-tuple-element.17), channel_id=1, source_target_pairs={{0,64},{32,96},{1,65},{33,97},{2,66},{34,98},{3,67},{35,99},{4,68}... | collective-permute-start | bytes 786440 | tf_op jit(solution)/shard_map/ppermute | solution.py:470
  102.9 18.5 %collective-permute-start.10 = (f32[2,128,256]{2,1,0:T(8,128)}, f32[2,128,256]{2,1,0:T(8,128)S(1)}, u32[]{:S(2)}, u32[]{:S(2)}) collective-permute-start(f32[2,128,256]{2,1,0:T(8,128)} %get-tuple-element.17), channel_id=1, source_target_pairs={{0,32},{32,64},{64,96},{1,33},{33,65},{65,97},{2,34},{34,66},{66,9... | collective-permute-start | bytes 786440 | tf_op jit(solution)/shard_map/ppermute | solution.py:469
  105.3 16.0 %collective-permute-start.12 = (f32[2,128,128]{2,1,0:T(8,128)S(1)}, f32[2,128,128]{2,1,0:T(8,128)S(1)}, u32[]{:S(2)}, u32[]{:S(2)}) collective-permute-start(f32[2,128,128]{2,1,0:T(8,128)S(1)} %slice.31), channel_id=1, source_target_pairs={{0,96},{1,97},{2,98},{3,99},{4,100},{5,101},{6,102},{7,103},{8,104... | collective-permute-start | bytes 393224 | tf_op jit(solution)/shard_map/ppermute | solution.py:471
  121.3 0.6 copy-start.5
  121.4 0.7 copy-start.2
  121.4 0.8 copy-start.3
Sparse Core Ops, SparseCore 0:
  9.0 37.8 all-gather.1

commit v4 on v3

--- a/solution.py
+++ b/solution.py
@@ -24,7 +24,7 @@
 UNIT = 64
 ROWS = D // 2
 PACK = ROWS // 2
-STEP = 2 * SHARD
+STEP = 4 * SHARD
 VMEM_LIMIT = 56 * 1024 * 1024
 
 
@@ -225,8 +225,8 @@
 
 def state_kernel(sp, tokens, halo, log_sums, betas, conv_k, conv_v, *rest):
     parts = rest[:8]
-    down_o, solved_o, carry_o, wq_o, state_o = rest[8:13]
-    halves, wbuf, mixed, state, sems = rest[13:]
+    down_o, solved_o, carry_o, wq_o, state_o, offset_o = rest[8:14]
+    halves, wbuf, mixed, state, sems = rest[14:]
     step = pl.program_id(0)
 
     @pl.when(step == 0)
@@ -279,6 +279,7 @@
     @pl.when(step == pl.num_programs(0) - 1)
     def _():
         state_o[...] = state[...]
+        offset_o[...] = state[:, :, DK:]
 
 
 def run_state(sp, tokens, halo, log_sums, betas, conv, parts):
@@ -291,6 +292,7 @@
             jax.ShapeDtypeStruct((GROUP, 4 * DK), F32),
             jax.ShapeDtypeStruct((D, 2 * DK), BF),
             jax.ShapeDtypeStruct((2, DK, 2 * DK), F32),
+            jax.ShapeDtypeStruct((2, DK, DK), F32),
         ),
         grid_spec=pltpu.PrefetchScalarGridSpec(
             num_scalar_prefetch=1,
@@ -310,6 +312,7 @@
                 by_step(4 * DK),
                 fixed((D, 2 * DK)),
                 fixed((2, DK, 2 * DK)),
+                fixed((2, DK, DK)),
             ],
             scratch_shapes=[
                 pltpu.VMEM((2, NZ, PACK, 128), BF),
@@ -337,19 +340,29 @@
     mixed[0:8] = mixed[STEP : STEP + 8]
     rows = lax.broadcasted_iota(jnp.int32, (SHARD, SHARD), 0)
     cols = lax.broadcasted_iota(jnp.int32, (SHARD, SHARD), 1)
-    for blk in range(STEP // SHARD):
-        for h in range(2):
-            ts = slice(SHARD * blk, SHARD * blk + SHARD)
-            hs = slice(DK * h, DK * h + DK)
-            both = slice(2 * DK * h, 2 * DK * h + 2 * DK)
-            q = query[ts, hs]
-            q = q * (lax.rsqrt(jnp.sum(q * q, axis=1, keepdims=True) + 1e-06) * DK**-0.5)
-            q_up = q * jnp.exp(log_sums[ts, hs])
-            attend = jnp.where(rows >= cols, mm3_nt(q_up, k_downs[ts, hs]), 0.0)
-            within = mm3(attend, solved[ts, both])
-            out = mm3(q_up - within[:, :DK], carries[ts, both])
-            qeff_o[ts, hs] = out[:, :DK]
-            core_o[ts, hs] = out[:, DK:] + within[:, DK:]
+    places = [
+        (
+            slice(SHARD * blk, SHARD * blk + SHARD),
+            slice(DK * h, DK * h + DK),
+            slice(2 * DK * h, 2 * DK * h + 2 * DK),
+        )
+        for blk in range(STEP // SHARD)
+        for h in range(2)
+    ]
+    ups = []
+    for ts, hs, _ in places:
+        q = query[ts, hs]
+        q = q * (lax.rsqrt(jnp.sum(q * q, axis=1, keepdims=True) + 1e-06) * DK**-0.5)
+        ups.append(q * jnp.exp(log_sums[ts, hs]))
+    scores = [mm3_nt(u, k_downs[ts, hs]) for u, (ts, hs, _) in zip(ups, places)]
+    attends = [jnp.where(rows >= cols, a, 0.0) for a in scores]
+    withins = [mm3(a, solved[ts, both]) for a, (ts, _, both) in zip(attends, places)]
+    outs = [
+        mm3(u - w[:, :DK], carries[ts, both]) for u, w, (ts, _, both) in zip(ups, withins, places)
+    ]
+    for out, w, (ts, hs, _) in zip(outs, withins, places):
+        qeff_o[ts, hs] = out[:, :DK]
+        core_o[ts, hs] = out[:, DK:] + w[:, DK:]
 
 
 def run_queries(sp, tokens, halo, wq, conv, log_sums, k_downs, solved, carries):
@@ -380,15 +393,19 @@
 
 
 def finish_kernel(near, middle, far, qeff, core, gate, gain, out, state):
+    heads = range(2)
+
     @pl.when(pl.program_id(0) == 0)
     def _():
-        for h in range(2):
-            carry = middle[h, :, DK:] + mm3(middle[h, :, :DK], far[h])
-            state[h] = near[h, :, DK:] + mm3(near[h, :, :DK], carry)
-
-    for h in range(2):
-        hs = slice(DK * h, DK * h + DK)
-        full = core[:, hs] + mm3(qeff[:, hs], state[h])
+        carries = [middle[h, :, DK:] + mm3(middle[h, :, :DK], far[h]) for h in heads]
+        starts = [near[h, :, DK:] + mm3(near[h, :, :DK], carries[h]) for h in heads]
+        for h in heads:
+            state[h] = starts[h]
+
+    spans = [slice(DK * h, DK * h + DK) for h in heads]
+    added = [mm3(qeff[:, hs], state[h]) for h, hs in zip(heads, spans)]
+    for hs, more in zip(spans, added):
+        full = core[:, hs] + more
         scale = lax.rsqrt(jnp.mean(full * full, axis=1, keepdims=True) + 1e-06)
         out[:, hs] = (full * scale * gain[...] * gate[:, hs]).astype(BF)
 
@@ -397,12 +414,12 @@
     def whole(shape):
         return pl.BlockSpec(shape, lambda i: (0,) * len(shape))
 
-    tile = pl.BlockSpec((256, 2 * DK), lambda i: (i, 0))
+    tile = pl.BlockSpec((512, 2 * DK), lambda i: (i, 0))
     return pl.pallas_call(
         finish_kernel,
         name="finish",
         out_shape=jax.ShapeDtypeStruct((GROUP, 2 * DK), BF),
-        grid=(GROUP // 256,),
+        grid=(GROUP // 512,),
         in_specs=[
             whole((2, DK, 2 * DK)),
             whole((2, DK, 2 * DK)),
@@ -463,12 +480,12 @@
         decay_rate.reshape(1, HV),
         scale,
     )
-    k_downs, solved, carries, wq, state = run_state(
+    k_downs, solved, carries, wq, state, offset = run_state(
         sp, row, halo, log_sums, betas, conv_weight, near + far
     )
     first = lax.ppermute(state, "z", ahead(1))
     second = lax.ppermute(state, "z", ahead(2))
-    third = lax.ppermute(state[:, :, DK:], "z", ahead(3))
+    third = lax.ppermute(offset, "z", ahead(3))
     qeff, core = run_queries(sp, row, halo, wq, conv_weight, log_sums, k_downs, solved, carries)
     out = run_finish(first, second, third, qeff, core, gate, norm_gain.reshape(1, DK))
     out = lax.all_to_all(out.reshape(ROW, SHARD, 2 * DK), ("x", "c"), 0, 0)

time: 150 us -> 143 us (0.953)
  Pallas kernels: 51 us -> 43.6 us
    pallas_call x1, Pallas kernels: 23.1 us -> 20.5 us  [run_state(): pl.pallas_call(state_kernel, name='block_state', out_shape=(jax.ShapeDtyp...]
    pallas_call x1, Pallas kernels: 14.5 us -> 11.9 us  [run_queries(): pl.pallas_call(query_kernel, name='block_query', out_shape=(wide, wide),...]
  transfers between devices with their start and end apart: 14 -> 14, of which waited for: 4 -> 4; matrix products, arithmetic and copies ran while one was open for 5% -> 6% of each run, Pallas kernels for 15% -> 14%
where the time goes in v4:
time: 143 us; the launch traced here: 142 us
  Pallas kernels  43.6 us (30%)
  starting transfers between devices  43.1 us (30%)
  waiting for transfers between devices  16.8 us (12%)
  blocking collectives  14.8 us (10%)
  between operations  13.7 us (10%)
  local copies, waits for them, and re-layouts  7.8 us (5%)
  other arithmetic  2.36 us (2%)
    pallas_call x1, Pallas kernels, run_state(): pl.pallas_call(state_kernel, name='block_state', out_shape=(jax.ShapeDtyp...  20.5 us
    all_to_all x1, blocking collectives, per_device(): out = lax.all_to_all(out.reshape(ROW, SHARD, 2 * DK), ('x', 'c'), 0, 0)  14.8 us
    ppermute x3, starting transfers between devices, gather_weights(): near = [mine] + [lax.ppermute(mine, 'z', ring(k)) for k in range(1, NZ)]  13.4 us
    ppermute x3, waiting for transfers between devices, gather_weights(): near = [mine] + [lax.ppermute(mine, 'z', ring(k)) for k in range(1, NZ)]  12.8 us
    pallas_call x1, Pallas kernels, run_queries(): pl.pallas_call(query_kernel, name='block_query', out_shape=(wide, wide),...  11.9 us
    ppermute x1, starting transfers between devices, gather_weights(): lax.ppermute(half, seq, HALF_ROUTE)  9.78 us
    pallas_call x1, Pallas kernels, run_gates(): pl.pallas_call(gate_kernel, name='block_gates', out_shape=(wide, wide, wi...  7.5 us
    ppermute x4, starting transfers between devices, gather_weights(): lax.ppermute(p, 'y', ring(d))  7.47 us
  transfers between devices with their start and end apart: 14, of which 4 were waited for; matrix products, arithmetic and copies ran while one was open for 6% of the time, Pallas kernels for 14%

profile of v4, /device:TPU:1, one launch (start us, length us, event | category | flops | bytes accessed | tf_op | source)
XLA Modules:
  0.0 142.3 jit_solution(13994236947982304085)
XLA Ops:
  6.5 0.7 all-gather.2.cloned.1.call-update
  7.3 1.1 fusion.3
  8.9 0.7 collective-permute-start.1
  9.6 1.0 constant_dynamic-slice_fusion.1
  11.3 9.8 %collective-permute-start.2 = (bf16[576,128]{1,0:T(8,128)(2,1)S(1)}, bf16[576,128]{1,0:T(8,128)(2,1)S(1)}, u32[]{:S(2)}, u32[]{:S(2)}) collective-permute-start(bf16[576,128]{1,0:T(8,128)(2,1)S(1)} %pad_maximum_fusion), channel_id=1, source_target_pairs={{0,0},{4,96},{8,8},{12,40},{16,12},{20,108},{24,20},{28,52},{32,24... | collective-permute-start | bytes 442376 | tf_op jit(solution)/shard_map/ppermute | solution.py:445
  21.1 2.0 %collective-permute-done.2 = bf16[576,128]{1,0:T(8,128)(2,1)S(1)} collective-permute-done((bf16[576,128]{1,0:T(8,128)(2,1)S(1)}, bf16[576,128]{1,0:T(8,128)(2,1)S(1)}, u32[]{:S(2)}, u32[]{:S(2)}) %collective-permute-start.2) | collective-permute-done | bytes 147488 | tf_op jit(solution)/shard_map/ppermute | solution.py:445
  23.2 8.4 %collective-permute-start.5 = (bf16[1728,128]{1,0:T(8,128)(2,1)S(1)}, bf16[1728,128]{1,0:T(8,128)(2,1)S(1)}, u32[]{:S(2)}, u32[]{:S(2)}) collective-permute-start(bf16[1728,128]{1,0:T(8,128)(2,1)S(1)} %constant_dynamic-update-slice_fusion.rest_0_), channel_id=1, source_target_pairs={{0,96},{32,0},{64,32},{96,64},{1,97},{33,1},{65,33},{97,65},{2,98}... | collective-permute-start | bytes 1327112 | tf_op jit(solution)/shard_map/ppermute | solution.py:447
  31.6 4.2 %collective-permute-start.4 = (bf16[1728,128]{1,0:T(8,128)(2,1)S(1)}, bf16[1728,128]{1,0:T(8,128)(2,1)S(1)}, u32[]{:S(2)}, u32[]{:S(2)}) collective-permute-start(bf16[1728,128]{1,0:T(8,128)(2,1)S(1)} %constant_dynamic-update-slice_fusion.rest_0_), channel_id=1, source_target_pairs={{0,64},{32,96},{64,0},{96,32},{1,65},{33,97},{65,1},{97,33},{2,66}... | collective-permute-start | bytes 1327112 | tf_op jit(solution)/shard_map/ppermute | solution.py:447
  35.8 0.8 collective-permute-start.3
  37.5 0.7 fusion.2
  38.2 0.6 pad_add_fusion.sp
  38.8 1.4 collective-permute-start.6
  40.2 10.8 %collective-permute-done.5.rest_3_ = bf16[1728,128]{1,0:T(8,128)(2,1)S(1)} collective-permute-done((bf16[1728,128]{1,0:T(8,128)(2,1)S(1)}, bf16[1728,128]{1,0:T(8,128)(2,1)S(1)}, u32[]{:S(2)}, u32[]{:S(2)}) %collective-permute-start.5) | collective-permute-done | bytes 442400 | tf_op jit(solution)/shard_map/ppermute | solution.py:447
  51.0 1.4 collective-permute-start.9
  52.4 1.7 %collective-permute-start.8 = (bf16[1728,128]{1,0:T(8,128)(2,1)S(1)}, bf16[1728,128]{1,0:T(8,128)(2,1)}, u32[]{:S(2)}, u32[]{:S(2)}) collective-permute-start(bf16[1728,128]{1,0:T(8,128)(2,1)S(1)} %collective-permute-done.4.rest_2_), channel_id=1, source_target_pairs={{0,3},{1,0},{2,1},{3,2},{4,7},{5,4},{6,5},{7,6},{8,11},{9,8},{10,9... | collective-permute-start | bytes 1327112 | tf_op jit(solution)/shard_map/ppermute | solution.py:448
  54.1 2.0 %collective-permute-done.3.rest_1_ = bf16[1728,128]{1,0:T(8,128)(2,1)} collective-permute-done((bf16[1728,128]{1,0:T(8,128)(2,1)S(1)}, bf16[1728,128]{1,0:T(8,128)(2,1)}, u32[]{:S(2)}, u32[]{:S(2)}) %collective-permute-start.3) | collective-permute-done | bytes 442400 | tf_op jit(solution)/shard_map/ppermute | solution.py:447
  56.0 3.0 %collective-permute-start.7 = (bf16[1728,128]{1,0:T(8,128)(2,1)}, bf16[1728,128]{1,0:T(8,128)(2,1)}, u32[]{:S(2)}, u32[]{:S(2)}) collective-permute-start(bf16[1728,128]{1,0:T(8,128)(2,1)} %collective-permute-done.3.rest_1_), channel_id=1, source_target_pairs={{0,3},{1,0},{2,1},{3,2},{4,7},{5,4},{6,5},{7,6},{8,11},{9,8},{10,9... | collective-permute-start | bytes 1327112 | tf_op jit(solution)/shard_map/ppermute | solution.py:448
  59.1 1.6 %fusion.1.wsmall = bf16[2304,384]{1,0:T(8,128)(2,1)} fusion(bf16[2304,16]{1,0:T(8,128)(2,1)S(1)} %copy.13, bf16[2304,128]{1,0:T(8,128)(2,1)S(1)} %copy-done, bf16[2304,128]{1,0:T(8,128)(2,1)S(1)} %copy-done.1), kind=kLoop, calls=%fused_computation.2 | loop fusion | flops 7077888 | bytes 3022848 | tf_op jit(solution)/shard_map/concatenate | solution.py:466
  60.6 0.9 slice.28
  61.5 2.8 %collective-permute-start = (bf16[16,2304]{1,0:T(8,128)(2,1)S(1)}, bf16[16,2304]{1,0:T(8,128)(2,1)S(1)}, u32[]{:S(2)}, u32[]{:S(2)}) collective-permute-start(bf16[16,2304]{1,0:T(8,128)(2,1)S(1)} %slice.28), channel_id=1, source_target_pairs={{0,32},{32,64},{64,96},{1,33},{33,65},{65,97},{2,34},{34,66},{66,9... | collective-permute-start | bytes 221192 | tf_op jit(solution)/shard_map/ppermute | solution.py:473
  64.4 7.5 %block_gates.1 = (f32[1024,256]{1,0:T(8,128)}, f32[1024,256]{1,0:T(8,128)}, f32[1024,256]{1,0:T(8,128)}) custom-call(s32[13]{0:T(128)} %pad_add_fusion.sp, bf16[1024,2304]{1,0:T(8,128)(2,1)} %all-gather.2.cloned.1.call-done.tokens, bf16[2304,384]{1,0:T(8,128)(2,1)} %fusion.1.wsmall, bf16[128,2048]{1,0:T(8,128)(2,1)} %decay_up.1, bf16[128,2048]{1,0:T(8,128)(2,1)} %gate_up.1, ...), custom_call_target="tpu_custom_call" | custom-call | flops 2000000000 | bytes 10000000 | tf_op jit(solution)/shard_map/block_gates/pallas_call | solution.py:197
  71.9 1.3 collective-permute-done.7.rest_5_
  73.2 0.6 copy-done.9
  73.8 20.5 %block_state.1 = (f32[1024,256]{1,0:T(8,128)}, f32[1024,512]{1,0:T(8,128)}, f32[1024,512]{1,0:T(8,128)}, bf16[2304,256]{1,0:T(8,128)(2,1)}, f32[2,128,256]{2,1,0:T(8,128)}, /*index=5*/f32[2,128,128]{2,1,0:T(8,128)}) custom-call(s32[13]{0:T(128)} %pad_add_fusion.sp, bf16[1024,2304]{1,0:T(8,128)(2,1)} %all-gather.2.cloned.1.call-done.tokens, ...), custom_call_target="tpu_custom_call" | custom-call | flops 10000000000 | bytes 20000000 | tf_op jit(solution)/shard_map/block_state/pallas_call | solution.py:286
  94.3 5.2 %collective-permute-start.11 = (f32[2,128,256]{2,1,0:T(8,128)}, f32[2,128,256]{2,1,0:T(8,128)S(1)}, u32[]{:S(2)}, u32[]{:S(2)}) collective-permute-start(f32[2,128,256]{2,1,0:T(8,128)} %get-tuple-element.18), channel_id=1, source_target_pairs={{0,64},{32,96},{1,65},{33,97},{2,66},{34,98},{3,67},{35,99},{4,68}... | collective-permute-start | bytes 786440 | tf_op jit(solution)/shard_map/ppermute | solution.py:487
  99.5 2.4 %collective-permute-start.10 = (f32[2,128,256]{2,1,0:T(8,128)}, f32[2,128,256]{2,1,0:T(8,128)S(1)}, u32[]{:S(2)}, u32[]{:S(2)}) collective-permute-start(f32[2,128,256]{2,1,0:T(8,128)} %get-tuple-element.18), channel_id=1, source_target_pairs={{0,32},{32,64},{64,96},{1,33},{33,65},{65,97},{2,34},{34,66},{66,9... | collective-permute-start | bytes 786440 | tf_op jit(solution)/shard_map/ppermute | solution.py:486
  101.9 1.3 collective-permute-start.12
  103.2 11.9 %block_query.1 = (f32[1024,256]{1,0:T(8,128)}, f32[1024,256]{1,0:T(8,128)}) custom-call(s32[13]{0:T(128)} %pad_add_fusion.sp, bf16[1024,2304]{1,0:T(8,128)(2,1)} %all-gather.2.cloned.1.call-done.tokens, bf16[16,2304]{1,0:T(8,128)(2,1)} %copy-done.9, bf16[2304,256]{1,0:T(8,128)(2,1)} %get-tuple-element.20.wq, f32[4,6144]{1,0:T(4,128)} %conv_q.1, ...), custom_call_target="tpu_custom_call" | custom-call | flops 5000000000 | bytes 20000000 | tf_op jit(solution)/shard_map/block_query/pallas_call | solution.py:370
  115.2 0.6 copy-done.5
  116.0 3.7 %finish.1 = bf16[1024,256]{1,0:T(8,128)(2,1)} custom-call(f32[2,128,256]{2,1,0:T(8,128)} %copy-done.3, f32[2,128,256]{2,1,0:T(8,128)} %copy-done.2, f32[2,128,128]{2,1,0:T(8,128)} %copy-done.5, f32[1024,256]{1,0:T(8,128)} %get-tuple-element.24.qeff, f32[1024,256]{1,0:T(8,128)} %get-tuple-element.25.core, f32[1024,256]{1,0:T(8,128)} %get-tuple-element.26.gate, ...), custom_call_target="tpu_custom_call" | custom-call | tf_op jit(solution)/shard_map/finish/pallas_call | solution.py:418
  119.7 14.8 %all_to_all.5 = bf16[8,128,256]{2,1,0:T(8,128)(2,1)S(1)} all-to-all(bf16[8,128,256]{2,1,0:T(8,128)(2,1)} %bitcast.13), channel_id=1, replica_groups=mesh['z'=4,'x'=4,'c'=2,'y'=4] {'x','c'}, dimensions={0} | all-to-all | bytes 1048576 | tf_op jit(solution)/shard_map/all_to_all | solution.py:491
  134.6 0.8 copy.21
  (43 shorter events, 2.2 us)
Async XLA Ops:
  6.5 54.1 %all-gather.2.cloned.1.call-start = ((), (), s32[]{:S(2)}) async-start(), calls=%async_computation.1 | async-start | bytes 5308416 | tf_op jit(solution)/shard_map/all_gather | solution.py:471
  8.9 12.2 %collective-permute-start.1 = (bf16[1152,128]{1,0:T(8,128)(2,1)S(1)}, bf16[1152,128]{1,0:T(8,128)(2,1)S(1)}, u32[]{:S(2)}, u32[]{:S(2)}) collective-permute-start(bf16[1152,128]{1,0:T(8,128)(2,1)S(1)} %broadcast_select_fusion.1), channel_id=1, source_target_pairs={{0,0},{4,4},{8,100},{12,8},{16,12},{20,16},{24,48},{28,20},{32,56}... | collective-permute-start | bytes 884744 | tf_op jit(solution)/shard_map/ppermute | solution.py:445
  9.5 27.1 %copy-start.6 = (bf16[2304,16]{0,1:T(8,128)(2,1)S(1)}, bf16[2304,16]{0,1:T(8,128)(2,1)}, u32[]{:S(2)}) copy-start(bf16[2304,16]{0,1:T(8,128)(2,1)} %param.18) | copy-start | bytes 221188
  10.6 26.3 %copy-start.10 = (f32[16]{0:T(128)S(1)}, f32[16]{0:T(128)}, u32[]{:S(2)}) copy-start(f32[16]{0:T(128)} %param.19) | copy-start | bytes 196
  10.6 48.4 %copy-start = (bf16[2304,128]{1,0:T(8,128)(2,1)S(1)}, bf16[2304,128]{1,0:T(8,128)(2,1)}, u32[]{:S(2)}) copy-start(bf16[2304,128]{1,0:T(8,128)(2,1)} %param.20) | copy-start | bytes 1769476
  10.6 48.4 %copy-start.1 = (bf16[2304,128]{1,0:T(8,128)(2,1)S(1)}, bf16[2304,128]{1,0:T(8,128)(2,1)}, u32[]{:S(2)}) copy-start(bf16[2304,128]{1,0:T(8,128)(2,1)} %param.15) | copy-start | bytes 1769476
  11.3 11.9 %collective-permute-start.2 = (bf16[576,128]{1,0:T(8,128)(2,1)S(1)}, bf16[576,128]{1,0:T(8,128)(2,1)S(1)}, u32[]{:S(2)}, u32[]{:S(2)}) collective-permute-start(bf16[576,128]{1,0:T(8,128)(2,1)S(1)} %pad_maximum_fusion), channel_id=1, source_target_pairs={{0,0},{4,96},{8,8},{12,40},{16,12},{20,108},{24,20},{28,52},{32,24... | collective-permute-start | bytes 442376 | tf_op jit(solution)/shard_map/ppermute | solution.py:445
  23.2 37.5 %copy-start.4 = (bf16[1728,128]{1,0:T(8,128)(2,1)}, bf16[1728,128]{1,0:T(8,128)(2,1)S(1)}, u32[]{:S(2)}) copy-start(bf16[1728,128]{1,0:T(8,128)(2,1)S(1)} %constant_dynamic-update-slice_fusion.rest_0_) | copy-start | bytes 1327108
  23.2 27.8 %collective-permute-start.5 = (bf16[1728,128]{1,0:T(8,128)(2,1)S(1)}, bf16[1728,128]{1,0:T(8,128)(2,1)S(1)}, u32[]{:S(2)}, u32[]{:S(2)}) collective-permute-start(bf16[1728,128]{1,0:T(8,128)(2,1)S(1)} %constant_dynamic-update-slice_fusion.rest_0_), channel_id=1, source_target_pairs={{0,96},{32,0},{64,32},{96,64},{1,97},{33,1},{65,33},{97,65},{2,98}... | collective-permute-start | bytes 1327112 | tf_op jit(solution)/shard_map/ppermute | solution.py:447
  31.6 20.8 %collective-permute-start.4 = (bf16[1728,128]{1,0:T(8,128)(2,1)S(1)}, bf16[1728,128]{1,0:T(8,128)(2,1)S(1)}, u32[]{:S(2)}, u32[]{:S(2)}) collective-permute-start(bf16[1728,128]{1,0:T(8,128)(2,1)S(1)} %constant_dynamic-update-slice_fusion.rest_0_), channel_id=1, source_target_pairs={{0,64},{32,96},{64,0},{96,32},{1,65},{33,97},{65,1},{97,33},{2,66}... | collective-permute-start | bytes 1327112 | tf_op jit(solution)/shard_map/ppermute | solution.py:447
  35.8 20.2 %collective-permute-start.3 = (bf16[1728,128]{1,0:T(8,128)(2,1)S(1)}, bf16[1728,128]{1,0:T(8,128)(2,1)}, u32[]{:S(2)}, u32[]{:S(2)}) collective-permute-start(bf16[1728,128]{1,0:T(8,128)(2,1)S(1)} %constant_dynamic-update-slice_fusion.rest_0_), channel_id=1, source_target_pairs={{0,32},{32,64},{64,96},{96,0},{1,33},{33,65},{65,97},{97,1},{2,34}... | collective-permute-start | bytes 1327112 | tf_op jit(solution)/shard_map/ppermute | solution.py:447
  38.8 33.1 %collective-permute-start.6 = (bf16[1728,128]{1,0:T(8,128)(2,1)S(1)}, bf16[1728,128]{1,0:T(8,128)(2,1)}, u32[]{:S(2)}, u32[]{:S(2)}) collective-permute-start(bf16[1728,128]{1,0:T(8,128)(2,1)S(1)} %constant_dynamic-update-slice_fusion.rest_0_), channel_id=1, source_target_pairs={{0,1},{1,2},{2,3},{3,0},{4,5},{5,6},{6,7},{7,4},{8,9},{9,10},{10,1... | collective-permute-start | bytes 1327112 | tf_op jit(solution)/shard_map/ppermute | solution.py:448
  51.0 20.9 %copy-start.7 = (bf16[1728,128]{1,0:T(8,128)(2,1)}, bf16[1728,128]{1,0:T(8,128)(2,1)S(1)}, u32[]{:S(2)}) copy-start(bf16[1728,128]{1,0:T(8,128)(2,1)S(1)} %collective-permute-done.5.rest_3_) | copy-start | bytes 1327108
  51.0 20.9 %collective-permute-start.9 = (bf16[1728,128]{1,0:T(8,128)(2,1)S(1)}, bf16[1728,128]{1,0:T(8,128)(2,1)}, u32[]{:S(2)}, u32[]{:S(2)}) collective-permute-start(bf16[1728,128]{1,0:T(8,128)(2,1)S(1)} %collective-permute-done.5.rest_3_), channel_id=1, source_target_pairs={{0,1},{1,2},{2,3},{3,0},{4,5},{5,6},{6,7},{7,4},{8,9},{9,10},{10,1... | collective-permute-start | bytes 1327112 | tf_op jit(solution)/shard_map/ppermute | solution.py:448
  52.4 19.5 %copy-start.8 = (bf16[1728,128]{1,0:T(8,128)(2,1)}, bf16[1728,128]{1,0:T(8,128)(2,1)S(1)}, u32[]{:S(2)}) copy-start(bf16[1728,128]{1,0:T(8,128)(2,1)S(1)} %collective-permute-done.4.rest_2_) | copy-start | bytes 1327108
  52.4 19.5 %collective-permute-start.8 = (bf16[1728,128]{1,0:T(8,128)(2,1)S(1)}, bf16[1728,128]{1,0:T(8,128)(2,1)}, u32[]{:S(2)}, u32[]{:S(2)}) collective-permute-start(bf16[1728,128]{1,0:T(8,128)(2,1)S(1)} %collective-permute-done.4.rest_2_), channel_id=1, source_target_pairs={{0,3},{1,0},{2,1},{3,2},{4,7},{5,4},{6,5},{7,6},{8,11},{9,8},{10,9... | collective-permute-start | bytes 1327112 | tf_op jit(solution)/shard_map/ppermute | solution.py:448
  56.0 17.1 %collective-permute-start.7 = (bf16[1728,128]{1,0:T(8,128)(2,1)}, bf16[1728,128]{1,0:T(8,128)(2,1)}, u32[]{:S(2)}, u32[]{:S(2)}) collective-permute-start(bf16[1728,128]{1,0:T(8,128)(2,1)} %collective-permute-done.3.rest_1_), channel_id=1, source_target_pairs={{0,3},{1,0},{2,1},{3,2},{4,7},{5,4},{6,5},{7,6},{8,11},{9,8},{10,9... | collective-permute-start | bytes 1327112 | tf_op jit(solution)/shard_map/ppermute | solution.py:448
  61.5 11.7 %collective-permute-start = (bf16[16,2304]{1,0:T(8,128)(2,1)S(1)}, bf16[16,2304]{1,0:T(8,128)(2,1)S(1)}, u32[]{:S(2)}, u32[]{:S(2)}) collective-permute-start(bf16[16,2304]{1,0:T(8,128)(2,1)S(1)} %slice.28), channel_id=1, source_target_pairs={{0,32},{32,64},{64,96},{1,33},{33,65},{65,97},{2,34},{34,66},{66,9... | collective-permute-start | bytes 221192 | tf_op jit(solution)/shard_map/ppermute | solution.py:473
  73.2 0.6 copy-start.9
  94.3 20.9 %collective-permute-start.11 = (f32[2,128,256]{2,1,0:T(8,128)}, f32[2,128,256]{2,1,0:T(8,128)S(1)}, u32[]{:S(2)}, u32[]{:S(2)}) collective-permute-start(f32[2,128,256]{2,1,0:T(8,128)} %get-tuple-element.18), channel_id=1, source_target_pairs={{0,64},{32,96},{1,65},{33,97},{2,66},{34,98},{3,67},{35,99},{4,68}... | collective-permute-start | bytes 786440 | tf_op jit(solution)/shard_map/ppermute | solution.py:487
  99.5 15.7 %collective-permute-start.10 = (f32[2,128,256]{2,1,0:T(8,128)}, f32[2,128,256]{2,1,0:T(8,128)S(1)}, u32[]{:S(2)}, u32[]{:S(2)}) collective-permute-start(f32[2,128,256]{2,1,0:T(8,128)} %get-tuple-element.18), channel_id=1, source_target_pairs={{0,32},{32,64},{64,96},{1,33},{33,65},{65,97},{2,34},{34,66},{66,9... | collective-permute-start | bytes 786440 | tf_op jit(solution)/shard_map/ppermute | solution.py:486
  101.9 13.2 %collective-permute-start.12 = (f32[2,128,128]{2,1,0:T(8,128)}, f32[2,128,128]{2,1,0:T(8,128)S(1)}, u32[]{:S(2)}, u32[]{:S(2)}) collective-permute-start(f32[2,128,128]{2,1,0:T(8,128)} %get-tuple-element.19), channel_id=1, source_target_pairs={{0,96},{1,97},{2,98},{3,99},{4,100},{5,101},{6,102},{7,103},{8,104... | collective-permute-start | bytes 393224 | tf_op jit(solution)/shard_map/ppermute | solution.py:488
  115.2 0.6 copy-start.5
  115.2 0.7 copy-start.2
  115.2 0.8 copy-start.3
Sparse Core Ops, SparseCore 0:
  9.0 37.8 all-gather.1

commit v5 on v4

--- a/solution.py
+++ b/solution.py
@@ -35,10 +35,15 @@
     return min(itertools.permutations(range(4)), key=way)
 
 
+def first_head(x, c):
+    return (x ^ 1) + 8 * c
+
+
 def block_plan():
     whole_route, half_route, tables = [], [], []
     for group in range(ROW):
-        blocks = [(kind, hp, 16 * kind + 2 * group + hp) for kind in range(3) for hp in range(2)]
+        head = first_head(group // NC, group % NC)
+        blocks = [(kind, hp, 16 * kind + head + 4 * hp) for kind in range(3) for hp in range(2)]
         whole = [b for b in blocks if b[2] % 3 != 1]
         halves = [b for b in blocks if b[2] % 3 == 1]
         sources = [2 * (m // 3) + (m % 3) // 2 for _, _, m in whole]
@@ -120,8 +125,8 @@
     return pl.BlockSpec(shape, lambda i, s: (0,) * len(shape))
 
 
-def by_group(shape, offset=0):
-    return pl.BlockSpec(shape, lambda i, s: (0, s[2] + offset))
+def columns(shape, block):
+    return pl.BlockSpec(shape, lambda i, s: (0, block))
 
 
 def by_step(columns):
@@ -171,7 +176,7 @@
 def gate_kernel(
     sp, tokens, wsmall, decay_up, gate_up, rate, scale, log_o, beta_o, gate_o
 ):
-    g = sp[2]
+    head = sp[2]
     small = dot(tokens[...], wsmall[...])
     decay_low = small[:, :128].astype(BF)
     gate_low = small[:, 128:256].astype(BF)
@@ -188,7 +193,7 @@
         log_o[ts] = dot(ones_twice, jnp.concatenate([high[ts], low[ts]], axis=0))
     lane = lax.broadcasted_iota(jnp.int32, (STEP, 128), 1)
     for h in range(2):
-        mine = jnp.sum(jnp.where(lane == 2 * g + h, beta_all, 0.0), axis=1, keepdims=True)
+        mine = jnp.sum(jnp.where(lane == head + 4 * h, beta_all, 0.0), axis=1, keepdims=True)
         beta_o[:, DK * h : DK * h + DK] = jnp.broadcast_to(mine, (STEP, DK))
 
 
@@ -204,9 +209,9 @@
             in_specs=[
                 by_step(D),
                 fixed((D, 384)),
-                by_group((128, 256)),
-                by_group((128, 256)),
-                by_group((1, 256)),
+                fixed((128, 256)),
+                fixed((128, 256)),
+                fixed((1, 256)),
                 fixed((1, 128)),
             ],
             out_specs=[by_step(2 * DK)] * 3,
@@ -302,8 +307,8 @@
                 fixed((16, D)),
                 by_step(2 * DK),
                 by_step(2 * DK),
-                by_group((CONV, 256), 8),
-                by_group((CONV, 256), 16),
+                columns((CONV, 256), 1),
+                columns((CONV, 256), 2),
             ]
             + [pl.BlockSpec(memory_space=pl.ANY)] * 8,
             out_specs=[
@@ -378,7 +383,7 @@
                 by_step(D),
                 fixed((16, D)),
                 fixed((D, 2 * DK)),
-                by_group((CONV, 256)),
+                columns((CONV, 256), 0),
                 by_step(2 * DK),
                 by_step(2 * DK),
                 by_step(4 * DK),
@@ -445,7 +450,7 @@
         [lax.ppermute(whole, seq, WHOLE_ROUTE), lax.ppermute(half, seq, HALF_ROUTE)], axis=0
     )
     near = [mine] + [lax.ppermute(mine, "z", ring(k)) for k in range(1, NZ)]
-    return near, [lax.ppermute(p, "y", ring(d)) for p, d in zip(near, (1, 3, 3, 1))]
+    return near, [lax.ppermute(p, "y", ring(d)) for p, d in zip(near, (1, 3, 1, 3))]
 
 
 def per_device(
@@ -466,7 +471,19 @@
     wsmall = jnp.concatenate(
         [decay_down, gate_down, jnp.pad(beta_weight, ((0, 0), (0, 128 - H)))], axis=1
     )
-    sp = jnp.concatenate([jnp.stack([z, y, g]).astype(jnp.int32), jnp.asarray(TABLES)[g]])
+    head = first_head(x, c)
+    sp = jnp.concatenate([jnp.stack([z, y, head]).astype(jnp.int32), jnp.asarray(TABLES)[g]])
+
+    def mine(array, start=0):
+        return jnp.concatenate(
+            [
+                lax.dynamic_slice(array, (0, start + DK * (head + 4 * h)), (array.shape[0], DK))
+                for h in range(2)
+            ],
+            axis=1,
+        )
+
+    taps = jnp.concatenate([mine(conv_weight, HV * kind) for kind in range(3)], axis=1)
     scale = jnp.pad(beta_scale, (0, 128 - H)).reshape(1, 128)
     row = lax.all_gather(tokens, ("x", "c"), axis=0, tiled=True)
     near, far = gather_weights(qkv_weight, c, y)
@@ -475,21 +492,26 @@
         sp,
         row,
         wsmall,
-        decay_up,
-        gate_up,
-        decay_rate.reshape(1, HV),
+        mine(decay_up),
+        mine(gate_up),
+        mine(decay_rate.reshape(1, HV)),
         scale,
     )
     k_downs, solved, carries, wq, state, offset = run_state(
-        sp, row, halo, log_sums, betas, conv_weight, near + far
+        sp, row, halo, log_sums, betas, taps, near + far
     )
     first = lax.ppermute(state, "z", ahead(1))
     second = lax.ppermute(state, "z", ahead(2))
     third = lax.ppermute(offset, "z", ahead(3))
-    qeff, core = run_queries(sp, row, halo, wq, conv_weight, log_sums, k_downs, solved, carries)
+    qeff, core = run_queries(sp, row, halo, wq, taps, log_sums, k_downs, solved, carries)
     out = run_finish(first, second, third, qeff, core, gate, norm_gain.reshape(1, DK))
     out = lax.all_to_all(out.reshape(ROW, SHARD, 2 * DK), ("x", "c"), 0, 0)
-    return out.transpose(1, 0, 2).reshape(SHARD, HV)
+    heads = {
+        first_head(i // NC, i % NC) + 4 * h: out[i, :, DK * h : DK * h + DK]
+        for i in range(ROW)
+        for h in range(2)
+    }
+    return jnp.concatenate([heads[h] for h in range(H)], axis=1)
 
 
 def solution(mesh):

time: 143 us -> 138 us (0.965)
  starting transfers between devices: 43.1 us -> 27.9 us
  local copies, waits for them, and re-layouts: 7.8 us -> 13.5 us
  waiting for transfers between devices: 16.8 us -> 19.1 us
  other arithmetic: 2.36 us -> 4.22 us
    ppermute x3, starting transfers between devices: 13.4 us -> 4.49 us  [gather_weights(): near = [mine] + [lax.ppermute(mine, 'z', ring(k)) for k in range(1, NZ)]]
    ppermute x1, starting transfers between devices: 9.78 us -> 4.94 us  [gather_weights(): lax.ppermute(half, seq, HALF_ROUTE)]
    unnamed x28 -> x60, local copies, waits for them, and re-layouts: 2.64 us -> 7.29 us
    ppermute x3, waiting for transfers between devices: 12.8 us -> 15.7 us  [gather_weights(): near = [mine] + [lax.ppermute(mine, 'z', ring(k)) for k in range(1, NZ)]]
    ppermute x1, waiting for transfers between devices: 2.04 us -> 0.01 us  [gather_weights(): lax.ppermute(half, seq, HALF_ROUTE)]
    concatenate x1 -> x4, other arithmetic: 0.61 us -> 2.48 us  [the longest x3 1.86 us: mine(): jnp.concatenate([lax.dynamic_slice(array, (0, start + DK * (head + 4 * h)...]
    ppermute x1, starting transfers between devices: 2.43 us -> 4.26 us  [per_device(): first = lax.ppermute(state, 'z', ahead(1))]
    dynamic_slice x0 -> x2, local copies, waits for them, and re-layouts: none -> 1.68 us  [mine(): lax.dynamic_slice(array, (0, start + DK * (head + 4 * h)), (array.shape[0...]
  transfers between devices with their start and end apart: 14 -> 14, of which waited for: 4 -> 3; matrix products, arithmetic and copies ran while one was open for 6% -> 11% of each run, Pallas kernels for 14% -> 14%
where the time goes in v5:
time: 138 us; the launch traced here: 137 us
  Pallas kernels  43.5 us (32%)
  starting transfers between devices  27.9 us (20%)
  waiting for transfers between devices  19.1 us (14%)
  blocking collectives  14.9 us (11%)
  between operations  13.8 us (10%)
  local copies, waits for them, and re-layouts  13.5 us (10%)
  other arithmetic  4.22 us (3%)
    pallas_call x1, Pallas kernels, run_state(): pl.pallas_call(state_kernel, name='block_state', out_shape=(jax.ShapeDtyp...  20.4 us
    ppermute x3, waiting for transfers between devices, gather_weights(): near = [mine] + [lax.ppermute(mine, 'z', ring(k)) for k in range(1, NZ)]  15.7 us
    all_to_all x1, blocking collectives, per_device(): out = lax.all_to_all(out.reshape(ROW, SHARD, 2 * DK), ('x', 'c'), 0, 0)  14.9 us
    pallas_call x1, Pallas kernels, run_queries(): pl.pallas_call(query_kernel, name='block_query', out_shape=(wide, wide),...  11.9 us
    pallas_call x1, Pallas kernels, run_gates(): pl.pallas_call(gate_kernel, name='block_gates', out_shape=(wide, wide, wi...  7.46 us
    unnamed x60, local copies, waits for them, and re-layouts  7.29 us
    ppermute x4, starting transfers between devices, gather_weights(): lax.ppermute(p, 'y', ring(d))  6.93 us
    ppermute x1, starting transfers between devices, gather_weights(): lax.ppermute(half, seq, HALF_ROUTE)  4.94 us
  transfers between devices with their start and end apart: 14, of which 3 were waited for; matrix products, arithmetic and copies ran while one was open for 11% of the time, Pallas kernels for 14%

profile of v5, /device:TPU:1, one launch (start us, length us, event | category | flops | bytes accessed | tf_op | source)
XLA Modules:
  0.0 136.9 jit_solution(215375556491656444)
XLA Ops:
  6.5 0.7 all-gather.2.cloned.1.call-update
  7.3 1.0 constant_dynamic-slice_fusion.1
  8.9 4.9 %collective-permute-start.2 = (bf16[576,128]{1,0:T(8,128)(2,1)S(1)}, bf16[576,128]{1,0:T(8,128)(2,1)S(1)}, u32[]{:S(2)}, u32[]{:S(2)}) collective-permute-start(bf16[576,128]{1,0:T(8,128)(2,1)S(1)} %pad_maximum_fusion), channel_id=1, source_target_pairs={{0,0},{4,32},{8,8},{12,104},{16,16},{20,112},{24,28},{28,60},{32,4... | collective-permute-start | bytes 442376 | tf_op jit(solution)/shard_map/ppermute | solution.py:450
  14.5 0.9 collective-permute-start.1
  15.4 0.8 dynamic-slice_bitcast_fusion.1
  17.5 0.7 constant_dynamic-update-slice_fusion.4
  18.2 0.7 constant_dynamic-update-slice_fusion.3
  18.9 0.7 constant_dynamic-update-slice_fusion.2
  19.6 0.7 constant_dynamic-update-slice_fusion.1
  20.8 0.7 constant_dynamic-update-slice_fusion.conv_k.conv_v.conv_q
  21.5 0.8 constant_dynamic-slice_fusion.9
  22.4 3.8 %collective-permute-start.5 = (bf16[1728,128]{1,0:T(8,128)(2,1)S(1)}, bf16[1728,128]{1,0:T(8,128)(2,1)S(1)}, u32[]{:S(2)}, u32[]{:S(2)}) collective-permute-start(bf16[1728,128]{1,0:T(8,128)(2,1)S(1)} %constant_dynamic-update-slice_fusion.6.rest_0_), channel_id=1, source_target_pairs={{0,96},{32,0},{64,32},{96,64},{1,97},{33,1},{65,33},{97,65},{2,98}... | collective-permute-start | bytes 1327112 | tf_op jit(solution)/shard_map/ppermute | solution.py:452
  26.9 0.7 fusion.2
  27.9 1.6 %fusion.1.wsmall = bf16[2304,384]{1,0:T(8,128)(2,1)} fusion(bf16[2304,16]{1,0:T(8,128)(2,1)S(1)} %copy.13, bf16[2304,128]{1,0:T(8,128)(2,1)S(1)} %copy-done.1, bf16[2304,128]{1,0:T(8,128)(2,1)S(1)} %copy-done.2), kind=kLoop, calls=%fused_computation.2 | loop fusion | flops 7077888 | bytes 3022848 | tf_op jit(solution)/shard_map/concatenate | solution.py:471
  29.5 1.3 collective-permute-start.6
  30.8 14.4 %collective-permute-done.5.rest_3_ = bf16[1728,128]{1,0:T(8,128)(2,1)S(1)} collective-permute-done((bf16[1728,128]{1,0:T(8,128)(2,1)S(1)}, bf16[1728,128]{1,0:T(8,128)(2,1)S(1)}, u32[]{:S(2)}, u32[]{:S(2)}) %collective-permute-start.5) | collective-permute-done | bytes 442400 | tf_op jit(solution)/shard_map/ppermute | solution.py:452
  45.2 2.9 %collective-permute-start.9 = (bf16[1728,128]{1,0:T(8,128)(2,1)S(1)}, bf16[1728,128]{1,0:T(8,128)(2,1)S(1)}, u32[]{:S(2)}, u32[]{:S(2)}) collective-permute-start(bf16[1728,128]{1,0:T(8,128)(2,1)S(1)} %collective-permute-done.5.rest_3_), channel_id=1, source_target_pairs={{0,3},{1,0},{2,1},{3,2},{4,7},{5,4},{6,5},{7,6},{8,11},{9,8},{10,9... | collective-permute-start | bytes 1327112 | tf_op jit(solution)/shard_map/ppermute | solution.py:453
  48.2 1.2 collective-permute-done.3.rest_1_
  49.4 2.7 %collective-permute-start.7 = (bf16[1728,128]{1,0:T(8,128)(2,1)}, bf16[1728,128]{1,0:T(8,128)(2,1)S(1)}, u32[]{:S(2)}, u32[]{:S(2)}) collective-permute-start(bf16[1728,128]{1,0:T(8,128)(2,1)} %collective-permute-done.3.rest_1_), channel_id=1, source_target_pairs={{0,3},{1,0},{2,1},{3,2},{4,7},{5,4},{6,5},{7,6},{8,11},{9,8},{10,9... | collective-permute-start | bytes 1327112 | tf_op jit(solution)/shard_map/ppermute | solution.py:453
  54.0 0.9 slice.92
  54.9 1.5 %collective-permute-start = (bf16[16,2304]{1,0:T(8,128)(2,1)S(1)}, bf16[16,2304]{1,0:T(8,128)(2,1)S(1)}, u32[]{:S(2)}, u32[]{:S(2)}) collective-permute-start(bf16[16,2304]{1,0:T(8,128)(2,1)S(1)} %slice.92), channel_id=1, source_target_pairs={{0,32},{32,64},{64,96},{1,33},{33,65},{65,97},{2,34},{34,66},{66,9... | collective-permute-start | bytes 221192 | tf_op jit(solution)/shard_map/ppermute | solution.py:490
  56.3 7.5 %block_gates.1 = (f32[1024,256]{1,0:T(8,128)}, f32[1024,256]{1,0:T(8,128)}, f32[1024,256]{1,0:T(8,128)}) custom-call(s32[13]{0:T(128)} %pad_add_fusion.sp, bf16[1024,2304]{1,0:T(8,128)(2,1)} %all-gather.2.cloned.1.call-done.tokens, bf16[2304,384]{1,0:T(8,128)(2,1)} %fusion.1.wsmall, bf16[128,256]{1,0:T(8,128)(2,1)} %pad_maximum_fusion.1.decay_up, ...), custom_call_target="tpu_custom_call" | custom-call | flops 2000000000 | bytes 10000000 | tf_op jit(solution)/shard_map/block_gates/pallas_call | solution.py:202
  63.9 2.7 %collective-permute-done.7.rest_5_ = bf16[1728,128]{1,0:T(8,128)(2,1)S(1)} collective-permute-done((bf16[1728,128]{1,0:T(8,128)(2,1)}, bf16[1728,128]{1,0:T(8,128)(2,1)S(1)}, u32[]{:S(2)}, u32[]{:S(2)}) %collective-permute-start.7) | collective-permute-done | bytes 442400 | tf_op jit(solution)/shard_map/ppermute | solution.py:453
  66.6 0.7 copy-done.14
  67.4 20.4 %block_state.1 = (f32[1024,256]{1,0:T(8,128)}, f32[1024,512]{1,0:T(8,128)}, f32[1024,512]{1,0:T(8,128)}, bf16[2304,256]{1,0:T(8,128)(2,1)}, f32[2,128,256]{2,1,0:T(8,128)}, /*index=5*/f32[2,128,128]{2,1,0:T(8,128)}) custom-call(s32[13]{0:T(128)} %pad_add_fusion.sp, bf16[1024,2304]{1,0:T(8,128)(2,1)} %all-gather.2.cloned.1.call-done.tokens, ...), custom_call_target="tpu_custom_call" | custom-call | flops 10000000000 | bytes 20000000 | tf_op jit(solution)/shard_map/block_state/pallas_call | solution.py:291
  87.8 3.6 %collective-permute-start.11 = (f32[2,128,256]{2,1,0:T(8,128)}, f32[2,128,256]{2,1,0:T(8,128)S(1)}, u32[]{:S(2)}, u32[]{:S(2)}) collective-permute-start(f32[2,128,256]{2,1,0:T(8,128)} %get-tuple-element.18), channel_id=1, source_target_pairs={{0,64},{32,96},{1,65},{33,97},{2,66},{34,98},{3,67},{35,99},{4,68}... | collective-permute-start | bytes 786440 | tf_op jit(solution)/shard_map/ppermute | solution.py:504
  91.3 4.3 %collective-permute-start.10 = (f32[2,128,256]{2,1,0:T(8,128)}, f32[2,128,256]{2,1,0:T(8,128)S(1)}, u32[]{:S(2)}, u32[]{:S(2)}) collective-permute-start(f32[2,128,256]{2,1,0:T(8,128)} %get-tuple-element.18), channel_id=1, source_target_pairs={{0,32},{32,64},{64,96},{1,33},{33,65},{65,97},{2,34},{34,66},{66,9... | collective-permute-start | bytes 786440 | tf_op jit(solution)/shard_map/ppermute | solution.py:503
  95.6 1.3 collective-permute-start.12
  96.9 11.9 %block_query.1 = (f32[1024,256]{1,0:T(8,128)}, f32[1024,256]{1,0:T(8,128)}) custom-call(s32[13]{0:T(128)} %pad_add_fusion.sp, bf16[1024,2304]{1,0:T(8,128)(2,1)} %all-gather.2.cloned.1.call-done.tokens, bf16[16,2304]{1,0:T(8,128)(2,1)} %copy-done.15, bf16[2304,256]{1,0:T(8,128)(2,1)} %get-tuple-element.20.wq, f32[4,768]{1,0:T(4,128)} %copy-done.9, ...), custom_call_target="tpu_custom_call" | custom-call | flops 5000000000 | bytes 20000000 | tf_op jit(solution)/shard_map/block_query/pallas_call | solution.py:375
  109.7 3.7 %finish.1 = bf16[1024,256]{1,0:T(8,128)(2,1)} custom-call(f32[2,128,256]{2,1,0:T(8,128)} %copy-done.4, f32[2,128,256]{2,1,0:T(8,128)} %copy-done.3, f32[2,128,128]{2,1,0:T(8,128)} %copy-done.6, f32[1024,256]{1,0:T(8,128)} %get-tuple-element.24.qeff, f32[1024,256]{1,0:T(8,128)} %get-tuple-element.25.core, f32[1024,256]{1,0:T(8,128)} %get-tuple-element.26.gate, ...), custom_call_target="tpu_custom_call" | custom-call | tf_op jit(solution)/shard_map/finish/pallas_call | solution.py:423
  113.5 14.9 %all_to_all.5 = bf16[8,128,256]{2,1,0:T(8,128)(2,1)S(1)} all-to-all(bf16[8,128,256]{2,1,0:T(8,128)(2,1)} %bitcast.77), channel_id=1, replica_groups=mesh['z'=4,'x'=4,'c'=2,'y'=4] {'x','c'}, dimensions={0} | all-to-all | bytes 1048576 | tf_op jit(solution)/shard_map/all_to_all | solution.py:508
  128.6 0.8 copy-done.8
  (81 shorter events, 7.6 us)
Async XLA Ops:
  6.5 7.3 %copy-start = (bf16[2304,192]{0,1:T(8,128)(2,1)S(1)}, bf16[2304,192]{0,1:T(8,128)(2,1)}, u32[]{:S(2)}) copy-start(bf16[2304,192]{0,1:T(8,128)(2,1)} %param.13) | copy-start | bytes 2654212
  6.5 47.4 %all-gather.2.cloned.1.call-start = ((), (), s32[]{:S(2)}) async-start(), calls=%async_computation.1 | async-start | bytes 5308416 | tf_op jit(solution)/shard_map/all_gather | solution.py:488
  8.8 11.5 %copy-start.16 = (f32[16]{0:T(128)S(1)}, f32[16]{0:T(128)}, u32[]{:S(2)}) copy-start(f32[16]{0:T(128)} %param.19) | copy-start | bytes 196
  8.9 13.4 %collective-permute-start.2 = (bf16[576,128]{1,0:T(8,128)(2,1)S(1)}, bf16[576,128]{1,0:T(8,128)(2,1)S(1)}, u32[]{:S(2)}, u32[]{:S(2)}) collective-permute-start(bf16[576,128]{1,0:T(8,128)(2,1)S(1)} %pad_maximum_fusion), channel_id=1, source_target_pairs={{0,0},{4,32},{8,8},{12,104},{16,16},{20,112},{24,28},{28,60},{32,4... | collective-permute-start | bytes 442376 | tf_op jit(solution)/shard_map/ppermute | solution.py:450
  13.9 13.7 %copy-start.7 = (bf16[2304,16]{0,1:T(8,128)(2,1)S(1)}, bf16[2304,16]{0,1:T(8,128)(2,1)}, u32[]{:S(2)}) copy-start(bf16[2304,16]{0,1:T(8,128)(2,1)} %param.18) | copy-start | bytes 221188
  14.0 13.9 %copy-start.1 = (bf16[2304,128]{1,0:T(8,128)(2,1)S(1)}, bf16[2304,128]{1,0:T(8,128)(2,1)}, u32[]{:S(2)}) copy-start(bf16[2304,128]{1,0:T(8,128)(2,1)} %param.20) | copy-start | bytes 1769476
  14.0 13.9 %copy-start.2 = (bf16[2304,128]{1,0:T(8,128)(2,1)S(1)}, bf16[2304,128]{1,0:T(8,128)(2,1)}, u32[]{:S(2)}) copy-start(bf16[2304,128]{1,0:T(8,128)(2,1)} %param.15) | copy-start | bytes 1769476
  14.5 7.8 %collective-permute-start.1 = (bf16[1152,128]{1,0:T(8,128)(2,1)S(1)}, bf16[1152,128]{1,0:T(8,128)(2,1)S(1)}, u32[]{:S(2)}, u32[]{:S(2)}) collective-permute-start(bf16[1152,128]{1,0:T(8,128)(2,1)S(1)} %broadcast_select_fusion.1), channel_id=1, source_target_pairs={{0,8},{4,24},{8,16},{12,0},{16,56},{20,12},{24,4},{28,20},{32,44},... | collective-permute-start | bytes 884744 | tf_op jit(solution)/shard_map/ppermute | solution.py:450
  21.5 8.0 %copy-start.9 = (f32[4,768]{1,0:T(4,128)}, f32[4,768]{1,0:T(4,128)S(1)}, u32[]{:S(2)}) copy-start(f32[4,768]{1,0:T(4,128)S(1)} %constant_dynamic-update-slice_fusion.conv_k.conv_v.conv_q) | copy-start | bytes 36868
  22.4 7.1 %copy-start.5 = (bf16[1728,128]{1,0:T(8,128)(2,1)}, bf16[1728,128]{1,0:T(8,128)(2,1)S(1)}, u32[]{:S(2)}) copy-start(bf16[1728,128]{1,0:T(8,128)(2,1)S(1)} %constant_dynamic-update-slice_fusion.6.rest_0_) | copy-start | bytes 1327108
  22.4 22.8 %collective-permute-start.5 = (bf16[1728,128]{1,0:T(8,128)(2,1)S(1)}, bf16[1728,128]{1,0:T(8,128)(2,1)S(1)}, u32[]{:S(2)}, u32[]{:S(2)}) collective-permute-start(bf16[1728,128]{1,0:T(8,128)(2,1)S(1)} %constant_dynamic-update-slice_fusion.6.rest_0_), channel_id=1, source_target_pairs={{0,96},{32,0},{64,32},{96,64},{1,97},{33,1},{65,33},{97,65},{2,98}... | collective-permute-start | bytes 1327112 | tf_op jit(solution)/shard_map/ppermute | solution.py:452
  26.2 21.9 %collective-permute-start.4 = (bf16[1728,128]{1,0:T(8,128)(2,1)S(1)}, bf16[1728,128]{1,0:T(8,128)(2,1)}, u32[]{:S(2)}, u32[]{:S(2)}) collective-permute-start(bf16[1728,128]{1,0:T(8,128)(2,1)S(1)} %constant_dynamic-update-slice_fusion.6.rest_0_), channel_id=1, source_target_pairs={{0,64},{32,96},{64,0},{96,32},{1,65},{33,97},{65,1},{97,33},{2,66}... | collective-permute-start | bytes 1327112 | tf_op jit(solution)/shard_map/ppermute | solution.py:452
  26.5 22.9 %collective-permute-start.3 = (bf16[1728,128]{1,0:T(8,128)(2,1)S(1)}, bf16[1728,128]{1,0:T(8,128)(2,1)}, u32[]{:S(2)}, u32[]{:S(2)}) collective-permute-start(bf16[1728,128]{1,0:T(8,128)(2,1)S(1)} %constant_dynamic-update-slice_fusion.6.rest_0_), channel_id=1, source_target_pairs={{0,32},{32,64},{64,96},{96,0},{1,33},{33,65},{65,97},{97,1},{2,34}... | collective-permute-start | bytes 1327112 | tf_op jit(solution)/shard_map/ppermute | solution.py:452
  29.5 34.3 %collective-permute-start.6 = (bf16[1728,128]{1,0:T(8,128)(2,1)S(1)}, bf16[1728,128]{1,0:T(8,128)(2,1)S(1)}, u32[]{:S(2)}, u32[]{:S(2)}) collective-permute-start(bf16[1728,128]{1,0:T(8,128)(2,1)S(1)} %constant_dynamic-update-slice_fusion.6.rest_0_), channel_id=1, source_target_pairs={{0,1},{1,2},{2,3},{3,0},{4,5},{5,6},{6,7},{7,4},{8,9},{9,10},{10,1... | collective-permute-start | bytes 1327112 | tf_op jit(solution)/shard_map/ppermute | solution.py:453
  45.2 18.6 %copy-start.10 = (bf16[1728,128]{1,0:T(8,128)(2,1)}, bf16[1728,128]{1,0:T(8,128)(2,1)S(1)}, u32[]{:S(2)}) copy-start(bf16[1728,128]{1,0:T(8,128)(2,1)S(1)} %collective-permute-done.5.rest_3_) | copy-start | bytes 1327108
  45.2 18.6 %collective-permute-start.9 = (bf16[1728,128]{1,0:T(8,128)(2,1)S(1)}, bf16[1728,128]{1,0:T(8,128)(2,1)S(1)}, u32[]{:S(2)}, u32[]{:S(2)}) collective-permute-start(bf16[1728,128]{1,0:T(8,128)(2,1)S(1)} %collective-permute-done.5.rest_3_), channel_id=1, source_target_pairs={{0,3},{1,0},{2,1},{3,2},{4,7},{5,4},{6,5},{7,6},{8,11},{9,8},{10,9... | collective-permute-start | bytes 1327112 | tf_op jit(solution)/shard_map/ppermute | solution.py:453
  48.2 15.7 %collective-permute-start.8 = (bf16[1728,128]{1,0:T(8,128)(2,1)}, bf16[1728,128]{1,0:T(8,128)(2,1)S(1)}, u32[]{:S(2)}, u32[]{:S(2)}) collective-permute-start(bf16[1728,128]{1,0:T(8,128)(2,1)} %collective-permute-done.4.rest_2_), channel_id=1, source_target_pairs={{0,1},{1,2},{2,3},{3,0},{4,5},{5,6},{6,7},{7,4},{8,9},{9,10},{10,1... | collective-permute-start | bytes 1327112 | tf_op jit(solution)/shard_map/ppermute | solution.py:453
  49.4 17.2 %collective-permute-start.7 = (bf16[1728,128]{1,0:T(8,128)(2,1)}, bf16[1728,128]{1,0:T(8,128)(2,1)S(1)}, u32[]{:S(2)}, u32[]{:S(2)}) collective-permute-start(bf16[1728,128]{1,0:T(8,128)(2,1)} %collective-permute-done.3.rest_1_), channel_id=1, source_target_pairs={{0,3},{1,0},{2,1},{3,2},{4,7},{5,4},{6,5},{7,6},{8,11},{9,8},{10,9... | collective-permute-start | bytes 1327112 | tf_op jit(solution)/shard_map/ppermute | solution.py:453
  54.9 11.7 %collective-permute-start = (bf16[16,2304]{1,0:T(8,128)(2,1)S(1)}, bf16[16,2304]{1,0:T(8,128)(2,1)S(1)}, u32[]{:S(2)}, u32[]{:S(2)}) collective-permute-start(bf16[16,2304]{1,0:T(8,128)(2,1)S(1)} %slice.92), channel_id=1, source_target_pairs={{0,32},{32,64},{64,96},{1,33},{33,65},{65,97},{2,34},{34,66},{66,9... | collective-permute-start | bytes 221192 | tf_op jit(solution)/shard_map/ppermute | solution.py:490
  63.8 2.8 %copy-start.11 = (bf16[1728,128]{1,0:T(8,128)(2,1)}, bf16[1728,128]{1,0:T(8,128)(2,1)S(1)}, u32[]{:S(2)}) copy-start(bf16[1728,128]{1,0:T(8,128)(2,1)S(1)} %collective-permute-done.6.rest_4_) | copy-start | bytes 1327108
  63.8 2.7 %copy-start.12 = (bf16[1728,128]{1,0:T(8,128)(2,1)}, bf16[1728,128]{1,0:T(8,128)(2,1)S(1)}, u32[]{:S(2)}) copy-start(bf16[1728,128]{1,0:T(8,128)(2,1)S(1)} %collective-permute-done.9.rest_7_) | copy-start | bytes 1327108
  63.9 2.7 %copy-start.13 = (bf16[1728,128]{1,0:T(8,128)(2,1)}, bf16[1728,128]{1,0:T(8,128)(2,1)S(1)}, u32[]{:S(2)}) copy-start(bf16[1728,128]{1,0:T(8,128)(2,1)S(1)} %collective-permute-done.8.rest_6_) | copy-start | bytes 1327108
  66.6 0.8 copy-start.14
  66.6 0.8 copy-start.15
  87.8 21.1 %collective-permute-start.11 = (f32[2,128,256]{2,1,0:T(8,128)}, f32[2,128,256]{2,1,0:T(8,128)S(1)}, u32[]{:S(2)}, u32[]{:S(2)}) collective-permute-start(f32[2,128,256]{2,1,0:T(8,128)} %get-tuple-element.18), channel_id=1, source_target_pairs={{0,64},{32,96},{1,65},{33,97},{2,66},{34,98},{3,67},{35,99},{4,68}... | collective-permute-start | bytes 786440 | tf_op jit(solution)/shard_map/ppermute | solution.py:504
  91.3 17.6 %collective-permute-start.10 = (f32[2,128,256]{2,1,0:T(8,128)}, f32[2,128,256]{2,1,0:T(8,128)S(1)}, u32[]{:S(2)}, u32[]{:S(2)}) collective-permute-start(f32[2,128,256]{2,1,0:T(8,128)} %get-tuple-element.18), channel_id=1, source_target_pairs={{0,32},{32,64},{64,96},{1,33},{33,65},{65,97},{2,34},{34,66},{66,9... | collective-permute-start | bytes 786440 | tf_op jit(solution)/shard_map/ppermute | solution.py:503
  95.6 13.3 %collective-permute-start.12 = (f32[2,128,128]{2,1,0:T(8,128)}, f32[2,128,128]{2,1,0:T(8,128)S(1)}, u32[]{:S(2)}, u32[]{:S(2)}) collective-permute-start(f32[2,128,128]{2,1,0:T(8,128)} %get-tuple-element.19), channel_id=1, source_target_pairs={{0,96},{1,97},{2,98},{3,99},{4,100},{5,101},{6,102},{7,103},{8,104... | collective-permute-start | bytes 393224 | tf_op jit(solution)/shard_map/ppermute | solution.py:505
  108.9 0.6 copy-start.6
  108.9 0.7 copy-start.3
  108.9 0.8 copy-start.4
  128.6 0.8 copy-start.8
Sparse Core Ops, SparseCore 0:
  9.0 37.8 all-gather.1

commit v6 on v5

--- a/solution.py
+++ b/solution.py
@@ -24,7 +24,9 @@
 UNIT = 64
 ROWS = D // 2
 PACK = ROWS // 2
-STEP = 4 * SHARD
+GATE_STEP = 4 * SHARD
+STATE_STEP = 8 * SHARD
+QUERY_STEP = 2 * SHARD
 VMEM_LIMIT = 56 * 1024 * 1024
 
 
@@ -129,8 +131,8 @@
     return pl.BlockSpec(shape, lambda i, s: (0, block))
 
 
-def by_step(columns):
-    return pl.BlockSpec((STEP, columns), lambda i, s: (i, 0))
+def by_step(step, columns):
+    return pl.BlockSpec((step, columns), lambda i, s: (i, 0))
 
 
 def block_columns(block):
@@ -188,13 +190,13 @@
     ones_low = jnp.where(rows >= cols, 1.0, 0.0).astype(BF)
     ones_twice = jnp.concatenate([ones_low, ones_low], axis=1)
     high, low = split(logdec)
-    for blk in range(STEP // SHARD):
+    for blk in range(GATE_STEP // SHARD):
         ts = slice(SHARD * blk, SHARD * blk + SHARD)
         log_o[ts] = dot(ones_twice, jnp.concatenate([high[ts], low[ts]], axis=0))
-    lane = lax.broadcasted_iota(jnp.int32, (STEP, 128), 1)
+    lane = lax.broadcasted_iota(jnp.int32, (GATE_STEP, 128), 1)
     for h in range(2):
         mine = jnp.sum(jnp.where(lane == head + 4 * h, beta_all, 0.0), axis=1, keepdims=True)
-        beta_o[:, DK * h : DK * h + DK] = jnp.broadcast_to(mine, (STEP, DK))
+        beta_o[:, DK * h : DK * h + DK] = jnp.broadcast_to(mine, (GATE_STEP, DK))
 
 
 def run_gates(sp, tokens, wsmall, decay_up, gate_up, rate, scale):
@@ -205,16 +207,16 @@
         out_shape=(wide, wide, wide),
         grid_spec=pltpu.PrefetchScalarGridSpec(
             num_scalar_prefetch=1,
-            grid=(GROUP // STEP,),
+            grid=(GROUP // GATE_STEP,),
             in_specs=[
-                by_step(D),
+                by_step(GATE_STEP, D),
                 fixed((D, 384)),
                 fixed((128, 256)),
                 fixed((128, 256)),
                 fixed((1, 256)),
                 fixed((1, 128)),
             ],
-            out_specs=[by_step(2 * DK)] * 3,
+            out_specs=[by_step(GATE_STEP, 2 * DK)] * 3,
         ),
         compiler_params=params(),
         cost_estimate=cost(2e9, 1e7),
@@ -222,9 +224,10 @@
 
 
 def active(mixed, cols, taps):
-    total = taps[0:1] * mixed[5 : 5 + STEP, cols]
+    count = mixed.shape[0] - 8
+    total = taps[0:1] * mixed[5 : 5 + count, cols]
     for j in range(1, CONV):
-        total = total + taps[j : j + 1] * mixed[5 + j : 5 + j + STEP, cols]
+        total = total + taps[j : j + 1] * mixed[5 + j : 5 + j + count, cols]
     return total * sigmoid(total)
 
 
@@ -249,13 +252,13 @@
     mixed[8:] = dot(tokens[...], wbuf[:, 2 * DK :]).astype(BF).astype(F32)
     keys = active(mixed, slice(0, 256), conv_k)
     values = active(mixed, slice(256, 512), conv_v)
-    mixed[0:8] = mixed[STEP : STEP + 8]
+    mixed[0:8] = mixed[STATE_STEP : STATE_STEP + 8]
 
     rows = lax.broadcasted_iota(jnp.int32, (SHARD, SHARD), 0)
     cols = lax.broadcasted_iota(jnp.int32, (SHARD, SHARD), 1)
     places = [
         (h, blk, slice(SHARD * blk, SHARD * blk + SHARD), slice(DK * h, DK * h + DK))
-        for blk in range(STEP // SHARD)
+        for blk in range(STATE_STEP // SHARD)
         for h in range(2)
     ]
     systems, sides, ends, tails = [], [], [], []
@@ -301,20 +304,20 @@
         ),
         grid_spec=pltpu.PrefetchScalarGridSpec(
             num_scalar_prefetch=1,
-            grid=(GROUP // STEP,),
+            grid=(GROUP // STATE_STEP,),
             in_specs=[
-                by_step(D),
+                by_step(STATE_STEP, D),
                 fixed((16, D)),
-                by_step(2 * DK),
-                by_step(2 * DK),
+                by_step(STATE_STEP, 2 * DK),
+                by_step(STATE_STEP, 2 * DK),
                 columns((CONV, 256), 1),
                 columns((CONV, 256), 2),
             ]
             + [pl.BlockSpec(memory_space=pl.ANY)] * 8,
             out_specs=[
-                by_step(2 * DK),
-                by_step(4 * DK),
-                by_step(4 * DK),
+                by_step(STATE_STEP, 2 * DK),
+                by_step(STATE_STEP, 4 * DK),
+                by_step(STATE_STEP, 4 * DK),
                 fixed((D, 2 * DK)),
                 fixed((2, DK, 2 * DK)),
                 fixed((2, DK, DK)),
@@ -322,7 +325,7 @@
             scratch_shapes=[
                 pltpu.VMEM((2, NZ, PACK, 128), BF),
                 pltpu.VMEM((D, 6 * DK), BF),
-                pltpu.VMEM((8 + STEP, 512), F32),
+                pltpu.VMEM((8 + STATE_STEP, 512), F32),
                 pltpu.VMEM((2, DK, 2 * DK), F32),
                 pltpu.SemaphoreType.DMA((16,)),
             ],
@@ -342,7 +345,7 @@
 
     mixed[8:] = dot(tokens[...], wq[...]).astype(BF).astype(F32)
     query = active(mixed, slice(0, 256), conv_q)
-    mixed[0:8] = mixed[STEP : STEP + 8]
+    mixed[0:8] = mixed[QUERY_STEP : QUERY_STEP + 8]
     rows = lax.broadcasted_iota(jnp.int32, (SHARD, SHARD), 0)
     cols = lax.broadcasted_iota(jnp.int32, (SHARD, SHARD), 1)
     places = [
@@ -351,7 +354,7 @@
             slice(DK * h, DK * h + DK),
             slice(2 * DK * h, 2 * DK * h + 2 * DK),
         )
-        for blk in range(STEP // SHARD)
+        for blk in range(QUERY_STEP // SHARD)
         for h in range(2)
     ]
     ups = []
@@ -378,19 +381,19 @@
         out_shape=(wide, wide),
         grid_spec=pltpu.PrefetchScalarGridSpec(
             num_scalar_prefetch=1,
-            grid=(GROUP // STEP,),
+            grid=(GROUP // QUERY_STEP,),
             in_specs=[
-                by_step(D),
+                by_step(QUERY_STEP, D),
                 fixed((16, D)),
                 fixed((D, 2 * DK)),
                 columns((CONV, 256), 0),
-                by_step(2 * DK),
-                by_step(2 * DK),
-                by_step(4 * DK),
-                by_step(4 * DK),
+                by_step(QUERY_STEP, 2 * DK),
+                by_step(QUERY_STEP, 2 * DK),
+                by_step(QUERY_STEP, 4 * DK),
+                by_step(QUERY_STEP, 4 * DK),
             ],
-            out_specs=[by_step(2 * DK)] * 2,
-            scratch_shapes=[pltpu.VMEM((8 + STEP, 256), F32)],
+            out_specs=[by_step(QUERY_STEP, 2 * DK)] * 2,
+            scratch_shapes=[pltpu.VMEM((8 + QUERY_STEP, 256), F32)],
         ),
         compiler_params=params(),
         cost_estimate=cost(5e9, 2e7),

time: 138 us -> 136 us (0.986)
  Pallas kernels: 43.5 us -> 41.2 us
    pallas_call x1, Pallas kernels: 20.4 us -> 18.7 us  [run_state(): pl.pallas_call(state_kernel, name='block_state', out_shape=(jax.ShapeDtyp...]
where the time goes in v6:
time: 136 us; the launch traced here: 135 us
  Pallas kernels  41.2 us (30%)
  starting transfers between devices  28.1 us (21%)
  waiting for transfers between devices  19.1 us (14%)
  blocking collectives  14.9 us (11%)
  between operations  13.8 us (10%)
  local copies, waits for them, and re-layouts  13.5 us (10%)
  other arithmetic  4.22 us (3%)
    pallas_call x1, Pallas kernels, run_state(): pl.pallas_call(state_kernel, name='block_state', out_shape=(jax.ShapeDtyp...  18.7 us
    ppermute x3, waiting for transfers between devices, gather_weights(): near = [mine] + [lax.ppermute(mine, 'z', ring(k)) for k in range(1, NZ)]  15.7 us
    all_to_all x1, blocking collectives, per_device(): out = lax.all_to_all(out.reshape(ROW, SHARD, 2 * DK), ('x', 'c'), 0, 0)  14.9 us
    pallas_call x1, Pallas kernels, run_queries(): pl.pallas_call(query_kernel, name='block_query', out_shape=(wide, wide),...  11.3 us
    pallas_call x1, Pallas kernels, run_gates(): pl.pallas_call(gate_kernel, name='block_gates', out_shape=(wide, wide, wi...  7.46 us
    unnamed x60, local copies, waits for them, and re-layouts  7.29 us
    ppermute x4, starting transfers between devices, gather_weights(): lax.ppermute(p, 'y', ring(d))  6.93 us
    ppermute x1, starting transfers between devices, gather_weights(): lax.ppermute(half, seq, HALF_ROUTE)  4.94 us
  transfers between devices with their start and end apart: 14, of which 3 were waited for; matrix products, arithmetic and copies ran while one was open for 11% of the time, Pallas kernels for 14%

profile of v6, /device:TPU:1, one launch (start us, length us, event | category | flops | bytes accessed | tf_op | source)
XLA Modules:
  0.0 134.8 jit_solution(15256555247116769593)
XLA Ops:
  6.5 0.7 all-gather.2.cloned.1.call-update
  7.3 1.0 constant_dynamic-slice_fusion.1
  8.9 4.9 %collective-permute-start.2 = (bf16[576,128]{1,0:T(8,128)(2,1)S(1)}, bf16[576,128]{1,0:T(8,128)(2,1)S(1)}, u32[]{:S(2)}, u32[]{:S(2)}) collective-permute-start(bf16[576,128]{1,0:T(8,128)(2,1)S(1)} %pad_maximum_fusion), channel_id=1, source_target_pairs={{0,0},{4,32},{8,8},{12,104},{16,16},{20,112},{24,28},{28,60},{32,4... | collective-permute-start | bytes 442376 | tf_op jit(solution)/shard_map/ppermute | solution.py:453
  14.5 0.9 collective-permute-start.1
  15.4 0.8 dynamic-slice_bitcast_fusion.1
  17.5 0.7 constant_dynamic-update-slice_fusion.4
  18.2 0.7 constant_dynamic-update-slice_fusion.3
  18.9 0.7 constant_dynamic-update-slice_fusion.2
  19.6 0.7 constant_dynamic-update-slice_fusion.1
  20.8 0.7 constant_dynamic-update-slice_fusion.conv_k.conv_v.conv_q
  21.5 0.8 constant_dynamic-slice_fusion.9
  22.4 3.8 %collective-permute-start.5 = (bf16[1728,128]{1,0:T(8,128)(2,1)S(1)}, bf16[1728,128]{1,0:T(8,128)(2,1)S(1)}, u32[]{:S(2)}, u32[]{:S(2)}) collective-permute-start(bf16[1728,128]{1,0:T(8,128)(2,1)S(1)} %constant_dynamic-update-slice_fusion.6.rest_0_), channel_id=1, source_target_pairs={{0,96},{32,0},{64,32},{96,64},{1,97},{33,1},{65,33},{97,65},{2,98}... | collective-permute-start | bytes 1327112 | tf_op jit(solution)/shard_map/ppermute | solution.py:455
  26.9 0.7 fusion.2
  27.9 1.6 %fusion.1.wsmall = bf16[2304,384]{1,0:T(8,128)(2,1)} fusion(bf16[2304,16]{1,0:T(8,128)(2,1)S(1)} %copy.13, bf16[2304,128]{1,0:T(8,128)(2,1)S(1)} %copy-done.1, bf16[2304,128]{1,0:T(8,128)(2,1)S(1)} %copy-done.2), kind=kLoop, calls=%fused_computation.2 | loop fusion | flops 7077888 | bytes 3022848 | tf_op jit(solution)/shard_map/concatenate | solution.py:474
  29.5 1.3 collective-permute-start.6
  30.8 14.4 %collective-permute-done.5.rest_3_ = bf16[1728,128]{1,0:T(8,128)(2,1)S(1)} collective-permute-done((bf16[1728,128]{1,0:T(8,128)(2,1)S(1)}, bf16[1728,128]{1,0:T(8,128)(2,1)S(1)}, u32[]{:S(2)}, u32[]{:S(2)}) %collective-permute-start.5) | collective-permute-done | bytes 442400 | tf_op jit(solution)/shard_map/ppermute | solution.py:455
  45.2 2.9 %collective-permute-start.9 = (bf16[1728,128]{1,0:T(8,128)(2,1)S(1)}, bf16[1728,128]{1,0:T(8,128)(2,1)S(1)}, u32[]{:S(2)}, u32[]{:S(2)}) collective-permute-start(bf16[1728,128]{1,0:T(8,128)(2,1)S(1)} %collective-permute-done.5.rest_3_), channel_id=1, source_target_pairs={{0,3},{1,0},{2,1},{3,2},{4,7},{5,4},{6,5},{7,6},{8,11},{9,8},{10,9... | collective-permute-start | bytes 1327112 | tf_op jit(solution)/shard_map/ppermute | solution.py:456
  48.2 1.2 collective-permute-done.3.rest_1_
  49.4 2.7 %collective-permute-start.7 = (bf16[1728,128]{1,0:T(8,128)(2,1)}, bf16[1728,128]{1,0:T(8,128)(2,1)S(1)}, u32[]{:S(2)}, u32[]{:S(2)}) collective-permute-start(bf16[1728,128]{1,0:T(8,128)(2,1)} %collective-permute-done.3.rest_1_), channel_id=1, source_target_pairs={{0,3},{1,0},{2,1},{3,2},{4,7},{5,4},{6,5},{7,6},{8,11},{9,8},{10,9... | collective-permute-start | bytes 1327112 | tf_op jit(solution)/shard_map/ppermute | solution.py:456
  54.0 0.9 slice.92
  54.9 1.5 %collective-permute-start = (bf16[16,2304]{1,0:T(8,128)(2,1)S(1)}, bf16[16,2304]{1,0:T(8,128)(2,1)S(1)}, u32[]{:S(2)}, u32[]{:S(2)}) collective-permute-start(bf16[16,2304]{1,0:T(8,128)(2,1)S(1)} %slice.92), channel_id=1, source_target_pairs={{0,32},{32,64},{64,96},{1,33},{33,65},{65,97},{2,34},{34,66},{66,9... | collective-permute-start | bytes 221192 | tf_op jit(solution)/shard_map/ppermute | solution.py:493
  56.3 7.5 %block_gates.1 = (f32[1024,256]{1,0:T(8,128)}, f32[1024,256]{1,0:T(8,128)}, f32[1024,256]{1,0:T(8,128)}) custom-call(s32[13]{0:T(128)} %pad_add_fusion.sp, bf16[1024,2304]{1,0:T(8,128)(2,1)} %all-gather.2.cloned.1.call-done.tokens, bf16[2304,384]{1,0:T(8,128)(2,1)} %fusion.1.wsmall, bf16[128,256]{1,0:T(8,128)(2,1)} %pad_maximum_fusion.1.decay_up, ...), custom_call_target="tpu_custom_call" | custom-call | flops 2000000000 | bytes 10000000 | tf_op jit(solution)/shard_map/block_gates/pallas_call | solution.py:204
  63.9 2.7 %collective-permute-done.7.rest_5_ = bf16[1728,128]{1,0:T(8,128)(2,1)S(1)} collective-permute-done((bf16[1728,128]{1,0:T(8,128)(2,1)}, bf16[1728,128]{1,0:T(8,128)(2,1)S(1)}, u32[]{:S(2)}, u32[]{:S(2)}) %collective-permute-start.7) | collective-permute-done | bytes 442400 | tf_op jit(solution)/shard_map/ppermute | solution.py:456
  66.6 0.7 copy-done.14
  67.4 18.7 %block_state.1 = (f32[1024,256]{1,0:T(8,128)}, f32[1024,512]{1,0:T(8,128)}, f32[1024,512]{1,0:T(8,128)}, bf16[2304,256]{1,0:T(8,128)(2,1)}, f32[2,128,256]{2,1,0:T(8,128)}, /*index=5*/f32[2,128,128]{2,1,0:T(8,128)}) custom-call(s32[13]{0:T(128)} %pad_add_fusion.sp, bf16[1024,2304]{1,0:T(8,128)(2,1)} %all-gather.2.cloned.1.call-done.tokens, ...), custom_call_target="tpu_custom_call" | custom-call | flops 10000000000 | bytes 20000000 | tf_op jit(solution)/shard_map/block_state/pallas_call | solution.py:294
  86.1 3.6 %collective-permute-start.11 = (f32[2,128,256]{2,1,0:T(8,128)}, f32[2,128,256]{2,1,0:T(8,128)S(1)}, u32[]{:S(2)}, u32[]{:S(2)}) collective-permute-start(f32[2,128,256]{2,1,0:T(8,128)} %get-tuple-element.18), channel_id=1, source_target_pairs={{0,64},{32,96},{1,65},{33,97},{2,66},{34,98},{3,67},{35,99},{4,68}... | collective-permute-start | bytes 786440 | tf_op jit(solution)/shard_map/ppermute | solution.py:507
  89.6 4.3 %collective-permute-start.10 = (f32[2,128,256]{2,1,0:T(8,128)}, f32[2,128,256]{2,1,0:T(8,128)S(1)}, u32[]{:S(2)}, u32[]{:S(2)}) collective-permute-start(f32[2,128,256]{2,1,0:T(8,128)} %get-tuple-element.18), channel_id=1, source_target_pairs={{0,32},{32,64},{64,96},{1,33},{33,65},{65,97},{2,34},{34,66},{66,9... | collective-permute-start | bytes 786440 | tf_op jit(solution)/shard_map/ppermute | solution.py:506
  93.9 1.5 %collective-permute-start.12 = (f32[2,128,128]{2,1,0:T(8,128)}, f32[2,128,128]{2,1,0:T(8,128)S(1)}, u32[]{:S(2)}, u32[]{:S(2)}) collective-permute-start(f32[2,128,128]{2,1,0:T(8,128)} %get-tuple-element.19), channel_id=1, source_target_pairs={{0,96},{1,97},{2,98},{3,99},{4,100},{5,101},{6,102},{7,103},{8,104... | collective-permute-start | bytes 393224 | tf_op jit(solution)/shard_map/ppermute | solution.py:508
  95.4 11.3 %block_query.1 = (f32[1024,256]{1,0:T(8,128)}, f32[1024,256]{1,0:T(8,128)}) custom-call(s32[13]{0:T(128)} %pad_add_fusion.sp, bf16[1024,2304]{1,0:T(8,128)(2,1)} %all-gather.2.cloned.1.call-done.tokens, bf16[16,2304]{1,0:T(8,128)(2,1)} %copy-done.15, bf16[2304,256]{1,0:T(8,128)(2,1)} %get-tuple-element.20.wq, f32[4,768]{1,0:T(4,128)} %copy-done.9, ...), custom_call_target="tpu_custom_call" | custom-call | flops 5000000000 | bytes 20000000 | tf_op jit(solution)/shard_map/block_query/pallas_call | solution.py:378
  107.7 3.7 %finish.1 = bf16[1024,256]{1,0:T(8,128)(2,1)} custom-call(f32[2,128,256]{2,1,0:T(8,128)} %copy-done.4, f32[2,128,256]{2,1,0:T(8,128)} %copy-done.3, f32[2,128,128]{2,1,0:T(8,128)} %copy-done.6, f32[1024,256]{1,0:T(8,128)} %get-tuple-element.24.qeff, f32[1024,256]{1,0:T(8,128)} %get-tuple-element.25.core, f32[1024,256]{1,0:T(8,128)} %get-tuple-element.26.gate, ...), custom_call_target="tpu_custom_call" | custom-call | tf_op jit(solution)/shard_map/finish/pallas_call | solution.py:426
  111.4 14.9 %all_to_all.5 = bf16[8,128,256]{2,1,0:T(8,128)(2,1)S(1)} all-to-all(bf16[8,128,256]{2,1,0:T(8,128)(2,1)} %bitcast.77), channel_id=1, replica_groups=mesh['z'=4,'x'=4,'c'=2,'y'=4] {'x','c'}, dimensions={0} | all-to-all | bytes 1048576 | tf_op jit(solution)/shard_map/all_to_all | solution.py:511
  126.5 0.8 copy-done.8
  (81 shorter events, 7.6 us)
Async XLA Ops:
  6.5 7.3 %copy-start = (bf16[2304,192]{0,1:T(8,128)(2,1)S(1)}, bf16[2304,192]{0,1:T(8,128)(2,1)}, u32[]{:S(2)}) copy-start(bf16[2304,192]{0,1:T(8,128)(2,1)} %param.13) | copy-start | bytes 2654212
  6.5 47.4 %all-gather.2.cloned.1.call-start = ((), (), s32[]{:S(2)}) async-start(), calls=%async_computation.1 | async-start | bytes 5308416 | tf_op jit(solution)/shard_map/all_gather | solution.py:491
  8.8 11.5 %copy-start.16 = (f32[16]{0:T(128)S(1)}, f32[16]{0:T(128)}, u32[]{:S(2)}) copy-start(f32[16]{0:T(128)} %param.19) | copy-start | bytes 196
  8.9 13.4 %collective-permute-start.2 = (bf16[576,128]{1,0:T(8,128)(2,1)S(1)}, bf16[576,128]{1,0:T(8,128)(2,1)S(1)}, u32[]{:S(2)}, u32[]{:S(2)}) collective-permute-start(bf16[576,128]{1,0:T(8,128)(2,1)S(1)} %pad_maximum_fusion), channel_id=1, source_target_pairs={{0,0},{4,32},{8,8},{12,104},{16,16},{20,112},{24,28},{28,60},{32,4... | collective-permute-start | bytes 442376 | tf_op jit(solution)/shard_map/ppermute | solution.py:453
  13.9 13.7 %copy-start.7 = (bf16[2304,16]{0,1:T(8,128)(2,1)S(1)}, bf16[2304,16]{0,1:T(8,128)(2,1)}, u32[]{:S(2)}) copy-start(bf16[2304,16]{0,1:T(8,128)(2,1)} %param.18) | copy-start | bytes 221188
  14.0 13.9 %copy-start.1 = (bf16[2304,128]{1,0:T(8,128)(2,1)S(1)}, bf16[2304,128]{1,0:T(8,128)(2,1)}, u32[]{:S(2)}) copy-start(bf16[2304,128]{1,0:T(8,128)(2,1)} %param.20) | copy-start | bytes 1769476
  14.0 13.9 %copy-start.2 = (bf16[2304,128]{1,0:T(8,128)(2,1)S(1)}, bf16[2304,128]{1,0:T(8,128)(2,1)}, u32[]{:S(2)}) copy-start(bf16[2304,128]{1,0:T(8,128)(2,1)} %param.15) | copy-start | bytes 1769476
  14.5 7.8 %collective-permute-start.1 = (bf16[1152,128]{1,0:T(8,128)(2,1)S(1)}, bf16[1152,128]{1,0:T(8,128)(2,1)S(1)}, u32[]{:S(2)}, u32[]{:S(2)}) collective-permute-start(bf16[1152,128]{1,0:T(8,128)(2,1)S(1)} %broadcast_select_fusion.1), channel_id=1, source_target_pairs={{0,8},{4,24},{8,16},{12,0},{16,56},{20,12},{24,4},{28,20},{32,44},... | collective-permute-start | bytes 884744 | tf_op jit(solution)/shard_map/ppermute | solution.py:453
  21.5 8.0 %copy-start.9 = (f32[4,768]{1,0:T(4,128)}, f32[4,768]{1,0:T(4,128)S(1)}, u32[]{:S(2)}) copy-start(f32[4,768]{1,0:T(4,128)S(1)} %constant_dynamic-update-slice_fusion.conv_k.conv_v.conv_q) | copy-start | bytes 36868
  22.4 7.1 %copy-start.5 = (bf16[1728,128]{1,0:T(8,128)(2,1)}, bf16[1728,128]{1,0:T(8,128)(2,1)S(1)}, u32[]{:S(2)}) copy-start(bf16[1728,128]{1,0:T(8,128)(2,1)S(1)} %constant_dynamic-update-slice_fusion.6.rest_0_) | copy-start | bytes 1327108
  22.4 22.8 %collective-permute-start.5 = (bf16[1728,128]{1,0:T(8,128)(2,1)S(1)}, bf16[1728,128]{1,0:T(8,128)(2,1)S(1)}, u32[]{:S(2)}, u32[]{:S(2)}) collective-permute-start(bf16[1728,128]{1,0:T(8,128)(2,1)S(1)} %constant_dynamic-update-slice_fusion.6.rest_0_), channel_id=1, source_target_pairs={{0,96},{32,0},{64,32},{96,64},{1,97},{33,1},{65,33},{97,65},{2,98}... | collective-permute-start | bytes 1327112 | tf_op jit(solution)/shard_map/ppermute | solution.py:455
  26.2 21.9 %collective-permute-start.4 = (bf16[1728,128]{1,0:T(8,128)(2,1)S(1)}, bf16[1728,128]{1,0:T(8,128)(2,1)}, u32[]{:S(2)}, u32[]{:S(2)}) collective-permute-start(bf16[1728,128]{1,0:T(8,128)(2,1)S(1)} %constant_dynamic-update-slice_fusion.6.rest_0_), channel_id=1, source_target_pairs={{0,64},{32,96},{64,0},{96,32},{1,65},{33,97},{65,1},{97,33},{2,66}... | collective-permute-start | bytes 1327112 | tf_op jit(solution)/shard_map/ppermute | solution.py:455
  26.5 22.9 %collective-permute-start.3 = (bf16[1728,128]{1,0:T(8,128)(2,1)S(1)}, bf16[1728,128]{1,0:T(8,128)(2,1)}, u32[]{:S(2)}, u32[]{:S(2)}) collective-permute-start(bf16[1728,128]{1,0:T(8,128)(2,1)S(1)} %constant_dynamic-update-slice_fusion.6.rest_0_), channel_id=1, source_target_pairs={{0,32},{32,64},{64,96},{96,0},{1,33},{33,65},{65,97},{97,1},{2,34}... | collective-permute-start | bytes 1327112 | tf_op jit(solution)/shard_map/ppermute | solution.py:455
  29.5 34.3 %collective-permute-start.6 = (bf16[1728,128]{1,0:T(8,128)(2,1)S(1)}, bf16[1728,128]{1,0:T(8,128)(2,1)S(1)}, u32[]{:S(2)}, u32[]{:S(2)}) collective-permute-start(bf16[1728,128]{1,0:T(8,128)(2,1)S(1)} %constant_dynamic-update-slice_fusion.6.rest_0_), channel_id=1, source_target_pairs={{0,1},{1,2},{2,3},{3,0},{4,5},{5,6},{6,7},{7,4},{8,9},{9,10},{10,1... | collective-permute-start | bytes 1327112 | tf_op jit(solution)/shard_map/ppermute | solution.py:456
  45.2 18.6 %copy-start.10 = (bf16[1728,128]{1,0:T(8,128)(2,1)}, bf16[1728,128]{1,0:T(8,128)(2,1)S(1)}, u32[]{:S(2)}) copy-start(bf16[1728,128]{1,0:T(8,128)(2,1)S(1)} %collective-permute-done.5.rest_3_) | copy-start | bytes 1327108
  45.2 18.6 %collective-permute-start.9 = (bf16[1728,128]{1,0:T(8,128)(2,1)S(1)}, bf16[1728,128]{1,0:T(8,128)(2,1)S(1)}, u32[]{:S(2)}, u32[]{:S(2)}) collective-permute-start(bf16[1728,128]{1,0:T(8,128)(2,1)S(1)} %collective-permute-done.5.rest_3_), channel_id=1, source_target_pairs={{0,3},{1,0},{2,1},{3,2},{4,7},{5,4},{6,5},{7,6},{8,11},{9,8},{10,9... | collective-permute-start | bytes 1327112 | tf_op jit(solution)/shard_map/ppermute | solution.py:456
  48.2 15.7 %collective-permute-start.8 = (bf16[1728,128]{1,0:T(8,128)(2,1)}, bf16[1728,128]{1,0:T(8,128)(2,1)S(1)}, u32[]{:S(2)}, u32[]{:S(2)}) collective-permute-start(bf16[1728,128]{1,0:T(8,128)(2,1)} %collective-permute-done.4.rest_2_), channel_id=1, source_target_pairs={{0,1},{1,2},{2,3},{3,0},{4,5},{5,6},{6,7},{7,4},{8,9},{9,10},{10,1... | collective-permute-start | bytes 1327112 | tf_op jit(solution)/shard_map/ppermute | solution.py:456
  49.4 17.2 %collective-permute-start.7 = (bf16[1728,128]{1,0:T(8,128)(2,1)}, bf16[1728,128]{1,0:T(8,128)(2,1)S(1)}, u32[]{:S(2)}, u32[]{:S(2)}) collective-permute-start(bf16[1728,128]{1,0:T(8,128)(2,1)} %collective-permute-done.3.rest_1_), channel_id=1, source_target_pairs={{0,3},{1,0},{2,1},{3,2},{4,7},{5,4},{6,5},{7,6},{8,11},{9,8},{10,9... | collective-permute-start | bytes 1327112 | tf_op jit(solution)/shard_map/ppermute | solution.py:456
  54.9 11.7 %collective-permute-start = (bf16[16,2304]{1,0:T(8,128)(2,1)S(1)}, bf16[16,2304]{1,0:T(8,128)(2,1)S(1)}, u32[]{:S(2)}, u32[]{:S(2)}) collective-permute-start(bf16[16,2304]{1,0:T(8,128)(2,1)S(1)} %slice.92), channel_id=1, source_target_pairs={{0,32},{32,64},{64,96},{1,33},{33,65},{65,97},{2,34},{34,66},{66,9... | collective-permute-start | bytes 221192 | tf_op jit(solution)/shard_map/ppermute | solution.py:493
  63.8 2.8 %copy-start.11 = (bf16[1728,128]{1,0:T(8,128)(2,1)}, bf16[1728,128]{1,0:T(8,128)(2,1)S(1)}, u32[]{:S(2)}) copy-start(bf16[1728,128]{1,0:T(8,128)(2,1)S(1)} %collective-permute-done.6.rest_4_) | copy-start | bytes 1327108
  63.8 2.7 %copy-start.12 = (bf16[1728,128]{1,0:T(8,128)(2,1)}, bf16[1728,128]{1,0:T(8,128)(2,1)S(1)}, u32[]{:S(2)}) copy-start(bf16[1728,128]{1,0:T(8,128)(2,1)S(1)} %collective-permute-done.9.rest_7_) | copy-start | bytes 1327108
  63.9 2.7 %copy-start.13 = (bf16[1728,128]{1,0:T(8,128)(2,1)}, bf16[1728,128]{1,0:T(8,128)(2,1)S(1)}, u32[]{:S(2)}) copy-start(bf16[1728,128]{1,0:T(8,128)(2,1)S(1)} %collective-permute-done.8.rest_6_) | copy-start | bytes 1327108
  66.6 0.8 copy-start.14
  66.6 0.8 copy-start.15
  86.1 20.7 %collective-permute-start.11 = (f32[2,128,256]{2,1,0:T(8,128)}, f32[2,128,256]{2,1,0:T(8,128)S(1)}, u32[]{:S(2)}, u32[]{:S(2)}) collective-permute-start(f32[2,128,256]{2,1,0:T(8,128)} %get-tuple-element.18), channel_id=1, source_target_pairs={{0,64},{32,96},{1,65},{33,97},{2,66},{34,98},{3,67},{35,99},{4,68}... | collective-permute-start | bytes 786440 | tf_op jit(solution)/shard_map/ppermute | solution.py:507
  89.6 17.2 %collective-permute-start.10 = (f32[2,128,256]{2,1,0:T(8,128)}, f32[2,128,256]{2,1,0:T(8,128)S(1)}, u32[]{:S(2)}, u32[]{:S(2)}) collective-permute-start(f32[2,128,256]{2,1,0:T(8,128)} %get-tuple-element.18), channel_id=1, source_target_pairs={{0,32},{32,64},{64,96},{1,33},{33,65},{65,97},{2,34},{34,66},{66,9... | collective-permute-start | bytes 786440 | tf_op jit(solution)/shard_map/ppermute | solution.py:506
  93.9 12.9 %collective-permute-start.12 = (f32[2,128,128]{2,1,0:T(8,128)}, f32[2,128,128]{2,1,0:T(8,128)S(1)}, u32[]{:S(2)}, u32[]{:S(2)}) collective-permute-start(f32[2,128,128]{2,1,0:T(8,128)} %get-tuple-element.19), channel_id=1, source_target_pairs={{0,96},{1,97},{2,98},{3,99},{4,100},{5,101},{6,102},{7,103},{8,104... | collective-permute-start | bytes 393224 | tf_op jit(solution)/shard_map/ppermute | solution.py:508
  106.8 0.6 copy-start.6
  106.8 0.7 copy-start.3
  106.8 0.8 copy-start.4
  126.5 0.8 copy-start.8
Sparse Core Ops, SparseCore 0:
  9.0 37.8 all-gather.1

commit v7 on v6

--- a/solution.py
+++ b/solution.py
@@ -149,7 +149,9 @@
             place = lax.rem(z - k + NZ, NZ)
             top = pl.multiple_of(rows * ROWS, 128)
             copies.append((part.at[pl.ds(0, ROWS)], weights.at[pl.ds(top, ROWS), block_columns(sp[3 + place])]))
-            copies.append((part.at[pl.ds(ROWS, PACK)], halves.at[rows, place]))
+            split_off = side == 1 and k == 1
+            half = parts[2 * NZ] if split_off else part.at[pl.ds(ROWS, PACK)]
+            copies.append((half, halves.at[rows, place]))
     copies = [pltpu.make_async_copy(s, d, sems.at[i]) for i, (s, d) in enumerate(copies)]
     for copy in copies:
         copy.start()
@@ -232,9 +234,9 @@
 
 
 def state_kernel(sp, tokens, halo, log_sums, betas, conv_k, conv_v, *rest):
-    parts = rest[:8]
-    down_o, solved_o, carry_o, wq_o, state_o, offset_o = rest[8:14]
-    halves, wbuf, mixed, state, sems = rest[14:]
+    parts = rest[:9]
+    down_o, solved_o, carry_o, wq_o, state_o, offset_o = rest[9:15]
+    halves, wbuf, mixed, state, sems = rest[15:]
     step = pl.program_id(0)
 
     @pl.when(step == 0)
@@ -313,7 +315,7 @@
                 columns((CONV, 256), 1),
                 columns((CONV, 256), 2),
             ]
-            + [pl.BlockSpec(memory_space=pl.ANY)] * 8,
+            + [pl.BlockSpec(memory_space=pl.ANY)] * 9,
             out_specs=[
                 by_step(STATE_STEP, 2 * DK),
                 by_step(STATE_STEP, 4 * DK),
@@ -453,7 +455,9 @@
         [lax.ppermute(whole, seq, WHOLE_ROUTE), lax.ppermute(half, seq, HALF_ROUTE)], axis=0
     )
     near = [mine] + [lax.ppermute(mine, "z", ring(k)) for k in range(1, NZ)]
-    return near, [lax.ppermute(p, "y", ring(d)) for p, d in zip(near, (1, 3, 1, 3))]
+    far = [lax.ppermute(p, "y", ring(d)) for p, d in zip(near, (1, 3, 1, 3)) if p is not near[1]]
+    last = [lax.ppermute(p, "y", ring(d)) for p, d in ((near[1][:ROWS], 3), (near[1][ROWS:], 1))]
+    return near, far[:1] + last[:1] + far[1:] + last[1:]
 
 
 def per_device(

time: 136 us -> 133 us (0.978)
  waiting for transfers between devices: 19.1 us -> 15.4 us
    ppermute x1, starting transfers between devices: 3.57 us -> 7.01 us  [per_device(): second = lax.ppermute(state, 'z', ahead(2))]
    ppermute x1, starting transfers between devices: 4.26 us -> 1.31 us  [per_device(): first = lax.ppermute(state, 'z', ahead(1))]
    ppermute x4 -> x5, waiting for transfers between devices: 2.7 us -> 0.22 us  [gather_weights(): lax.ppermute(p, 'y', ring(d))]
    unnamed x60 -> x62, local copies, waits for them, and re-layouts: 7.29 us -> 7.37 us
    ppermute x4 -> x5, starting transfers between devices: 6.93 us -> 6.91 us  [gather_weights(): lax.ppermute(p, 'y', ring(d))]
  transfers between devices with their start and end apart: 14 -> 15, of which waited for: 3 -> 2; matrix products, arithmetic and copies ran while one was open for 11% -> 11% of each run, Pallas kernels for 14% -> 14%
where the time goes in v7:
time: 133 us; the launch traced here: 132 us
  Pallas kernels  41.3 us (31%)
  starting transfers between devices  28.6 us (22%)
  waiting for transfers between devices  15.4 us (12%)
  blocking collectives  15 us (11%)
  between operations  13.9 us (10%)
  local copies, waits for them, and re-layouts  13.6 us (10%)
  other arithmetic  4.15 us (3%)
    pallas_call x1, Pallas kernels, run_state(): pl.pallas_call(state_kernel, name='block_state', out_shape=(jax.ShapeDtyp...  18.7 us
    all_to_all x1, blocking collectives, per_device(): out = lax.all_to_all(out.reshape(ROW, SHARD, 2 * DK), ('x', 'c'), 0, 0)  15 us
    ppermute x3, waiting for transfers between devices, gather_weights(): near = [mine] + [lax.ppermute(mine, 'z', ring(k)) for k in range(1, NZ)]  14.4 us
    pallas_call x1, Pallas kernels, run_queries(): pl.pallas_call(query_kernel, name='block_query', out_shape=(wide, wide),...  11.3 us
    pallas_call x1, Pallas kernels, run_gates(): pl.pallas_call(gate_kernel, name='block_gates', out_shape=(wide, wide, wi...  7.48 us
    unnamed x62, local copies, waits for them, and re-layouts  7.37 us
    ppermute x1, starting transfers between devices, per_device(): second = lax.ppermute(state, 'z', ahead(2))  7.01 us
    ppermute x5, starting transfers between devices, gather_weights(): lax.ppermute(p, 'y', ring(d))  6.91 us
  transfers between devices with their start and end apart: 15, of which 2 were waited for; matrix products, arithmetic and copies ran while one was open for 11% of the time, Pallas kernels for 14%

profile of v7, /device:TPU:1, one launch (start us, length us, event | category | flops | bytes accessed | tf_op | source)
XLA Modules:
  0.0 131.9 jit_solution(15249428545124754591)
XLA Ops:
  6.5 0.7 all-gather.2.cloned.1.call-update
  7.3 1.0 constant_dynamic-slice_fusion.1
  8.9 4.9 %collective-permute-start.2 = (bf16[576,128]{1,0:T(8,128)(2,1)S(1)}, bf16[576,128]{1,0:T(8,128)(2,1)S(1)}, u32[]{:S(2)}, u32[]{:S(2)}) collective-permute-start(bf16[576,128]{1,0:T(8,128)(2,1)S(1)} %pad_maximum_fusion), channel_id=1, source_target_pairs={{0,0},{4,32},{8,8},{12,104},{16,16},{20,112},{24,28},{28,60},{32,4... | collective-permute-start | bytes 442376 | tf_op jit(solution)/shard_map/ppermute | solution.py:455
  14.5 0.9 collective-permute-start.1
  15.7 0.7 constant_dynamic-update-slice_fusion.5
  16.4 0.7 constant_dynamic-update-slice_fusion.4
  17.1 0.7 constant_dynamic-update-slice_fusion.3
  17.8 0.7 constant_dynamic-update-slice_fusion.2
  18.5 0.7 constant_dynamic-update-slice_fusion.1
  19.2 0.7 constant_dynamic-update-slice_fusion.conv_k.conv_v.conv_q
  19.9 0.8 constant_dynamic-slice_fusion.9
  20.7 1.5 %fusion.1.wsmall = bf16[2304,384]{1,0:T(8,128)(2,1)} fusion(bf16[2304,16]{1,0:T(8,128)(2,1)S(1)} %copy.13, bf16[2304,128]{1,0:T(8,128)(2,1)S(1)} %copy-done.1, bf16[2304,128]{1,0:T(8,128)(2,1)S(1)} %copy-done.2), kind=kLoop, calls=%fused_computation.2 | loop fusion | flops 7077888 | bytes 3022848 | tf_op jit(solution)/shard_map/concatenate | solution.py:478
  22.4 3.8 %collective-permute-start.5 = (bf16[1728,128]{1,0:T(8,128)(2,1)S(1)}, bf16[1728,128]{1,0:T(8,128)(2,1)S(1)}, u32[]{:S(2)}, u32[]{:S(2)}) collective-permute-start(bf16[1728,128]{1,0:T(8,128)(2,1)S(1)} %constant_dynamic-update-slice_fusion.6.rest_0_), channel_id=1, source_target_pairs={{0,96},{32,0},{64,32},{96,64},{1,97},{33,1},{65,33},{97,65},{2,98}... | collective-permute-start | bytes 1327112 | tf_op jit(solution)/shard_map/ppermute | solution.py:457
  26.5 0.8 dynamic-slice_bitcast_fusion.1
  27.3 0.6 pad_maximum_fusion.2.gate_up
  28.9 1.3 collective-permute-start.6
  30.8 14.4 %collective-permute-done.5.rest_3_ = bf16[1728,128]{1,0:T(8,128)(2,1)S(1)} collective-permute-done((bf16[1728,128]{1,0:T(8,128)(2,1)S(1)}, bf16[1728,128]{1,0:T(8,128)(2,1)S(1)}, u32[]{:S(2)}, u32[]{:S(2)}) %collective-permute-start.5) | collective-permute-done | bytes 442400 | tf_op jit(solution)/shard_map/ppermute | solution.py:457
  45.2 2.7 %collective-permute-start.9 = (bf16[1728,128]{1,0:T(8,128)(2,1)S(1)}, bf16[1728,128]{1,0:T(8,128)(2,1)S(1)}, u32[]{:S(2)}, u32[]{:S(2)}) collective-permute-start(bf16[1728,128]{1,0:T(8,128)(2,1)S(1)} %collective-permute-done.5.rest_3_), channel_id=1, source_target_pairs={{0,3},{1,0},{2,1},{3,2},{4,7},{5,4},{6,5},{7,6},{8,11},{9,8},{10,9... | collective-permute-start | bytes 1327112 | tf_op jit(solution)/shard_map/ppermute | solution.py:458
  48.0 0.7 fusion.2
  49.3 2.8 %collective-permute-start.7 = (bf16[1152,128]{1,0:T(8,128)(2,1)S(1)}, bf16[1152,128]{1,0:T(8,128)(2,1)S(1)}, u32[]{:S(2)}, u32[]{:S(2)}) collective-permute-start(bf16[1152,128]{1,0:T(8,128)(2,1)S(1)} %slice.103), channel_id=1, source_target_pairs={{0,3},{1,0},{2,1},{3,2},{4,7},{5,4},{6,5},{7,6},{8,11},{9,8},{10,9... | collective-permute-start | bytes 884744 | tf_op jit(solution)/shard_map/ppermute | solution.py:459
  52.8 0.9 slice.100
  53.7 1.5 %collective-permute-start = (bf16[16,2304]{1,0:T(8,128)(2,1)S(1)}, bf16[16,2304]{1,0:T(8,128)(2,1)S(1)}, u32[]{:S(2)}, u32[]{:S(2)}) collective-permute-start(bf16[16,2304]{1,0:T(8,128)(2,1)S(1)} %slice.100), channel_id=1, source_target_pairs={{0,32},{32,64},{64,96},{1,33},{33,65},{65,97},{2,34},{34,66},{66,9... | collective-permute-start | bytes 221192 | tf_op jit(solution)/shard_map/ppermute | solution.py:497
  55.2 7.5 %block_gates.1 = (f32[1024,256]{1,0:T(8,128)}, f32[1024,256]{1,0:T(8,128)}, f32[1024,256]{1,0:T(8,128)}) custom-call(s32[13]{0:T(128)} %pad_add_fusion.sp, bf16[1024,2304]{1,0:T(8,128)(2,1)} %all-gather.2.cloned.1.call-done.tokens, bf16[2304,384]{1,0:T(8,128)(2,1)} %fusion.1.wsmall, bf16[128,256]{1,0:T(8,128)(2,1)} %pad_maximum_fusion.1.decay_up, ...), custom_call_target="tpu_custom_call" | custom-call | flops 2000000000 | bytes 10000000 | tf_op jit(solution)/shard_map/block_gates/pallas_call | solution.py:206
  63.0 0.7 copy-done.15
  63.9 18.7 %block_state.1 = (f32[1024,256]{1,0:T(8,128)}, f32[1024,512]{1,0:T(8,128)}, f32[1024,512]{1,0:T(8,128)}, bf16[2304,256]{1,0:T(8,128)(2,1)}, f32[2,128,256]{2,1,0:T(8,128)}, /*index=5*/f32[2,128,128]{2,1,0:T(8,128)}) custom-call(s32[13]{0:T(128)} %pad_add_fusion.sp, bf16[1024,2304]{1,0:T(8,128)(2,1)} %all-gather.2.cloned.1.call-done.tokens, ...), custom_call_target="tpu_custom_call" | custom-call | flops 10000000000 | bytes 20000000 | tf_op jit(solution)/shard_map/block_state/pallas_call | solution.py:296
  82.6 7.0 %collective-permute-start.12 = (f32[2,128,256]{2,1,0:T(8,128)}, f32[2,128,256]{2,1,0:T(8,128)S(1)}, u32[]{:S(2)}, u32[]{:S(2)}) collective-permute-start(f32[2,128,256]{2,1,0:T(8,128)} %get-tuple-element.18), channel_id=1, source_target_pairs={{0,64},{32,96},{1,65},{33,97},{2,66},{34,98},{3,67},{35,99},{4,68}... | collective-permute-start | bytes 786440 | tf_op jit(solution)/shard_map/ppermute | solution.py:511
  89.6 1.3 collective-permute-start.11
  90.9 1.5 %collective-permute-start.13 = (f32[2,128,128]{2,1,0:T(8,128)}, f32[2,128,128]{2,1,0:T(8,128)S(1)}, u32[]{:S(2)}, u32[]{:S(2)}) collective-permute-start(f32[2,128,128]{2,1,0:T(8,128)} %get-tuple-element.19), channel_id=1, source_target_pairs={{0,96},{1,97},{2,98},{3,99},{4,100},{5,101},{6,102},{7,103},{8,104... | collective-permute-start | bytes 393224 | tf_op jit(solution)/shard_map/ppermute | solution.py:512
  92.4 11.3 %block_query.1 = (f32[1024,256]{1,0:T(8,128)}, f32[1024,256]{1,0:T(8,128)}) custom-call(s32[13]{0:T(128)} %pad_add_fusion.sp, bf16[1024,2304]{1,0:T(8,128)(2,1)} %all-gather.2.cloned.1.call-done.tokens, bf16[16,2304]{1,0:T(8,128)(2,1)} %copy-done.16, bf16[2304,256]{1,0:T(8,128)(2,1)} %get-tuple-element.20.wq, f32[4,768]{1,0:T(4,128)} %copy-done.10, ...), custom_call_target="tpu_custom_call" | custom-call | flops 5000000000 | bytes 20000000 | tf_op jit(solution)/shard_map/block_query/pallas_call | solution.py:380
  104.6 3.7 %finish.1 = bf16[1024,256]{1,0:T(8,128)(2,1)} custom-call(f32[2,128,256]{2,1,0:T(8,128)} %copy-done.5, f32[2,128,256]{2,1,0:T(8,128)} %copy-done.4, f32[2,128,128]{2,1,0:T(8,128)} %copy-done.7, f32[1024,256]{1,0:T(8,128)} %get-tuple-element.24.qeff, f32[1024,256]{1,0:T(8,128)} %get-tuple-element.25.core, f32[1024,256]{1,0:T(8,128)} %get-tuple-element.26.gate, ...), custom_call_target="tpu_custom_call" | custom-call | tf_op jit(solution)/shard_map/finish/pallas_call | solution.py:428
  108.3 15.0 %all_to_all.5 = bf16[8,128,256]{2,1,0:T(8,128)(2,1)S(1)} all-to-all(bf16[8,128,256]{2,1,0:T(8,128)(2,1)} %bitcast.77), channel_id=1, replica_groups=mesh['z'=4,'x'=4,'c'=2,'y'=4] {'x','c'}, dimensions={0} | all-to-all | bytes 1048576 | tf_op jit(solution)/shard_map/all_to_all | solution.py:515
  123.7 0.8 copy-done.9
  (87 shorter events, 6.8 us)
Async XLA Ops:
  6.5 7.3 %copy-start = (bf16[2304,192]{0,1:T(8,128)(2,1)S(1)}, bf16[2304,192]{0,1:T(8,128)(2,1)}, u32[]{:S(2)}) copy-start(bf16[2304,192]{0,1:T(8,128)(2,1)} %param.13) | copy-start | bytes 2654212
  6.5 46.3 %all-gather.2.cloned.1.call-start = ((), (), s32[]{:S(2)}) async-start(), calls=%async_computation.1 | async-start | bytes 5308416 | tf_op jit(solution)/shard_map/all_gather | solution.py:495
  8.8 6.6 %copy-start.8 = (bf16[2304,16]{0,1:T(8,128)(2,1)S(1)}, bf16[2304,16]{0,1:T(8,128)(2,1)}, u32[]{:S(2)}) copy-start(bf16[2304,16]{0,1:T(8,128)(2,1)} %param.18) | copy-start | bytes 221188
  8.9 13.4 %collective-permute-start.2 = (bf16[576,128]{1,0:T(8,128)(2,1)S(1)}, bf16[576,128]{1,0:T(8,128)(2,1)S(1)}, u32[]{:S(2)}, u32[]{:S(2)}) collective-permute-start(bf16[576,128]{1,0:T(8,128)(2,1)S(1)} %pad_maximum_fusion), channel_id=1, source_target_pairs={{0,0},{4,32},{8,8},{12,104},{16,16},{20,112},{24,28},{28,60},{32,4... | collective-permute-start | bytes 442376 | tf_op jit(solution)/shard_map/ppermute | solution.py:455
  13.9 6.8 %copy-start.1 = (bf16[2304,128]{1,0:T(8,128)(2,1)S(1)}, bf16[2304,128]{1,0:T(8,128)(2,1)}, u32[]{:S(2)}) copy-start(bf16[2304,128]{1,0:T(8,128)(2,1)} %param.20) | copy-start | bytes 1769476
  13.9 6.8 %copy-start.2 = (bf16[2304,128]{1,0:T(8,128)(2,1)S(1)}, bf16[2304,128]{1,0:T(8,128)(2,1)}, u32[]{:S(2)}) copy-start(bf16[2304,128]{1,0:T(8,128)(2,1)} %param.15) | copy-start | bytes 1769476
  14.5 7.8 %collective-permute-start.1 = (bf16[1152,128]{1,0:T(8,128)(2,1)S(1)}, bf16[1152,128]{1,0:T(8,128)(2,1)S(1)}, u32[]{:S(2)}, u32[]{:S(2)}) collective-permute-start(bf16[1152,128]{1,0:T(8,128)(2,1)S(1)} %broadcast_select_fusion.1), channel_id=1, source_target_pairs={{0,8},{4,24},{8,16},{12,0},{16,56},{20,12},{24,4},{28,20},{32,44},... | collective-permute-start | bytes 884744 | tf_op jit(solution)/shard_map/ppermute | solution.py:455
  19.9 2.4 %copy-start.10 = (f32[4,768]{1,0:T(4,128)}, f32[4,768]{1,0:T(4,128)S(1)}, u32[]{:S(2)}) copy-start(f32[4,768]{1,0:T(4,128)S(1)} %constant_dynamic-update-slice_fusion.conv_k.conv_v.conv_q) | copy-start | bytes 36868
  20.7 9.5 %copy-start.17 = (f32[16]{0:T(128)S(1)}, f32[16]{0:T(128)}, u32[]{:S(2)}) copy-start(f32[16]{0:T(128)} %param.19) | copy-start | bytes 196
  22.4 40.3 %copy-start.6 = (bf16[1728,128]{1,0:T(8,128)(2,1)}, bf16[1728,128]{1,0:T(8,128)(2,1)S(1)}, u32[]{:S(2)}) copy-start(bf16[1728,128]{1,0:T(8,128)(2,1)S(1)} %constant_dynamic-update-slice_fusion.6.rest_0_) | copy-start | bytes 1327108
  22.4 22.8 %collective-permute-start.5 = (bf16[1728,128]{1,0:T(8,128)(2,1)S(1)}, bf16[1728,128]{1,0:T(8,128)(2,1)S(1)}, u32[]{:S(2)}, u32[]{:S(2)}) collective-permute-start(bf16[1728,128]{1,0:T(8,128)(2,1)S(1)} %constant_dynamic-update-slice_fusion.6.rest_0_), channel_id=1, source_target_pairs={{0,96},{32,0},{64,32},{96,64},{1,97},{33,1},{65,33},{97,65},{2,98}... | collective-permute-start | bytes 1327112 | tf_op jit(solution)/shard_map/ppermute | solution.py:457
  26.2 21.7 %collective-permute-start.4 = (bf16[1728,128]{1,0:T(8,128)(2,1)S(1)}, bf16[1728,128]{1,0:T(8,128)(2,1)S(1)}, u32[]{:S(2)}, u32[]{:S(2)}) collective-permute-start(bf16[1728,128]{1,0:T(8,128)(2,1)S(1)} %constant_dynamic-update-slice_fusion.6.rest_0_), channel_id=1, source_target_pairs={{0,64},{32,96},{64,0},{96,32},{1,65},{33,97},{65,1},{97,33},{2,66}... | collective-permute-start | bytes 1327112 | tf_op jit(solution)/shard_map/ppermute | solution.py:457
  28.0 21.3 %collective-permute-start.3 = (bf16[1728,128]{1,0:T(8,128)(2,1)S(1)}, bf16[1728,128]{1,0:T(8,128)(2,1)S(1)}, u32[]{:S(2)}, u32[]{:S(2)}) collective-permute-start(bf16[1728,128]{1,0:T(8,128)(2,1)S(1)} %constant_dynamic-update-slice_fusion.6.rest_0_), channel_id=1, source_target_pairs={{0,32},{32,64},{64,96},{96,0},{1,33},{33,65},{65,97},{97,1},{2,34}... | collective-permute-start | bytes 1327112 | tf_op jit(solution)/shard_map/ppermute | solution.py:457
  28.9 24.8 %collective-permute-start.6 = (bf16[1728,128]{1,0:T(8,128)(2,1)S(1)}, bf16[1728,128]{1,0:T(8,128)(2,1)S(1)}, u32[]{:S(2)}, u32[]{:S(2)}) collective-permute-start(bf16[1728,128]{1,0:T(8,128)(2,1)S(1)} %constant_dynamic-update-slice_fusion.6.rest_0_), channel_id=1, source_target_pairs={{0,1},{1,2},{2,3},{3,0},{4,5},{5,6},{6,7},{7,4},{8,9},{9,10},{10,1... | collective-permute-start | bytes 1327112 | tf_op jit(solution)/shard_map/ppermute | solution.py:458
  45.2 17.5 %copy-start.11 = (bf16[1728,128]{1,0:T(8,128)(2,1)}, bf16[1728,128]{1,0:T(8,128)(2,1)S(1)}, u32[]{:S(2)}) copy-start(bf16[1728,128]{1,0:T(8,128)(2,1)S(1)} %collective-permute-done.5.rest_3_) | copy-start | bytes 1327108
  45.2 17.8 %collective-permute-start.9 = (bf16[1728,128]{1,0:T(8,128)(2,1)S(1)}, bf16[1728,128]{1,0:T(8,128)(2,1)S(1)}, u32[]{:S(2)}, u32[]{:S(2)}) collective-permute-start(bf16[1728,128]{1,0:T(8,128)(2,1)S(1)} %collective-permute-done.5.rest_3_), channel_id=1, source_target_pairs={{0,3},{1,0},{2,1},{3,2},{4,7},{5,4},{6,5},{7,6},{8,11},{9,8},{10,9... | collective-permute-start | bytes 1327112 | tf_op jit(solution)/shard_map/ppermute | solution.py:458
  47.9 14.8 %copy-start.12 = (bf16[1728,128]{1,0:T(8,128)(2,1)}, bf16[1728,128]{1,0:T(8,128)(2,1)S(1)}, u32[]{:S(2)}) copy-start(bf16[1728,128]{1,0:T(8,128)(2,1)S(1)} %collective-permute-done.4.rest_2_) | copy-start | bytes 1327108
  48.0 15.0 %collective-permute-start.8 = (bf16[1728,128]{1,0:T(8,128)(2,1)S(1)}, bf16[1728,128]{1,0:T(8,128)(2,1)}, u32[]{:S(2)}, u32[]{:S(2)}) collective-permute-start(bf16[1728,128]{1,0:T(8,128)(2,1)S(1)} %collective-permute-done.4.rest_2_), channel_id=1, source_target_pairs={{0,1},{1,2},{2,3},{3,0},{4,5},{5,6},{6,7},{7,4},{8,9},{9,10},{10,1... | collective-permute-start | bytes 1327112 | tf_op jit(solution)/shard_map/ppermute | solution.py:458
  49.3 13.4 %copy-start.3 = (bf16[1728,128]{1,0:T(8,128)(2,1)}, bf16[1728,128]{1,0:T(8,128)(2,1)S(1)}, u32[]{:S(2)}) copy-start(bf16[1728,128]{1,0:T(8,128)(2,1)S(1)} %collective-permute-done.3.rest_1_) | copy-start | bytes 1327108
  49.3 13.6 %collective-permute-start.7 = (bf16[1152,128]{1,0:T(8,128)(2,1)S(1)}, bf16[1152,128]{1,0:T(8,128)(2,1)S(1)}, u32[]{:S(2)}, u32[]{:S(2)}) collective-permute-start(bf16[1152,128]{1,0:T(8,128)(2,1)S(1)} %slice.103), channel_id=1, source_target_pairs={{0,3},{1,0},{2,1},{3,2},{4,7},{5,4},{6,5},{7,6},{8,11},{9,8},{10,9... | collective-permute-start | bytes 884744 | tf_op jit(solution)/shard_map/ppermute | solution.py:459
  52.7 10.2 %collective-permute-start.10 = (bf16[576,128]{1,0:T(8,128)(2,1)S(1)}, bf16[576,128]{1,0:T(8,128)(2,1)}, u32[]{:S(2)}, u32[]{:S(2)}) collective-permute-start(bf16[576,128]{1,0:T(8,128)(2,1)S(1)} %slice.104), channel_id=1, source_target_pairs={{0,1},{1,2},{2,3},{3,0},{4,5},{5,6},{6,7},{7,4},{8,9},{9,10},{10,1... | collective-permute-start | bytes 442376 | tf_op jit(solution)/shard_map/ppermute | solution.py:459
  53.7 9.0 %copy-start.13 = (bf16[1728,128]{1,0:T(8,128)(2,1)}, bf16[1728,128]{1,0:T(8,128)(2,1)S(1)}, u32[]{:S(2)}) copy-start(bf16[1728,128]{1,0:T(8,128)(2,1)S(1)} %collective-permute-done.6.rest_4_) | copy-start | bytes 1327108
  53.7 9.2 %collective-permute-start = (bf16[16,2304]{1,0:T(8,128)(2,1)S(1)}, bf16[16,2304]{1,0:T(8,128)(2,1)S(1)}, u32[]{:S(2)}, u32[]{:S(2)}) collective-permute-start(bf16[16,2304]{1,0:T(8,128)(2,1)S(1)} %slice.100), channel_id=1, source_target_pairs={{0,32},{32,64},{64,96},{1,33},{33,65},{65,97},{2,34},{34,66},{66,9... | collective-permute-start | bytes 221192 | tf_op jit(solution)/shard_map/ppermute | solution.py:497
  62.9 0.7 copy-start.15
  63.0 0.9 copy-start.14
  63.0 0.9 copy-start.16
  82.6 21.2 %collective-permute-start.12 = (f32[2,128,256]{2,1,0:T(8,128)}, f32[2,128,256]{2,1,0:T(8,128)S(1)}, u32[]{:S(2)}, u32[]{:S(2)}) collective-permute-start(f32[2,128,256]{2,1,0:T(8,128)} %get-tuple-element.18), channel_id=1, source_target_pairs={{0,64},{32,96},{1,65},{33,97},{2,66},{34,98},{3,67},{35,99},{4,68}... | collective-permute-start | bytes 786440 | tf_op jit(solution)/shard_map/ppermute | solution.py:511
  89.6 14.2 %collective-permute-start.11 = (f32[2,128,256]{2,1,0:T(8,128)}, f32[2,128,256]{2,1,0:T(8,128)S(1)}, u32[]{:S(2)}, u32[]{:S(2)}) collective-permute-start(f32[2,128,256]{2,1,0:T(8,128)} %get-tuple-element.18), channel_id=1, source_target_pairs={{0,32},{32,64},{64,96},{1,33},{33,65},{65,97},{2,34},{34,66},{66,9... | collective-permute-start | bytes 786440 | tf_op jit(solution)/shard_map/ppermute | solution.py:510
  90.9 12.9 %collective-permute-start.13 = (f32[2,128,128]{2,1,0:T(8,128)}, f32[2,128,128]{2,1,0:T(8,128)S(1)}, u32[]{:S(2)}, u32[]{:S(2)}) collective-permute-start(f32[2,128,128]{2,1,0:T(8,128)} %get-tuple-element.19), channel_id=1, source_target_pairs={{0,96},{1,97},{2,98},{3,99},{4,100},{5,101},{6,102},{7,103},{8,104... | collective-permute-start | bytes 393224 | tf_op jit(solution)/shard_map/ppermute | solution.py:512
  103.8 0.7 copy-start.4
  103.8 0.8 copy-start.5
  123.6 0.8 copy-start.9
  (1 other events, 0.7 us)
Sparse Core Ops, SparseCore 0:
  9.0 37.8 all-gather.1
